TPU v7x, 128 devices: a whole 4x4x4 slice. The times are simulated.
128 devices in a mesh: users: 16 (over x, y), items: 8 (over z, core).
Axes of the slice: x: 4, y: 4, z: 4, core: 2. Of those that a mesh axis runs over, the one named last changes fastest.
Arguments:
- tiles: float32 [16, 8, 4, 32, 128, 128], P('users', 'items'), may hold values from -6 to 6
- user_blocks: int32 [16, 8, 4], P('users', 'items'), may hold values from 0 to 15, as said below
- item_blocks: int32 [16, 8, 4], P('users', 'items'), may hold values from 0 to 127, as said below
- counts: int32 [16, 8], P('users', 'items'), may hold values from 1 to 4, as said below
- user_factor: float32 [64, 32768], P(None, ('users', 'items')), may hold values from -0.5 to 0.5
- item_factor: float32 [64, 131072], P(None, ('items', 'users')), may hold values from -0.5 to 0.5
- week_factor: float32 [32, 64], replicated, may hold values from -1 to 1
Outputs:
- m_users: float32 [64, 32768], P(None, ('users', 'items'))
- m_items: float32 [64, 131072], P(None, ('items', 'users'))
Inputs may be any that keep to these rules, and one draw needn't show every extreme that they name: `user_blocks`: within one device the first 4 slots name distinct (user block, item block) pairs of its grid row and grid column. `item_blocks`: paired with user_blocks slot by slot. `counts`: some device holds 4 tiles in every draw.
All inputs are finite; a program needn't handle non-finite values.
Results may differ from a plain program's by a relative error of at most 0.0001.
Values sent between devices are 32-bit elements; how exact they have to be, the bound alone decides.
A program may use at most 128 MiB of HBM per device.

v0:
```python
import jax
import jax.numpy as jnp
from jax import lax
from jax.sharding import PartitionSpec as P


def on_device(tiles, user_blocks, item_blocks, counts, user_factor, item_factor, week_factor):
    user_rows = lax.all_gather(user_factor, "items", axis=1, tiled=True)
    item_rows = lax.all_gather(item_factor, "users", axis=1, tiled=True)
    slot_total = tiles.shape[2]
    user_width = tiles.shape[4]
    item_width = tiles.shape[5]
    rank_size = week_factor.shape[1]
    user_block_total = user_rows.shape[1] // user_width
    item_block_total = item_rows.shape[1] // item_width
    tile_count = counts[0, 0]
    highest = lax.Precision.HIGHEST
    user_ids = user_blocks[0, 0]
    item_ids = item_blocks[0, 0]

    def slot_terms(carry, packed):
        tile_data, user_index, item_index, slot_index = packed
        user_at = user_index * user_width
        item_at = item_index * item_width

        def tile_work(unused):
            user_block = lax.dynamic_slice_in_dim(user_rows, user_at, user_width, 1)
            item_block = lax.dynamic_slice_in_dim(item_rows, item_at, item_width, 1)
            by_items = jnp.einsum(
                "kab,rb->rka",
                tile_data,
                item_block,
                precision=highest,
                preferred_element_type=jnp.float32,
            )
            user_term = jnp.einsum(
                "rka,kr->ra",
                by_items,
                week_factor,
                precision=highest,
                preferred_element_type=jnp.float32,
            )
            by_users = jnp.einsum(
                "kab,ra->rkb",
                tile_data,
                user_block,
                precision=highest,
                preferred_element_type=jnp.float32,
            )
            item_term = jnp.einsum(
                "rkb,kr->rb",
                by_users,
                week_factor,
                precision=highest,
                preferred_element_type=jnp.float32,
            )
            return (user_term, item_term)

        def skip_tile(unused):
            return (
                jnp.zeros((rank_size, user_width), jnp.float32),
                jnp.zeros((rank_size, item_width), jnp.float32),
            )

        return (carry, lax.cond(slot_index < tile_count, tile_work, skip_tile, 0))

    slot_order = jnp.arange(slot_total, dtype=jnp.int32)
    _, (user_terms, item_terms) = lax.scan(
        slot_terms, 0, (tiles[0, 0], user_ids, item_ids, slot_order)
    )
    user_hot = (user_ids[:, None] == jnp.arange(user_block_total, dtype=jnp.int32)[None, :]).astype(
        jnp.float32
    )
    item_hot = (item_ids[:, None] == jnp.arange(item_block_total, dtype=jnp.int32)[None, :]).astype(
        jnp.float32
    )
    part_users = jnp.einsum(
        "sn,sra->rna", user_hot, user_terms, precision=highest, preferred_element_type=jnp.float32
    ).reshape(rank_size, user_rows.shape[1])
    part_items = jnp.einsum(
        "sn,srb->rnb", item_hot, item_terms, precision=highest, preferred_element_type=jnp.float32
    ).reshape(rank_size, item_rows.shape[1])
    full_users = lax.psum(part_users, "items")
    user_piece = full_users.shape[1] // lax.axis_size("items")
    m_users = lax.dynamic_slice_in_dim(
        full_users, lax.axis_index("items") * user_piece, user_piece, 1
    )
    full_items = lax.psum(part_items, "users")
    item_piece = full_items.shape[1] // lax.axis_size("users")
    m_items = lax.dynamic_slice_in_dim(
        full_items, lax.axis_index("users") * item_piece, item_piece, 1
    )
    return (m_users, m_items)


def solution(mesh):
    return jax.shard_map(
        on_device,
        mesh=mesh,
        in_specs=(
            P("users", "items", None, None, None, None),
            P("users", "items", None),
            P("users", "items", None),
            P("users", "items"),
            P(None, ("users", "items")),
            P(None, ("items", "users")),
            P(),
        ),
        out_specs=(P(None, ("users", "items")), P(None, ("items", "users"))),
        check_vma=False,
    )
```

profile of v0, /device:TPU:1, one launch (start us, length us, event | category | flops | bytes accessed | tf_op | source)
XLA Modules:
  0.0 308.2 jit_solution(918094241476090509)
XLA Ops:
  7.2 0.7 all-gather.2.cloned.1.call-update
  8.0 15.9 %all_gather.7 = f32[64,2048]{1,0:T(8,128)S(1)} all-gather(f32[64,256]{1,0:T(8,128)} %param.15), channel_id=1, replica_groups=mesh['users'=16,'items'=8] {'items'}, dimensions={1}, use_global_device_ids=true | all-gather | bytes 589824 | tf_op jit(solution)/shard_map/all_gather | solution.py:8
  23.8 41.1 %all-gather.2.cloned.1.call-done = f32[64,16384]{1,0:T(8,128)} async-done(((f32[64,1024]{1,0:T(8,128)}), f32[64,16384]{1,0:T(8,128)}) %all-gather.2.cloned.1.call-update) | async-done | bytes 4194320 | tf_op jit(solution)/shard_map/all_gather | solution.py:9
  64.9 23.6 %while.12 = (s32[]{:T(128)}, f32[4,64,128]{2,0,1:T(4,128)S(1)}, f32[4,64,128]{2,0,1:T(4,128)S(1)}, s32[4]{0:T(128)S(1)}, s32[]{:T(128)}, /*index=5*/s32[4]{0:T(1...) while((s32[]{:T(128)}, f32[4,64,128]{2,0,1:T(4,128)S(1)}, ...), condition=%wide.region_3.4_spmd, body=%wide.region_0.3_spmd.sunk | while | flops 811597824 | bytes 8684907 | solution.py:68
  66.8 14.6 %conditional.2 = (f32[1,64,128]{2,1,0:T(8,128)S(1)}, f32[1,64,128]{2,1,0:T(8,128)S(1)}) conditional(s32[]{:T(128)} %convert_element_type.6, () %tuple.43, (s32[4]{0:T(128)}, s32[]{:T(128)}, f32[64,16384]{1,0:T(8,128)}, f32[4,32,128,128]{3,2,1,0:T(8,128)}, f32[32,64]{1,0:T(8,128)}, /*index=5*/s32[4]{0:T(128)}, f32[64,2048]{1,0:T(8,128)S(1)}) %tuple.44), branch_computations={%region_1.1_spmd, %region_2.2_spmd} | conditional | flops 811597824 | bytes 8553612 | solution.py:65
  66.8 1.3 dynamic_slice.41
  68.7 1.3 dynamic_slice.38
  70.6 4.0 %fusion.2 = f32[64,32,128]{2,0,1:T(8,128)S(1)} fusion(f32[4,32,128,128]{3,2,1,0:T(8,128)} %get-tuple-element.127, s32[]{:T(128)} %get-tuple-element.126, f32[64,16384]{1,0:T(8,128)} %get-tuple-element.124, s32[]{:T(128)S(6)} %select_n.14), kind=kOutput, calls=%fused_computation.2 | convolution fusion | flops 402653184 | bytes 3179012 | tf_op jit(solution)/shard_map/while/body/eval_jaxpr/cond/branch_1_fun/kab,rb->rka/dot_general | solution.py:29
  74.6 0.8 copy.15
  75.4 1.6 fusion.8
  77.0 2.8 fusion
  79.8 1.6 fusion.6
  81.7 0.6 dynamic_slice.67
  84.0 0.6 dynamic_slice.67
  86.3 0.6 dynamic_slice.67
  88.5 1.1 fusion.17
  89.7 1.0 copy.32
  90.9 5.6 %convolution_bitcast_fusion = f32[64,128,128]{1,2,0:T(8,128)} fusion(f32[4,64,128]{2,0,1:T(4,128)S(1)} %get-tuple-element.150, s32[4]{0:T(128)} %get-tuple-element.299), kind=kOutput, calls=%fused_computation.17 | convolution fusion | flops 50332160 | bytes 4325392 | tf_op jit(solution)/shard_map/sn,srb->rnb/dot_general | solution.py:80
  96.6 5.6 %copy.13 = f32[64,128,128]{2,1,0:T(8,128)} copy(f32[64,128,128]{1,2,0:T(8,128)} %convolution_bitcast_fusion) | data formatting | bytes 8388608 | tf_op jit(solution)/shard_map/sn,srb->rnb/transpose | solution.py:80
  102.2 6.5 %copy.31 = f32[8,8,128,128]{3,1,2,0:T(8,128)} copy(f32[8,8,128,128]{3,2,1,0:T(8,128)} %bitcast.56) | data formatting | bytes 8388608
  108.8 83.3 %all-reduce.3.cloned.1.call-done = f32[64,2048]{1,0:T(8,128)} async-done(((f32[64,2048]{1,0:T(8,128)}), f32[64,2048]{1,0:T(8,128)}) %all-reduce.3.cloned.1.call-update) | async-done | bytes 524304 | tf_op jit(solution)/shard_map/psum | solution.py:83
  192.0 1.5 constant_dynamic-slice_fusion.1
  193.5 106.5 %all-reduce.5.cloned.1.call-done = f32[64,16384]{1,0:T(8,128)} async-done(((f32[64,16384]{1,0:T(8,128)}), f32[64,16384]{1,0:T(8,128)}) %all-reduce.5.cloned.1.call-update) | async-done | bytes 4194320 | tf_op jit(solution)/shard_map/psum | solution.py:88
  300.0 1.7 constant_dynamic-slice_fusion
  (26 shorter events, 2.4 us)
Async XLA Ops:
  7.2 57.7 %all-gather.2.cloned.1.call-start = ((), (), s32[]{:S(2)}) async-start(), calls=%async_computation | async-start | bytes 4456448 | tf_op jit(solution)/shard_map/all_gather | solution.py:9
  7.9 184.1 %all-reduce.3.cloned.1.call-start = ((), (), s32[]{:S(2)}) async-start(), calls=%async_computation.1 | async-start | bytes 1048576 | tf_op jit(solution)/shard_map/psum | solution.py:83
  90.7 209.3 %all-reduce.5.cloned.1.call-start = ((), (), s32[]{:S(2)}) async-start(), calls=%async_computation.2 | async-start | bytes 8388608 | tf_op jit(solution)/shard_map/psum | solution.py:88
Sparse Core Ops, SparseCore 0:
  10.2 54.6 all-gather.1
  90.8 101.1 all-reduce.2
  195.8 104.1 all-reduce.4
where the time goes:
time: 309 us; the launch traced here: 308 us
  waiting for transfers between devices  232 us (75%)
  local copies, waits for them, and re-layouts  23.4 us (8%)
  matrix products  16.8 us (5%)
  blocking collectives  15.9 us (5%)
  between operations  13.8 us (4%)
  loops' own time  6.53 us (2%)
    psum x1, waiting for transfers between devices, on_device(): full_items = lax.psum(part_items, 'users')  106 us
    psum x1, waiting for transfers between devices, on_device(): full_users = lax.psum(part_users, 'items')  83.3 us
    all_gather x1, waiting for transfers between devices, on_device(): item_rows = lax.all_gather(item_factor, 'users', axis=1, tiled=True)  41.1 us
    all_gather x1, blocking collectives, on_device(): user_rows = lax.all_gather(user_factor, 'items', axis=1, tiled=True)  15.9 us
    unnamed x2, local copies, waits for them, and re-layouts  7.5 us
  transfers between devices with their start and end apart: 3, of which 3 were waited for; matrix products, arithmetic and copies ran while one was open for 6% of the time, Pallas kernels for 0%

commit v1 on v0

v1 whole, which is shorter than its diff:
```python
import jax
import jax.numpy as jnp
import numpy as np
from jax import lax
from jax.sharding import Mesh
from jax.sharding import PartitionSpec as P

HIGHEST = lax.Precision.HIGHEST


def on_device(tiles, user_blocks, item_blocks, counts, user_factor, item_factor, week_factor):
    x_size = lax.axis_size("ux")
    slot_total = tiles.shape[2]
    user_width = tiles.shape[4]
    item_width = tiles.shape[5]
    rank_size = week_factor.shape[1]
    me_x = lax.axis_index("ux")

    user_ids = user_blocks[0, 0]
    item_ids = item_blocks[0, 0]
    live = (jnp.arange(slot_total, dtype=jnp.int32) < counts[0, 0]).astype(jnp.float32)

    user_rows = lax.all_gather(user_factor, ("iz", "ic"), axis=1, tiled=True)
    user_block_total = user_rows.shape[1] // user_width
    user_rows = user_rows.reshape(rank_size, user_block_total, user_width)
    user_hot = (user_ids[:, None] == jnp.arange(user_block_total, dtype=jnp.int32)[None, :]).astype(jnp.float32)
    user_sel = jnp.einsum("sn,rna->sra", user_hot, user_rows, precision=HIGHEST)

    group_rows = lax.all_gather(item_factor, "uy", axis=1, tiled=True)
    group_blocks = group_rows.shape[1] // item_width
    group_rows = group_rows.reshape(rank_size, group_blocks, item_width)
    wanted = lax.all_gather(item_ids, "ux", axis=0, tiled=False)
    owner_group = wanted // group_blocks
    local_block = wanted % group_blocks
    send_hot = jnp.where(
        (owner_group == me_x)[:, :, None],
        (local_block[:, :, None] == jnp.arange(group_blocks, dtype=jnp.int32)[None, None, :]).astype(jnp.float32),
        0.0,
    )
    send = jnp.einsum("xsl,rlb->xsrb", send_hot, group_rows, precision=HIGHEST)
    item_sel = lax.psum_scatter(send, "ux", scatter_dimension=0, tiled=True)[0]

    data = tiles[0, 0]
    by_items = jnp.einsum("skab,srb->srka", data, item_sel, precision=HIGHEST)
    user_terms = jnp.einsum("srka,kr->sra", by_items, week_factor, precision=HIGHEST) * live[:, None, None]
    by_users = jnp.einsum("skab,sra->srkb", data, user_sel, precision=HIGHEST)
    item_terms = jnp.einsum("srkb,kr->srb", by_users, week_factor, precision=HIGHEST) * live[:, None, None]

    part_users = jnp.einsum("sn,sra->rna", user_hot, user_terms, precision=HIGHEST).reshape(
        rank_size, user_block_total * user_width
    )
    m_users = lax.psum_scatter(part_users, ("iz", "ic"), scatter_dimension=1, tiled=True)

    all_terms = lax.all_gather(item_terms, "ux", axis=0, tiled=False)
    take_hot = jnp.where(
        (owner_group == me_x)[:, :, None],
        (local_block[:, :, None] == jnp.arange(group_blocks, dtype=jnp.int32)[None, None, :]).astype(jnp.float32),
        0.0,
    )
    part_items = jnp.einsum("xsl,xsrb->rlb", take_hot, all_terms, precision=HIGHEST).reshape(
        rank_size, group_blocks * item_width
    )
    m_items = lax.psum_scatter(part_items, "uy", scatter_dimension=1, tiled=True)
    del x_size
    return (m_users, m_items)


def solution(mesh):
    users, items = mesh.shape["users"], mesh.shape["items"]
    devices = np.asarray(mesh.devices).reshape(users // 4, 4, items // 2, 2)
    fine = Mesh(devices, ("ux", "uy", "iz", "ic"))
    rows = ("ux", "uy")
    cols = ("iz", "ic")
    return jax.shard_map(
        on_device,
        mesh=fine,
        in_specs=(
            P(rows, cols, None, None, None, None),
            P(rows, cols, None),
            P(rows, cols, None),
            P(rows, cols),
            P(None, rows + cols),
            P(None, cols + rows),
            P(),
        ),
        out_specs=(P(None, rows + cols), P(None, cols + rows)),
        check_vma=False,
    )
```

time: 309 us -> 143 us (0.46)
  waiting for transfers between devices: 232 us -> 52.6 us
  blocking collectives: 15.9 us -> 36.8 us
  local copies, waits for them, and re-layouts: 23.4 us -> 5.19 us
  matrix products: 16.8 us -> 32.7 us
  loops' own time: 6.53 us -> 0 us
    psum x2 -> x0, waiting for transfers between devices: 190 us -> none  [the longest x1 106 us: on_device(): full_items = lax.psum(part_items, 'users')]
    reduce_scatter x0 -> x3, waiting for transfers between devices: none -> 50.4 us  [the longest x1 26.6 us: on_device(): lax.psum_scatter(part_items, 'uy', scatter_dimension=1, tiled=True)]
    all_gather x1, waiting for transfers between devices: 41.1 us -> 1.46 us  [on_device(): group_rows = lax.all_gather(item_factor, 'uy', axis=1, tiled=True)]
    all_gather x1 -> x3, blocking collectives: 15.9 us -> 36.8 us  [the longest x1 17.1 us: on_device(): user_rows = lax.all_gather(user_factor, ('iz', 'ic'), axis=1, tiled=True)]
    dot_general x6 -> x8, matrix products: 16.8 us -> 32.7 us  [the longest x1 11.7 us: on_device(): by_items = jnp.einsum('skab,srb->srka', data, item_sel, precision=HIGHEST)]
    dynamic_slice x8 -> x0, local copies, waits for them, and re-layouts: 8.06 us -> none  [the longest x6 4.92 us: on_device(): lax.scan(slot_terms, 0, (tiles[0, 0], user_ids, item_ids, slot_order))]
    another operation x5 -> x0, loops' own time: 6.53 us -> none  [the longest x1 5.18 us: on_device(): lax.scan(slot_terms, 0, (tiles[0, 0], user_ids, item_ids, slot_order))]
    transpose x1 -> x0, local copies, waits for them, and re-layouts: 5.63 us -> none  [on_device(): jnp.einsum('sn,srb->rnb', item_hot, item_terms, precision=highest, prefer...]
  transfers between devices with their start and end apart: 3 -> 4, of which waited for: 3 -> 4; matrix products, arithmetic and copies ran while one was open for 6% -> 11% of each run, Pallas kernels for 0% -> 0%
where the time goes in v1:
time: 143 us; the launch traced here: 142 us
  waiting for transfers between devices  52.6 us (37%)
  blocking collectives  36.8 us (26%)
  matrix products  32.7 us (23%)
  between operations  14.5 us (10%)
  local copies, waits for them, and re-layouts  5.19 us (4%)
    reduce_scatter x1, waiting for transfers between devices, on_device(): lax.psum_scatter(part_items, 'uy', scatter_dimension=1, tiled=True)  26.6 us
    all_gather x1, blocking collectives, on_device(): user_rows = lax.all_gather(user_factor, ('iz', 'ic'), axis=1, tiled=True)  17.1 us
    reduce_scatter x1, waiting for transfers between devices, on_device(): lax.psum_scatter(part_users, ('iz', 'ic'), scatter_dimension=1, tiled=True)  15.7 us
    dot_general x1, matrix products, on_device(): by_items = jnp.einsum('skab,srb->srka', data, item_sel, precision=HIGHEST)  11.7 us
    all_gather x1, blocking collectives, on_device(): all_terms = lax.all_gather(item_terms, 'ux', axis=0, tiled=False)  11.1 us
    all_gather x1, blocking collectives, on_device(): wanted = lax.all_gather(item_ids, 'ux', axis=0, tiled=False)  8.65 us
    reduce_scatter x1, waiting for transfers between devices, on_device(): item_sel = lax.psum_scatter(send, 'ux', scatter_dimension=0, tiled=True)[0]  8.03 us
    dot_general x1, matrix products, on_device(): by_users = jnp.einsum('skab,sra->srkb', data, user_sel, precision=HIGHEST)  6.8 us
  transfers between devices with their start and end apart: 4, of which 4 were waited for; matrix products, arithmetic and copies ran while one was open for 11% of the time, Pallas kernels for 0%

profile of v1, /device:TPU:1, one launch (start us, length us, event | category | flops | bytes accessed | tf_op | source)
XLA Modules:
  0.0 142.1 jit_solution(14950030643989074315)
XLA Ops:
  7.2 0.7 all-gather.4.cloned.1.call-update
  8.0 8.6 %all-gather = s32[4,1,4]{2,1,0:T(1,128)S(1)} all-gather(s32[1,1,4]{2,1,0:T(1,128)} %param.9), channel_id=2, replica_groups=mesh['ux'=4,'uy'=4,'iz'=4,'ic'=2] {'ux'}, dimensions={0}, use_global_device_ids=true | all-gather | bytes 80 | tf_op jit(solution)/shard_map/all_gather | solution.py:32
  16.6 0.1 copy.18
  16.7 0.1 copy.17
  17.5 17.1 %all_gather.17 = f32[64,2048]{1,0:T(8,128)S(1)} all-gather(f32[64,256]{1,0:T(8,128)} %param.11), channel_id=1, replica_groups=mesh['ux'=4,'uy'=4,'iz'=4,'ic'=2] {'iz','ic'}, dimensions={1}, use_global_device_ids=true | all-gather | bytes 589824 | tf_op jit(solution)/shard_map/all_gather | solution.py:23
  34.5 1.5 %all-gather.4.cloned.1.call-done = f32[64,4096]{1,0:T(8,128)} async-done(((f32[64,1024]{1,0:T(8,128)}), f32[64,4096]{1,0:T(8,128)}) %all-gather.4.cloned.1.call-update) | async-done | bytes 1048592 | tf_op jit(solution)/shard_map/all_gather | solution.py:29
  36.0 1.4 copy.39
  37.4 0.8 fusion.16
  38.2 0.8 copy.20
  39.3 0.1 copy.41
  39.4 0.3 convolution_bitcast_fusion
  39.7 6.8 %fusion = f32[4,64,32,128]{3,1,2,0:T(8,128)S(1)} fusion(f32[1,1,4,32,128,128]{5,4,3,2,1,0:T(8,128)} %param.7, f32[4,64,128,1]{2,0,1,3:T(4,128)S(1)} %convolution_bitcast_fusion), kind=kOutput, calls=%fused_computation | convolution fusion | flops 1610612736 | bytes 12713984 | tf_op jit(solution)/shard_map/skab,sra->srkb/dot_general | solution.py:46
  46.5 5.7 %fusion.4 = f32[64,1,4,128]{3,1,2,0:T(1,128)S(1)} fusion(f32[32,64,1,1]{0,2,3,1:T(1,128)S(1)} %copy.28, f32[4,64,32,128]{3,1,2,0:T(8,128)S(1)} %fusion), kind=kOutput, calls=%fused_computation.4 | convolution fusion | flops 12582912 | bytes 4333568 | tf_op jit(solution)/shard_map/srkb,kr->srb/dot_general | solution.py:47
  52.2 8.0 %reduce-scatter.4.cloned.1.call-done = f32[1,4,64,128]{3,2,1,0:T(8,128)} async-done(((f32[4,4,64,128]{3,2,1,0:T(8,128)}), f32[1,4,64,128]{3,2,1,0:T(8,128)}) %reduce-scatter.4.cloned.1.call-update) | async-done | bytes 131088 | tf_op jit(solution)/shard_map/reduce_scatter | solution.py:41
  60.2 11.7 %fusion.2 = f32[4,64,32,128]{3,1,2,0:T(8,128)S(1)} fusion(f32[1,1,4,32,128,128]{5,4,3,2,1,0:T(8,128)} %param.7, f32[1,4,64,128]{3,2,1,0:T(8,128)} %reduce-scatter.4.cloned.1.call-done), kind=kOutput, calls=%fused_computation.2 | convolution fusion | flops 1610612736 | bytes 12713984 | tf_op jit(solution)/shard_map/skab,srb->srka/dot_general | solution.py:44
  71.8 5.7 %fusion.6 = f32[64,1,4,128]{3,1,2,0:T(1,128)S(1)} fusion(f32[32,64,1,1]{0,2,3,1:T(1,128)S(1)} %copy.28, f32[4,64,32,128]{3,1,2,0:T(8,128)S(1)} %fusion.2), kind=kOutput, calls=%fused_computation.6 | convolution fusion | flops 12582912 | bytes 4333568 | tf_op jit(solution)/shard_map/srka,kr->sra/dot_general | solution.py:45
  77.5 0.1 fusion.11
  77.6 0.5 fusion.14
  78.1 1.0 copy.58
  79.1 11.1 %all-gather.1 = f32[16,64,128]{2,1,0:T(8,128)S(1)} all-gather(f32[4,64,128]{2,1,0:T(8,128)S(1)} %get-tuple-element.2), channel_id=3, replica_groups=mesh['ux'=4,'uy'=4,'iz'=4,'ic'=2] {'ux'}, dimensions={0}, use_global_device_ids=true | all-gather | bytes 655360 | tf_op jit(solution)/shard_map/all_gather | solution.py:54
  90.2 1.4 fusion.8
  91.6 1.6 %copy.57 = f32[8,8,32,128]{3,1,2,0:T(8,128)} copy(f32[8,8,32,128]{3,2,1,0:T(8,128)S(1)} %bitcast.67) | data formatting | bytes 2097152
  93.2 15.7 %reduce-scatter.6.cloned.1.call-done = f32[64,256]{1,0:T(8,128)} async-done(((f32[64,2048]{1,0:T(8,128)}), f32[64,256]{1,0:T(8,128)}) %reduce-scatter.6.cloned.1.call-update) | async-done | bytes 65552 | tf_op jit(solution)/shard_map/reduce_scatter | solution.py:52
  108.9 26.6 %reduce-scatter.8.cloned.1.call-done = f32[64,1024]{1,0:T(8,128)} async-done(((f32[64,4096]{1,0:T(8,128)}), f32[64,1024]{1,0:T(8,128)}) %reduce-scatter.8.cloned.1.call-update) | async-done | bytes 262160 | tf_op jit(solution)/shard_map/reduce_scatter | solution.py:63
  (15 shorter events, 0.3 us)
Async XLA Ops:
  7.2 32.0 %copy-start = (f32[32,64]{1,0:T(8,128)S(1)}, f32[32,64]{1,0:T(8,128)}, u32[]{:S(2)}) copy-start(f32[32,64]{1,0:T(8,128)} %param.13) | copy-start | bytes 24580
  7.2 32.2 %copy-start.1 = (s32[1,1,4]{2,1,0:T(1,128)S(1)}, s32[1,1,4]{2,1,0:T(1,128)}, u32[]{:S(2)}) copy-start(s32[1,1,4]{2,1,0:T(1,128)} %param.8) | copy-start | bytes 52
  7.2 28.8 %all-gather.4.cloned.1.call-start = ((), (), s32[]{:S(2)}) async-start(), calls=%async_computation.3 | async-start | bytes 1310720 | tf_op jit(solution)/shard_map/all_gather | solution.py:29
  7.9 52.3 %reduce-scatter.4.cloned.1.call-start = ((), (), s32[]{:S(2)}) async-start(), calls=%async_computation.4 | async-start | bytes 655360 | tf_op jit(solution)/shard_map/reduce_scatter | solution.py:41
  39.1 69.8 %reduce-scatter.6.cloned.1.call-start = ((), (), s32[]{:S(2)}) async-start(), calls=%async_computation.5 | async-start | bytes 589824 | tf_op jit(solution)/shard_map/reduce_scatter | solution.py:52
  79.1 56.5 %reduce-scatter.8.cloned.1.call-start = ((), (), s32[]{:S(2)}) async-start(), calls=%async_computation.6 | async-start | bytes 1310720 | tf_op jit(solution)/shard_map/reduce_scatter | solution.py:63
Sparse Core Ops, SparseCore 0:
  9.7 26.2 all-gather.3
  39.2 20.9 reduce-scatter.3
  79.2 29.6 reduce-scatter.5
  111.9 23.6 reduce-scatter.7

commit v2 on v1

v2 whole, which is shorter than its diff:
```python
import functools
import jax
import jax.numpy as jnp
import numpy as np
from jax import lax
from jax.experimental import pallas as pl
from jax.experimental.pallas import tpu as pltpu
from jax.sharding import Mesh
from jax.sharding import PartitionSpec as P

MESH_IDS = pl.DeviceIdType.MESH


def _group_me(axes, sizes):
    me = 0
    for a, n in zip(axes, sizes):
        me = me * n + lax.axis_index(a)
    return me


def _peer(axes, sizes, d):
    coords = {}
    for a, n in reversed(list(zip(axes, sizes))):
        coords[a] = d % n
        d = d // n
    return coords


def _exchange_kernel(plan, *refs):
    ne = len(plan)
    ins, outs = refs[:ne], refs[ne:2 * ne]
    lands, sends, recvs = refs[2 * ne:3 * ne], refs[3 * ne:4 * ne], refs[4 * ne:5 * ne]
    barrier = pltpu.get_barrier_semaphore()
    total = 0
    for axes, sizes, mode in plan:
        n = 1
        for s in sizes:
            n *= s
        me = _group_me(axes, sizes)
        for k in range(1, n):
            pl.semaphore_signal(barrier, inc=1, device_id=_peer(axes, sizes, lax.rem(me + k, n)),
                                device_id_type=MESH_IDS)
        total += n - 1
    pl.semaphore_wait(barrier, total)
    copies = []
    for e, (axes, sizes, mode) in enumerate(plan):
        n = 1
        for s in sizes:
            n *= s
        me = _group_me(axes, sizes)
        for k in range(1, n):
            d = lax.rem(me + k, n)
            src = ins[e].at[d] if mode == "a2a" else ins[e]
            cp = pltpu.make_async_remote_copy(
                src_ref=src, dst_ref=lands[e].at[me], send_sem=sends[e].at[k], recv_sem=recvs[e].at[k],
                device_id=_peer(axes, sizes, d), device_id_type=MESH_IDS)
            cp.start()
            copies.append((e, n, me, k, cp))
    for e, n, me, k, cp in copies:
        cp.wait_send()
        src = lax.rem(me + n - k, n)
        pltpu.make_async_remote_copy(
            src_ref=lands[e].at[src], dst_ref=lands[e].at[src], send_sem=sends[e].at[k], recv_sem=recvs[e].at[k],
            device_id=_peer(plan[e][0], plan[e][1], src), device_id_type=MESH_IDS).wait_recv()
    for e, (axes, sizes, mode) in enumerate(plan):
        n = 1
        for s in sizes:
            n *= s
        me = _group_me(axes, sizes)
        for k in range(1, n):
            src = lax.rem(me + k, n)
            outs[e][src] = lands[e][src]
        outs[e][me] = ins[e][me] if mode == "a2a" else ins[e][...]


def exchange(plan, arrays, collective_id):
    out_shapes, scratch_lands, sems_s, sems_r = [], [], [], []
    for (axes, sizes, mode), x in zip(plan, arrays):
        n = 1
        for s in sizes:
            n *= s
        piece = x.shape[1:] if mode == "a2a" else x.shape
        out_shapes.append(jax.ShapeDtypeStruct((n,) + tuple(piece), x.dtype))
        scratch_lands.append(pltpu.VMEM((n,) + tuple(piece), x.dtype))
        sems_s.append(pltpu.SemaphoreType.DMA((n,)))
        sems_r.append(pltpu.SemaphoreType.DMA((n,)))
    return pl.pallas_call(
        functools.partial(_exchange_kernel, plan),
        out_shape=tuple(out_shapes),
        in_specs=[pl.BlockSpec(memory_space=pltpu.VMEM)] * len(plan),
        out_specs=tuple(pl.BlockSpec(memory_space=pltpu.VMEM) for _ in plan),
        scratch_shapes=scratch_lands + sems_s + sems_r,
        compiler_params=pltpu.CompilerParams(collective_id=collective_id, has_side_effects=True),
    )(*arrays)


HIGHEST = lax.Precision.HIGHEST


def on_device(tiles, user_blocks, item_blocks, counts, user_factor, item_factor, week_factor):
    x_size, y_size = lax.axis_size("ux"), lax.axis_size("uy")
    z_size, c_size = lax.axis_size("iz"), lax.axis_size("ic")
    slot_total = tiles.shape[2]
    user_width = tiles.shape[4]
    item_width = tiles.shape[5]
    rank_size = week_factor.shape[1]
    me_x = lax.axis_index("ux")
    user_own = user_factor.shape[1] // user_width
    item_own = item_factor.shape[1] // item_width
    group_blocks = y_size * item_own

    user_ids = user_blocks[0, 0]
    item_ids = item_blocks[0, 0]
    live = (jnp.arange(slot_total, dtype=jnp.int32) < counts[0, 0]).astype(jnp.float32)
    id_piece = jnp.zeros((8, 128), jnp.int32).at[0, :slot_total].set(item_ids)

    group_rows, id_rows, user_rows = exchange(
        [(("uy",), (y_size,), "bcast"), (("ux",), (x_size,), "bcast"), (("iz", "ic"), (z_size, c_size), "bcast")],
        [item_factor, id_piece, user_factor],
        0,
    )
    user_block_total = z_size * c_size * user_own
    user_hot = (user_ids[:, None] == jnp.arange(user_block_total, dtype=jnp.int32)[None, :]).astype(jnp.float32)
    user_hot = user_hot.reshape(slot_total, z_size * c_size, user_own)
    user_sel = jnp.einsum(
        "svt,vrta->sra", user_hot, user_rows.reshape(z_size * c_size, rank_size, user_own, user_width),
        precision=HIGHEST)

    wanted = id_rows[:, 0, :slot_total]
    owner_group = wanted // group_blocks
    local_block = wanted % group_blocks
    hot = jnp.where(
        (owner_group == me_x)[:, :, None],
        (local_block[:, :, None] == jnp.arange(group_blocks, dtype=jnp.int32)[None, None, :]).astype(jnp.float32),
        0.0,
    ).reshape(x_size, slot_total, y_size, item_own)
    send = jnp.einsum(
        "xsyl,yrlb->xsrb", hot, group_rows.reshape(y_size, rank_size, item_own, item_width), precision=HIGHEST)
    (got,) = exchange([(("ux",), (x_size,), "a2a")], [send], 1)
    item_sel = jnp.sum(got, axis=0)

    data = tiles[0, 0]
    by_items = jnp.einsum("skab,srb->srka", data, item_sel, precision=HIGHEST)
    user_terms = jnp.einsum("srka,kr->sra", by_items, week_factor, precision=HIGHEST) * live[:, None, None]
    by_users = jnp.einsum("skab,sra->srkb", data, user_sel, precision=HIGHEST)
    item_terms = jnp.einsum("srkb,kr->srb", by_users, week_factor, precision=HIGHEST) * live[:, None, None]

    part_users = jnp.einsum("svt,sra->vrta", user_hot, user_terms, precision=HIGHEST).reshape(
        z_size * c_size, rank_size, user_own * user_width)
    all_terms, user_parts = exchange(
        [(("ux",), (x_size,), "bcast"), (("iz", "ic"), (z_size, c_size), "a2a")], [item_terms, part_users], 2)
    m_users = jnp.sum(user_parts, axis=0)

    part_items = jnp.einsum("xsyl,xsrb->yrlb", hot, all_terms, precision=HIGHEST).reshape(
        y_size, rank_size, item_own * item_width)
    (item_parts,) = exchange([(("uy",), (y_size,), "a2a")], [part_items], 3)
    m_items = jnp.sum(item_parts, axis=0)
    return (m_users, m_items)


def solution(mesh):
    users, items = mesh.shape["users"], mesh.shape["items"]
    devices = np.asarray(mesh.devices).reshape(users // 4, 4, items // 2, 2)
    fine = Mesh(devices, ("ux", "uy", "iz", "ic"))
    rows = ("ux", "uy")
    cols = ("iz", "ic")
    return jax.shard_map(
        on_device,
        mesh=fine,
        in_specs=(
            P(rows, cols, None, None, None, None),
            P(rows, cols, None),
            P(rows, cols, None),
            P(rows, cols),
            P(None, rows + cols),
            P(None, cols + rows),
            P(),
        ),
        out_specs=(P(None, rows + cols), P(None, cols + rows)),
        check_vma=False,
    )
```

time: 143 us -> 118 us (0.83)
  Pallas kernels: 0 us -> 64.4 us
  waiting for transfers between devices: 52.6 us -> 0 us
  blocking collectives: 36.8 us -> 0 us
  between operations: 14.5 us -> 1.43 us
  other arithmetic: 0.11 us -> 5.58 us
  local copies, waits for them, and re-layouts: 5.19 us -> 9.99 us
  matrix products: 32.7 us -> 35.9 us
    pallas_call x0 -> x4, Pallas kernels: none -> 64.4 us  [exchange(): pl.pallas_call(functools.partial(_exchange_kernel, plan), out_shape=tuple...]
    reduce_scatter x3 -> x0, waiting for transfers between devices: 50.4 us -> none  [the longest x1 26.6 us: on_device(): lax.psum_scatter(part_items, 'uy', scatter_dimension=1, tiled=True)]
    all_gather x3 -> x0, blocking collectives: 36.8 us -> none  [the longest x1 17.1 us: on_device(): user_rows = lax.all_gather(user_factor, ('iz', 'ic'), axis=1, tiled=True)]
    reduce_sum x0 -> x3, other arithmetic: none -> 4.8 us  [the longest x1 2.01 us: on_device(): m_items = jnp.sum(item_parts, axis=0)]
    reshape x0 -> x4, local copies, waits for them, and re-layouts: none -> 4.47 us  [the longest x2 1.96 us: on_device(): jnp.einsum('xsyl,xsrb->yrlb', hot, all_terms, precision=HIGHEST)]
    dot_general x4, matrix products: 2.99 us -> 5.92 us  [the longest x1 2.45 us: on_device(): jnp.einsum('xsyl,xsrb->yrlb', hot, all_terms, precision=HIGHEST)]
    unnamed x9 -> x4, local copies, waits for them, and re-layouts: 4.14 us -> 2.22 us
    all_gather x1 -> x0, waiting for transfers between devices: 1.46 us -> none  [on_device(): group_rows = lax.all_gather(item_factor, 'uy', axis=1, tiled=True)]
  transfers between devices with their start and end apart: 4 -> 0, of which waited for: 4 -> 0; matrix products, arithmetic and copies ran while one was open for 11% -> 0% of each run, Pallas kernels for 0% -> 0%
where the time goes in v2:
time: 118 us; the launch traced here: 117 us
  Pallas kernels  64.4 us (55%)
  matrix products  35.9 us (30%)
  local copies, waits for them, and re-layouts  9.99 us (8%)
  other arithmetic  5.58 us (5%)
  between operations  1.43 us (1%)
    pallas_call x4, Pallas kernels, exchange(): pl.pallas_call(functools.partial(_exchange_kernel, plan), out_shape=tuple...  64.4 us
    dot_general x1, matrix products, on_device(): by_items = jnp.einsum('skab,srb->srka', data, item_sel, precision=HIGHEST)  11.6 us
    dot_general x1, matrix products, on_device(): by_users = jnp.einsum('skab,sra->srkb', data, user_sel, precision=HIGHEST)  7.02 us
    dot_general x1, matrix products, on_device(): jnp.einsum('srkb,kr->srb', by_users, week_factor, precision=HIGHEST)  5.65 us
    dot_general x1, matrix products, on_device(): jnp.einsum('srka,kr->sra', by_items, week_factor, precision=HIGHEST)  5.65 us
    dot_general x1, matrix products, on_device(): jnp.einsum('xsyl,xsrb->yrlb', hot, all_terms, precision=HIGHEST)  2.45 us

profile of v2, /device:TPU:1, one launch (start us, length us, event | category | flops | bytes accessed | tf_op | source)
XLA Modules:
  0.0 117.3 jit_solution(11962008546691690013)
XLA Ops:
  1.3 1.3 %scatter.4.refs_1_ = s32[8,128]{1,0:T(8,128)} pad(s32[1,4]{1,0:T(1,128)} %bitcast.72, s32[]{:T(128)} %constant.56.clone.1), padding=0_7x0_124 | pad | bytes 4116 | tf_op jit(solution)/shard_map/scatter | solution.py:115
  2.6 0.8 copy.20
  3.4 22.7 %shard_map.86 = (f32[4,64,1024]{2,1,0:T(8,128)}, s32[4,8,128]{2,1,0:T(8,128)}, f32[8,64,256]{2,1,0:T(8,128)}) custom-call(f32[64,1024]{1,0:T(8,128)} %refs_0_.1, s32[8,128]{1,0:T(8,128)} %scatter.4.refs_1_, f32[64,256]{1,0:T(8,128)} %refs_2_.1), custom_call_target="tpu_custom_call" | custom-call | tf_op jit(solution)/shard_map/pallas_call | solution.py:87
  26.1 1.3 %reshape.122 = f32[8,64,2,128]{3,2,1,0:T(2,128)S(1)} reshape(f32[8,64,256]{2,1,0:T(8,128)} %get-tuple-element.19) | data formatting | bytes 1048576 | tf_op jit(solution)/shard_map/reshape | solution.py:126
  27.4 1.3 %fusion.11 = f32[4,64,128,1]{2,0,3,1:T(4,128)S(1)} fusion(f32[8,64,2,128]{3,2,1,0:T(2,128)S(1)} %reshape.122, s32[8,2]{0,1:T(2,128)S(1)} %multiply_add_fusion.1, s32[4]{0:T(128)} %bitcast.70), kind=kOutput, calls=%fused_computation.14 | convolution fusion | flops 6291520 | bytes 655440 | tf_op jit(solution)/shard_map/svt,vrta->sra/dot_general | solution.py:125
  28.7 0.7 slice.19
  29.6 1.4 %copy.40 = f32[32,8,8,128]{3,2,1,0:T(8,128)S(1)} copy(f32[32,8,8,128]{3,1,2,0:T(8,128)} %bitcast.65) | data formatting | bytes 2097152
  31.1 1.7 %fusion.8 = f32[4,4,64,128,1]{3,0,4,2,1:T(4,128)S(1)} fusion(f32[4,64,8,128,1]{3,2,1,0,4:T(8,128)S(1)} %bitcast.63, s32[4,8]{1,0:T(4,128)S(1)} %multiply_add_fusion, s32[4,4]{0,1:T(4,128)S(1)} %copy.10, pred[4,4]{0,1:T(4,128)(4,1)S(1)} %copy.9), kind=kOutput, calls=%fused_computation.10 | convolution fusion | flops 50333184 | bytes 1573072 | tf_op jit(solution)/shard_map/xsyl,yrlb->xsrb/dot_general | solution.py:137
  32.8 0.8 copy.60
  33.6 11.1 %shard_map.87 = f32[4,4,64,128]{3,2,1,0:T(8,128)} custom-call(f32[4,4,64,128]{3,2,1,0:T(8,128)} %bitcast.64), custom_call_target="tpu_custom_call" | custom-call | tf_op jit(solution)/shard_map/pallas_call | solution.py:87
  44.7 1.1 reduce_sum.27
  45.8 11.6 %fusion = f32[4,64,32,128]{3,1,2,0:T(8,128)S(1)} fusion(f32[1,1,4,32,128,128]{5,4,3,2,1,0:T(8,128)} %param.9, f32[4,64,128]{2,1,0:T(8,128)S(1)} %reduce_sum.27), kind=kOutput, calls=%fused_computation | convolution fusion | flops 1610612736 | bytes 12713984 | tf_op jit(solution)/shard_map/skab,srb->srka/dot_general | solution.py:143
  57.4 5.7 %fusion.4 = f32[64,1,4,128]{3,1,2,0:T(1,128)S(1)} fusion(f32[32,64,1,1]{0,2,3,1:T(1,128)S(1)} %copy.20, f32[4,64,32,128]{3,1,2,0:T(8,128)S(1)} %fusion), kind=kOutput, calls=%fused_computation.4 | convolution fusion | flops 12582912 | bytes 4333568 | tf_op jit(solution)/shard_map/srka,kr->sra/dot_general | solution.py:144
  63.1 7.0 %fusion.2 = f32[4,64,32,128]{3,1,2,0:T(8,128)S(1)} fusion(f32[1,1,4,32,128,128]{5,4,3,2,1,0:T(8,128)} %param.9, f32[4,64,128,1]{2,0,3,1:T(4,128)S(1)} %fusion.11), kind=kOutput, calls=%fused_computation.2 | convolution fusion | flops 1610612736 | bytes 12713984 | tf_op jit(solution)/shard_map/skab,sra->srkb/dot_general | solution.py:145
  70.1 5.7 %fusion.6 = f32[64,1,4,128]{3,1,2,0:T(1,128)S(1)} fusion(f32[32,64,1,1]{0,2,3,1:T(1,128)S(1)} %copy.20, f32[4,64,32,128]{3,1,2,0:T(8,128)S(1)} %fusion.2), kind=kOutput, calls=%fused_computation.6 | convolution fusion | flops 12582912 | bytes 4333568 | tf_op jit(solution)/shard_map/srkb,kr->srb/dot_general | solution.py:146
  75.8 0.7 fusion.15
  76.5 0.5 convolution_bitcast_fusion.1
  77.3 1.2 %reshape.124.refs_1_ = f32[8,64,256]{2,1,0:T(8,128)} reshape(f32[8,64,2,128]{3,2,1,0:T(2,128)S(1)} %copy.12) | data formatting | bytes 1048576 | tf_op jit(solution)/shard_map/reshape | solution.py:148
  78.5 13.9 %shard_map.88 = (f32[4,4,64,128]{3,2,1,0:T(8,128)}, f32[8,64,256]{2,1,0:T(8,128)}) custom-call(f32[4,64,128]{2,1,0:T(8,128)} %get-tuple-element.25.refs_0_, f32[8,64,256]{2,1,0:T(8,128)} %reshape.124.refs_1_), custom_call_target="tpu_custom_call" | custom-call | tf_op jit(solution)/shard_map/pallas_call | solution.py:87
  92.4 1.7 %reduce_sum.28 = f32[64,256]{1,0:T(8,128)} reduce(f32[8,64,256]{2,1,0:T(8,128)} %get-tuple-element.22, f32[]{:T(128)} %constant.65.clone.1), dimensions={0}, to_apply=%region_1.2 | reduce | flops 114688 | bytes 589828 | tf_op jit(solution)/shard_map/reduce_sum | solution.py:152
  94.1 2.4 %convolution_bitcast_fusion = f32[4,64,8,128]{3,2,0,1:T(8,128)S(1)} fusion(f32[4,4,64,128,1]{3,2,1,0,4:T(8,128)} %bitcast.66, s32[4,8]{1,0:T(4,128)S(1)} %multiply_add_fusion, s32[4,4]{0,1:T(4,128)S(1)} %copy.10, pred[4,4]{0,1:T(4,128)(4,1)S(1)} %copy.9), kind=kOutput, calls=%fused_computation.8 | convolution fusion | flops 50333184 | bytes 1573072 | tf_op jit(solution)/shard_map/xsyl,xsrb->yrlb/dot_general | solution.py:154
  97.0 1.6 %copy.39.refs_0_ = f32[4,64,1024]{2,1,0:T(8,128)} copy(f32[4,64,1024]{2,0,1:T(4,128)S(1)} %reshape.140) | data formatting | bytes 2097152 | tf_op jit(solution)/shard_map/reshape | solution.py:154
  98.6 16.7 %shard_map.89 = f32[4,64,1024]{2,1,0:T(8,128)} custom-call(f32[4,64,1024]{2,1,0:T(8,128)} %copy.39.refs_0_), custom_call_target="tpu_custom_call" | custom-call | tf_op jit(solution)/shard_map/pallas_call | solution.py:87
  115.3 2.0 %reduce_sum.29 = f32[64,1024]{1,0:T(8,128)} reduce(f32[4,64,1024]{2,1,0:T(8,128)} %shard_map.89, f32[]{:T(128)} %constant.65.clone.1), dimensions={0}, to_apply=%region_2.3 | reduce | flops 196608 | bytes 1310724 | tf_op jit(solution)/shard_map/reduce_sum | solution.py:157
  (11 shorter events, 0.9 us)
Async XLA Ops:
  70.1 6.4 %copy-start = (s32[1,1,4]{2,1,0:T(1,128)S(1)}, s32[1,1,4]{2,1,0:T(1,128)}, u32[]{:S(2)}) copy-start(s32[1,1,4]{2,1,0:T(1,128)} %param.10) | copy-start | bytes 52

commit v3 on v2

--- a/solution.py
+++ b/solution.py
@@ -97,6 +97,46 @@
 HIGHEST = lax.Precision.HIGHEST
 
 
+def _terms_kernel(x_ref, isel_ref, usel_ref, w_ref, wt_ref, uterm_ref, iterm_ref):
+    weeks, users, items = x_ref.shape[1], x_ref.shape[2], x_ref.shape[3]
+    flat = x_ref[0].reshape(weeks * users, items)
+    by_items = lax.dot_general(
+        flat, isel_ref[0], (((1,), (1,)), ((), ())), precision=HIGHEST, preferred_element_type=jnp.float32)
+    weighted = by_items.reshape(weeks, users, -1) * w_ref[...][:, None, :]
+    uterm_ref[0] = jnp.sum(weighted, axis=0).T
+    usel = usel_ref[0]
+    wt = wt_ref[...]
+    stacked = jnp.concatenate([usel * wt[:, k:k + 1] for k in range(weeks)], axis=1)
+    iterm_ref[0] = jnp.dot(stacked, flat, precision=HIGHEST, preferred_element_type=jnp.float32)
+
+
+def slot_terms(data, item_sel, user_sel, week_factor):
+    slots, weeks, users, items = data.shape
+    rank = week_factor.shape[1]
+    return pl.pallas_call(
+        _terms_kernel,
+        grid=(slots,),
+        out_shape=(
+            jax.ShapeDtypeStruct((slots, rank, users), jnp.float32),
+            jax.ShapeDtypeStruct((slots, rank, items), jnp.float32),
+        ),
+        in_specs=[
+            pl.BlockSpec((1, weeks, users, items), lambda s: (s, 0, 0, 0)),
+            pl.BlockSpec((1, rank, items), lambda s: (s, 0, 0)),
+            pl.BlockSpec((1, rank, users), lambda s: (s, 0, 0)),
+            pl.BlockSpec((weeks, rank), lambda s: (0, 0)),
+            pl.BlockSpec((rank, weeks), lambda s: (0, 0)),
+        ],
+        out_specs=(
+            pl.BlockSpec((1, rank, users), lambda s: (s, 0, 0)),
+            pl.BlockSpec((1, rank, items), lambda s: (s, 0, 0)),
+        ),
+        cost_estimate=pl.CostEstimate(
+            flops=4 * slots * weeks * users * items * rank, transcendentals=0,
+            bytes_accessed=4 * slots * weeks * users * items),
+    )(data, item_sel, user_sel, week_factor, week_factor.T)
+
+
 def on_device(tiles, user_blocks, item_blocks, counts, user_factor, item_factor, week_factor):
     x_size, y_size = lax.axis_size("ux"), lax.axis_size("uy")
     z_size, c_size = lax.axis_size("iz"), lax.axis_size("ic")
@@ -139,11 +179,9 @@
     (got,) = exchange([(("ux",), (x_size,), "a2a")], [send], 1)
     item_sel = jnp.sum(got, axis=0)
 
-    data = tiles[0, 0]
-    by_items = jnp.einsum("skab,srb->srka", data, item_sel, precision=HIGHEST)
-    user_terms = jnp.einsum("srka,kr->sra", by_items, week_factor, precision=HIGHEST) * live[:, None, None]
-    by_users = jnp.einsum("skab,sra->srkb", data, user_sel, precision=HIGHEST)
-    item_terms = jnp.einsum("srkb,kr->srb", by_users, week_factor, precision=HIGHEST) * live[:, None, None]
+    user_terms, item_terms = slot_terms(tiles[0, 0], item_sel, user_sel, week_factor)
+    user_terms = user_terms * live[:, None, None]
+    item_terms = item_terms * live[:, None, None]
 
     part_users = jnp.einsum("svt,sra->vrta", user_hot, user_terms, precision=HIGHEST).reshape(
         z_size * c_size, rank_size, user_own * user_width)

time: 118 us -> 103 us (0.87)
  matrix products: 35.9 us -> 5.98 us
  Pallas kernels: 64.4 us -> 77.8 us
    dot_general x4 -> x0, matrix products: 30 us -> none  [the longest x1 11.6 us: on_device(): by_items = jnp.einsum('skab,srb->srka', data, item_sel, precision=HIGHEST)]
    pallas_call x0 -> x1, Pallas kernels: none -> 13.5 us  [slot_terms(): pl.pallas_call(_terms_kernel, grid=(slots,), out_shape=(jax.ShapeDtypeStr...]
where the time goes in v3:
time: 103 us; the launch traced here: 102 us
  Pallas kernels  77.8 us (76%)
  local copies, waits for them, and re-layouts  10.6 us (10%)
  other arithmetic  6.16 us (6%)
  matrix products  5.98 us (6%)
  between operations  1.41 us (1%)
    pallas_call x4, Pallas kernels, exchange(): pl.pallas_call(functools.partial(_exchange_kernel, plan), out_shape=tuple...  64.3 us
    pallas_call x1, Pallas kernels, slot_terms(): pl.pallas_call(_terms_kernel, grid=(slots,), out_shape=(jax.ShapeDtypeStr...  13.5 us
    dot_general x1, matrix products, on_device(): jnp.einsum('xsyl,xsrb->yrlb', hot, all_terms, precision=HIGHEST)  2.51 us
    unnamed x8, local copies, waits for them, and re-layouts  2.15 us

profile of v3, /device:TPU:1, one launch (start us, length us, event | category | flops | bytes accessed | tf_op | source)
XLA Modules:
  0.0 101.9 jit_solution(6426976211653362222)
XLA Ops:
  0.6 1.3 %scatter.4.refs_1_ = s32[8,128]{1,0:T(8,128)} pad(s32[1,4]{1,0:T(1,128)} %bitcast.59, s32[]{:T(128)} %constant.55.clone.1), padding=0_7x0_124 | pad | bytes 4116 | tf_op jit(solution)/shard_map/scatter | solution.py:155
  1.9 22.7 %shard_map.86 = (f32[4,64,1024]{2,1,0:T(8,128)}, s32[4,8,128]{2,1,0:T(8,128)}, f32[8,64,256]{2,1,0:T(8,128)}) custom-call(f32[64,1024]{1,0:T(8,128)} %refs_0_.1, s32[8,128]{1,0:T(8,128)} %scatter.4.refs_1_, f32[64,256]{1,0:T(8,128)} %refs_2_.1), custom_call_target="tpu_custom_call" | custom-call | tf_op jit(solution)/shard_map/pallas_call | solution.py:87
  24.6 0.7 slice.19
  25.5 1.4 %copy.36 = f32[32,8,8,128]{3,2,1,0:T(8,128)S(1)} copy(f32[32,8,8,128]{3,1,2,0:T(8,128)} %bitcast.52) | data formatting | bytes 2097152
  27.0 1.7 %convolution_bitcast_fusion.2 = f32[4,4,64,128]{3,0,2,1:T(4,128)S(1)} fusion(s32[4,8]{1,0:T(4,128)S(1)} %multiply_add_fusion, s32[4,4]{0,1:T(4,128)S(1)} %copy.10, pred[4,4]{0,1:T(4,128)(4,1)S(1)} %copy.9, f32[4,64,8,128]{3,2,1,0:T(8,128)S(1)} %bitcast.51), kind=kOutput, calls=%fused_computation.2 | convolution fusion | flops 50333184 | bytes 1573072 | tf_op jit(solution)/shard_map/xsyl,yrlb->xsrb/dot_general | solution.py:177
  28.6 0.8 copy.13.refs_0_
  29.5 11.1 %shard_map.87 = f32[4,4,64,128]{3,2,1,0:T(8,128)} custom-call(f32[4,4,64,128]{3,2,1,0:T(8,128)} %copy.13.refs_0_), custom_call_target="tpu_custom_call" | custom-call | tf_op jit(solution)/shard_map/pallas_call | solution.py:87
  40.6 1.7 %reduce_sum.27.isel_ref = f32[4,64,128]{2,1,0:T(8,128)} reduce(f32[4,4,64,128]{3,2,1,0:T(8,128)} %shard_map.87, f32[]{:T(128)} %constant.64.clone.1), dimensions={0}, to_apply=%region_0.0 | reduce | flops 98304 | bytes 655364 | tf_op jit(solution)/shard_map/reduce_sum | solution.py:180
  42.3 1.3 %reshape.123 = f32[8,64,2,128]{3,2,1,0:T(2,128)S(1)} reshape(f32[8,64,256]{2,1,0:T(8,128)} %get-tuple-element.23) | data formatting | bytes 1048576 | tf_op jit(solution)/shard_map/reshape | solution.py:166
  43.7 1.3 %convolution_bitcast_fusion.3 = f32[4,64,128]{2,0,1:T(4,128)S(1)} fusion(f32[8,64,2,128]{3,2,1,0:T(2,128)S(1)} %reshape.123, s32[8,2]{0,1:T(2,128)S(1)} %multiply_add_fusion.1, s32[4]{0:T(128)} %bitcast.57), kind=kOutput, calls=%fused_computation.3 | convolution fusion | flops 6291520 | bytes 655440 | tf_op jit(solution)/shard_map/svt,vrta->sra/dot_general | solution.py:165
  45.0 0.6 copy.16.usel_ref
  45.6 0.7 copy.15
  46.3 13.5 %shard_map.88 = (f32[4,64,128]{2,1,0:T(8,128)}, f32[4,64,128]{2,1,0:T(8,128)}) custom-call(f32[4,32,128,128]{3,2,1,0:T(8,128)} %bitcast.50, f32[4,64,128]{2,1,0:T(8,128)} %reduce_sum.27.isel_ref, f32[4,64,128]{2,1,0:T(8,128)} %copy.16.usel_ref, f32[32,64]{1,0:T(8,128)} %w_ref.1, f32[64,32]{1,0:T(8,128)} %bitcast.54), custom_call_target="tpu_custom_call" | custom-call | flops 536870912 | bytes 8388608 | tf_op jit(solution)/shard_map/pallas_call | solution.py:116
  60.4 1.7 %multiply_bitcast_fusion = (f32[4,64,128,1]{2,1,0,3:T(8,128)S(1)}, f32[4,64,128]{2,1,0:T(8,128)}) fusion(f32[4,64,128]{2,1,0:T(8,128)} %get-tuple-element.25, f32[4]{0:T(128)S(1)} %compare_convert_fusion, f32[4,64,128]{2,1,0:T(8,128)} %get-tuple-element.24), kind=kLoop, calls=%fused_computation.9 | loop fusion | flops 65536 | bytes 524304 | tf_op jit(solution)/shard_map/mul | solution.py:183
  62.2 0.5 convolution_bitcast_fusion.1
  62.6 0.3 copy.18
  62.9 1.2 %reshape.124.refs_1_ = f32[8,64,256]{2,1,0:T(8,128)} reshape(f32[8,64,2,128]{3,2,1,0:T(2,128)S(1)} %copy.18) | data formatting | bytes 1048576 | tf_op jit(solution)/shard_map/reshape | solution.py:186
  64.1 13.9 %shard_map.89 = (f32[4,4,64,128]{3,2,1,0:T(8,128)}, f32[8,64,256]{2,1,0:T(8,128)}) custom-call(f32[4,64,128]{2,1,0:T(8,128)} %get-tuple-element.29.refs_0_, f32[8,64,256]{2,1,0:T(8,128)} %reshape.124.refs_1_), custom_call_target="tpu_custom_call" | custom-call | tf_op jit(solution)/shard_map/pallas_call | solution.py:87
  78.1 2.5 %convolution_bitcast_fusion = f32[4,64,8,128]{3,2,0,1:T(8,128)S(1)} fusion(f32[4,4,64,128,1]{3,2,1,0,4:T(8,128)} %bitcast.53, s32[4,8]{1,0:T(4,128)S(1)} %multiply_add_fusion, s32[4,4]{0,1:T(4,128)S(1)} %copy.10, pred[4,4]{0,1:T(4,128)(4,1)S(1)} %copy.9), kind=kOutput, calls=%fused_computation | convolution fusion | flops 50333184 | bytes 1573072 | tf_op jit(solution)/shard_map/xsyl,xsrb->yrlb/dot_general | solution.py:192
  80.6 0.4 reshape.135
  80.9 1.6 %copy.35.refs_0_ = f32[4,64,1024]{2,1,0:T(8,128)} copy(f32[4,64,1024]{2,0,1:T(4,128)S(1)} %reshape.135) | data formatting | bytes 2097152 | tf_op jit(solution)/shard_map/reshape | solution.py:192
  82.5 16.7 %shard_map.90 = f32[4,64,1024]{2,1,0:T(8,128)} custom-call(f32[4,64,1024]{2,1,0:T(8,128)} %copy.35.refs_0_), custom_call_target="tpu_custom_call" | custom-call | tf_op jit(solution)/shard_map/pallas_call | solution.py:87
  99.2 2.0 %reduce_sum.29 = f32[64,1024]{1,0:T(8,128)} reduce(f32[4,64,1024]{2,1,0:T(8,128)} %shard_map.90, f32[]{:T(128)} %constant.64.clone.1), dimensions={0}, to_apply=%region_2.3 | reduce | flops 196608 | bytes 1310724 | tf_op jit(solution)/shard_map/reduce_sum | solution.py:195
  101.2 0.7 reduce_sum.28
  (13 shorter events, 0.3 us)
Async XLA Ops:
  0.6 45.0 %copy-start.1 = (f32[32,64]{1,0:T(8,128)S(1)}, f32[32,64]{1,0:T(8,128)}, u32[]{:S(2)}) copy-start(f32[32,64]{1,0:T(8,128)} %w_ref.1) | copy-start | bytes 24580
  25.5 36.6 %copy-start.2 = (s32[1,1,4]{2,1,0:T(1,128)S(1)}, s32[1,1,4]{2,1,0:T(1,128)}, u32[]{:S(2)}) copy-start(s32[1,1,4]{2,1,0:T(1,128)} %param.10) | copy-start | bytes 52
  78.0 23.2 %copy-start = (f32[8,64,256]{2,1,0:T(8,128)S(1)}, f32[8,64,256]{2,1,0:T(8,128)}, u32[]{:S(2)}) copy-start(f32[8,64,256]{2,1,0:T(8,128)} %get-tuple-element.26) | copy-start | bytes 1572868

commit v4 on v3

--- a/solution.py
+++ b/solution.py
@@ -95,6 +95,7 @@
 
 
 HIGHEST = lax.Precision.HIGHEST
+Y_SPLIT = 4
 
 
 def _terms_kernel(x_ref, isel_ref, usel_ref, w_ref, wt_ref, uterm_ref, iterm_ref):
@@ -108,6 +109,158 @@
     wt = wt_ref[...]
     stacked = jnp.concatenate([usel * wt[:, k:k + 1] for k in range(weeks)], axis=1)
     iterm_ref[0] = jnp.dot(stacked, flat, precision=HIGHEST, preferred_element_type=jnp.float32)
+
+
+def _fused_kernel(hot_ref, tiles_hbm, send_sel, usel_ref, w_ref, wt_ref, terms_out, parts_out,
+                  xbuf, xsem, land_sel, iterm, land_terms, upart, land_up,
+                  sel_s, sel_r, trm_s, trm_r, up_s, up_r):
+    slots, weeks, users, items = xbuf.shape
+    n_x = send_sel.shape[0]
+    n_z, n_c = lax.axis_size("iz"), lax.axis_size("ic")
+    n_v = n_z * n_c
+    per_owner = parts_out.shape[2] // users
+    me_x = lax.axis_index("ux")
+    me_v = lax.axis_index("iz") * n_c + lax.axis_index("ic")
+
+    def xpeer(d):
+        return {"ux": d}
+
+    def vpeer(d):
+        return {"iz": d // n_c, "ic": d % n_c}
+
+    barrier = pltpu.get_barrier_semaphore()
+    for k in range(1, n_x):
+        pl.semaphore_signal(barrier, inc=1, device_id=xpeer(lax.rem(me_x + k, n_x)), device_id_type=MESH_IDS)
+    for k in range(1, n_v):
+        pl.semaphore_signal(barrier, inc=1, device_id=vpeer(lax.rem(me_v + k, n_v)), device_id_type=MESH_IDS)
+    pl.semaphore_wait(barrier, n_x - 1 + n_v - 1)
+
+    loads = []
+    for s in range(slots):
+        cp = pltpu.make_async_copy(tiles_hbm.at[s], xbuf.at[s], xsem.at[s])
+        cp.start()
+        loads.append(cp)
+
+    sel_copies = []
+    for k in range(1, n_x):
+        d = lax.rem(me_x + k, n_x)
+        cp = pltpu.make_async_remote_copy(
+            src_ref=send_sel.at[d], dst_ref=land_sel.at[me_x], send_sem=sel_s.at[k], recv_sem=sel_r.at[k],
+            device_id=xpeer(d), device_id_type=MESH_IDS)
+        cp.start()
+        sel_copies.append((k, cp))
+
+    wt = wt_ref[...]
+    for s in range(slots):
+        loads[s].wait()
+        flat = xbuf[s].reshape(weeks * users, items)
+        usel = usel_ref[s]
+        stacked = jnp.concatenate([usel * wt[:, k:k + 1] for k in range(weeks)], axis=1)
+        iterm[s] = jnp.dot(stacked, flat, precision=HIGHEST, preferred_element_type=jnp.float32)
+
+    trm_copies = []
+    for k in range(1, n_x):
+        d = lax.rem(me_x + k, n_x)
+        cp = pltpu.make_async_remote_copy(
+            src_ref=iterm, dst_ref=land_terms.at[me_x], send_sem=trm_s.at[k], recv_sem=trm_r.at[k],
+            device_id=xpeer(d), device_id_type=MESH_IDS)
+        cp.start()
+        trm_copies.append((k, cp))
+
+    for k, cp in sel_copies:
+        cp.wait_send()
+        src = lax.rem(me_x + n_x - k, n_x)
+        pltpu.make_async_remote_copy(
+            src_ref=land_sel.at[src], dst_ref=land_sel.at[src], send_sem=sel_s.at[k], recv_sem=sel_r.at[k],
+            device_id=xpeer(src), device_id_type=MESH_IDS).wait_recv()
+
+    w = w_ref[...]
+    uterms = []
+    for s in range(slots):
+        isel = send_sel[me_x, s]
+        for k in range(1, n_x):
+            isel = isel + land_sel[lax.rem(me_x + k, n_x), s]
+        flat = xbuf[s].reshape(weeks * users, items)
+        by_items = lax.dot_general(
+            flat, isel, (((1,), (1,)), ((), ())), precision=HIGHEST, preferred_element_type=jnp.float32)
+        weighted = by_items.reshape(weeks, users, -1) * w[:, None, :]
+        uterms.append(jnp.sum(weighted, axis=0).T)
+
+    for v in range(n_v):
+        for t in range(per_owner):
+            col = v * per_owner + t
+            acc = uterms[0] * hot_ref[col]
+            for s in range(1, slots):
+                acc = acc + uterms[s] * hot_ref[s * n_v * per_owner + col]
+            upart[v, :, t * users:(t + 1) * users] = acc
+
+    up_copies = []
+    for k in range(1, n_v):
+        d = lax.rem(me_v + k, n_v)
+        cp = pltpu.make_async_remote_copy(
+            src_ref=upart.at[d], dst_ref=land_up.at[me_v], send_sem=up_s.at[k], recv_sem=up_r.at[k],
+            device_id=vpeer(d), device_id_type=MESH_IDS)
+        cp.start()
+        up_copies.append((k, cp))
+
+    for k, cp in trm_copies:
+        cp.wait_send()
+        src = lax.rem(me_x + n_x - k, n_x)
+        pltpu.make_async_remote_copy(
+            src_ref=land_terms.at[src], dst_ref=land_terms.at[src], send_sem=trm_s.at[k], recv_sem=trm_r.at[k],
+            device_id=xpeer(src), device_id_type=MESH_IDS).wait_recv()
+    for k, cp in up_copies:
+        cp.wait_send()
+        src = lax.rem(me_v + n_v - k, n_v)
+        pltpu.make_async_remote_copy(
+            src_ref=land_up.at[src], dst_ref=land_up.at[src], send_sem=up_s.at[k], recv_sem=up_r.at[k],
+            device_id=vpeer(src), device_id_type=MESH_IDS).wait_recv()
+
+    for k in range(1, n_x):
+        src = lax.rem(me_x + k, n_x)
+        terms_out[src] = land_terms[src]
+    terms_out[me_x] = iterm[...]
+    for k in range(1, n_v):
+        src = lax.rem(me_v + k, n_v)
+        parts_out[src] = land_up[src]
+    parts_out[me_v] = upart[me_v]
+
+
+def fused_middle(hot, data, send_sel, user_sel, week_factor, n_v, collective_id):
+    slots, weeks, users, items = data.shape
+    n_x = send_sel.shape[0]
+    rank = week_factor.shape[1]
+    per_owner = hot.shape[0] // (slots * n_v)
+    vmem = pl.BlockSpec(memory_space=pltpu.VMEM)
+    return pl.pallas_call(
+        _fused_kernel,
+        out_shape=(
+            jax.ShapeDtypeStruct((n_x, slots, rank, items), jnp.float32),
+            jax.ShapeDtypeStruct((n_v, rank, per_owner * users), jnp.float32),
+        ),
+        in_specs=[pl.BlockSpec(memory_space=pltpu.SMEM), pl.BlockSpec(memory_space=pl.ANY), vmem, vmem, vmem, vmem],
+        out_specs=(vmem, vmem),
+        scratch_shapes=[
+            pltpu.VMEM((slots, weeks, users, items), jnp.float32),
+            pltpu.SemaphoreType.DMA((slots,)),
+            pltpu.VMEM((n_x, slots, rank, items), jnp.float32),
+            pltpu.VMEM((slots, rank, items), jnp.float32),
+            pltpu.VMEM((n_x, slots, rank, items), jnp.float32),
+            pltpu.VMEM((n_v, rank, per_owner * users), jnp.float32),
+            pltpu.VMEM((n_v, rank, per_owner * users), jnp.float32),
+            pltpu.SemaphoreType.DMA((n_x,)),
+            pltpu.SemaphoreType.DMA((n_x,)),
+            pltpu.SemaphoreType.DMA((n_x,)),
+            pltpu.SemaphoreType.DMA((n_x,)),
+            pltpu.SemaphoreType.DMA((n_v,)),
+            pltpu.SemaphoreType.DMA((n_v,)),
+        ],
+        compiler_params=pltpu.CompilerParams(
+            collective_id=collective_id, has_side_effects=True, vmem_limit_bytes=48 * 1024 * 1024),
+        cost_estimate=pl.CostEstimate(
+            flops=4 * slots * weeks * users * items * rank, transcendentals=0,
+            bytes_accessed=4 * slots * weeks * users * items),
+    )(hot, data, send_sel, user_sel, week_factor, week_factor.T)
 
 
 def slot_terms(data, item_sel, user_sel, week_factor):
@@ -151,54 +304,48 @@
 
     user_ids = user_blocks[0, 0]
     item_ids = item_blocks[0, 0]
-    live = (jnp.arange(slot_total, dtype=jnp.int32) < counts[0, 0]).astype(jnp.float32)
-    id_piece = jnp.zeros((8, 128), jnp.int32).at[0, :slot_total].set(item_ids)
+    slot_order = jnp.arange(slot_total, dtype=jnp.int32)
+    live = (slot_order < counts[0, 0]).astype(jnp.float32)
+    id_piece = jnp.zeros((8, 128), jnp.int32).at[0, :slot_total].set(item_ids).at[1, 0].set(counts[0, 0])
 
     group_rows, id_rows, user_rows = exchange(
         [(("uy",), (y_size,), "bcast"), (("ux",), (x_size,), "bcast"), (("iz", "ic"), (z_size, c_size), "bcast")],
         [item_factor, id_piece, user_factor],
         0,
     )
-    user_block_total = z_size * c_size * user_own
+    n_v = z_size * c_size
+    user_block_total = n_v * user_own
     user_hot = (user_ids[:, None] == jnp.arange(user_block_total, dtype=jnp.int32)[None, :]).astype(jnp.float32)
-    user_hot = user_hot.reshape(slot_total, z_size * c_size, user_own)
+    user_hot = user_hot.reshape(slot_total, n_v, user_own)
     user_sel = jnp.einsum(
-        "svt,vrta->sra", user_hot, user_rows.reshape(z_size * c_size, rank_size, user_own, user_width),
-        precision=HIGHEST)
+        "svt,vrta->sra", user_hot, user_rows.reshape(n_v, rank_size, user_own, user_width),
+        precision=HIGHEST) * live[:, None, None]
 
     wanted = id_rows[:, 0, :slot_total]
+    wanted_live = slot_order[None, :] < id_rows[:, 1, 0:1]
     owner_group = wanted // group_blocks
     local_block = wanted % group_blocks
     hot = jnp.where(
-        (owner_group == me_x)[:, :, None],
+        ((owner_group == me_x) & wanted_live)[:, :, None],
         (local_block[:, :, None] == jnp.arange(group_blocks, dtype=jnp.int32)[None, None, :]).astype(jnp.float32),
         0.0,
     ).reshape(x_size, slot_total, y_size, item_own)
     send = jnp.einsum(
         "xsyl,yrlb->xsrb", hot, group_rows.reshape(y_size, rank_size, item_own, item_width), precision=HIGHEST)
-    (got,) = exchange([(("ux",), (x_size,), "a2a")], [send], 1)
-    item_sel = jnp.sum(got, axis=0)
-
-    user_terms, item_terms = slot_terms(tiles[0, 0], item_sel, user_sel, week_factor)
-    user_terms = user_terms * live[:, None, None]
-    item_terms = item_terms * live[:, None, None]
-
-    part_users = jnp.einsum("svt,sra->vrta", user_hot, user_terms, precision=HIGHEST).reshape(
-        z_size * c_size, rank_size, user_own * user_width)
-    all_terms, user_parts = exchange(
-        [(("ux",), (x_size,), "bcast"), (("iz", "ic"), (z_size, c_size), "a2a")], [item_terms, part_users], 2)
+    all_terms, user_parts = fused_middle(
+        user_hot.reshape(-1), tiles[0, 0], send, user_sel, week_factor, n_v, 1)
     m_users = jnp.sum(user_parts, axis=0)
 
     part_items = jnp.einsum("xsyl,xsrb->yrlb", hot, all_terms, precision=HIGHEST).reshape(
         y_size, rank_size, item_own * item_width)
-    (item_parts,) = exchange([(("uy",), (y_size,), "a2a")], [part_items], 3)
+    (item_parts,) = exchange([(("uy",), (y_size,), "a2a")], [part_items], 2)
     m_items = jnp.sum(item_parts, axis=0)
     return (m_users, m_items)
 
 
 def solution(mesh):
     users, items = mesh.shape["users"], mesh.shape["items"]
-    devices = np.asarray(mesh.devices).reshape(users // 4, 4, items // 2, 2)
+    devices = np.asarray(mesh.devices).reshape(users // Y_SPLIT, Y_SPLIT, items // 2, 2)
     fine = Mesh(devices, ("ux", "uy", "iz", "ic"))
     rows = ("ux", "uy")
     cols = ("iz", "ic")

time: 103 us -> 87.6 us (0.85)
  Pallas kernels: 77.8 us -> 68.2 us
  other arithmetic: 6.16 us -> 3.58 us
  matrix products: 5.98 us -> 4.41 us
  local copies, waits for them, and re-layouts: 10.6 us -> 9.43 us
    pallas_call x4 -> x2, Pallas kernels: 64.3 us -> 40.1 us  [exchange(): pl.pallas_call(functools.partial(_exchange_kernel, plan), out_shape=tuple...]
    pallas_call x1, Pallas kernels: 13.5 us -> 28.1 us  [fused_middle(): pl.pallas_call(_fused_kernel, out_shape=(jax.ShapeDtypeStruct((n_x, slots...]
    reduce_sum x1 -> x0, other arithmetic: 1.74 us -> none  [on_device(): item_sel = jnp.sum(got, axis=0)]
    mul x1, other arithmetic: 1.71 us -> 0.08 us  [on_device(): jnp.einsum('svt,vrta->sra', user_hot, user_rows.reshape(n_v, rank_size, u...]
    unnamed x8 -> x6, local copies, waits for them, and re-layouts: 2.15 us -> 3.53 us
    reshape x2 -> x1, local copies, waits for them, and re-layouts: 2.51 us -> 1.3 us  [on_device(): user_rows.reshape(n_v, rank_size, user_own, user_width)]
    dot_general x1, matrix products: 2.51 us -> 1.42 us  [on_device(): jnp.einsum('xsyl,xsrb->yrlb', hot, all_terms, precision=HIGHEST)]
where the time goes in v4:
time: 87.6 us; the launch traced here: 87.1 us
  Pallas kernels  68.2 us (78%)
  local copies, waits for them, and re-layouts  9.43 us (11%)
  matrix products  4.41 us (5%)
  other arithmetic  3.58 us (4%)
  between operations  1.4 us (2%)
    pallas_call x2, Pallas kernels, exchange(): pl.pallas_call(functools.partial(_exchange_kernel, plan), out_shape=tuple...  40.1 us
    pallas_call x1, Pallas kernels, fused_middle(): pl.pallas_call(_fused_kernel, out_shape=(jax.ShapeDtypeStruct((n_x, slots...  28.1 us
    unnamed x6, local copies, waits for them, and re-layouts  3.53 us
    reduce_sum x1, other arithmetic, on_device(): m_items = jnp.sum(item_parts, axis=0)  2.01 us
    reshape x2, local copies, waits for them, and re-layouts, on_device(): jnp.einsum('xsyl,xsrb->yrlb', hot, all_terms, precision=HIGHEST)  1.96 us

profile of v4, /device:TPU:1, one launch (start us, length us, event | category | flops | bytes accessed | tf_op | source)
XLA Modules:
  0.0 87.1 jit_solution(7180096135467855298)
XLA Ops:
  1.3 0.7 scatter.6
  2.0 0.6 copy-done.1
  2.6 22.7 %shard_map.86 = (f32[4,64,1024]{2,1,0:T(8,128)}, s32[4,8,128]{2,1,0:T(8,128)}, f32[8,64,256]{2,1,0:T(8,128)}) custom-call(f32[64,1024]{1,0:T(8,128)} %refs_0_.1, s32[8,128]{1,0:T(8,128)} %copy-done.1, f32[64,256]{1,0:T(8,128)} %refs_2_.1), custom_call_target="tpu_custom_call" | custom-call | tf_op jit(solution)/shard_map/pallas_call | solution.py:87
  25.2 0.7 slice.41
  26.0 0.9 %slice_reduce_fusion = s32[4]{0:T(128)S(1)} fusion(s32[4,8,128]{2,1,0:T(8,128)} %get-tuple-element.31), kind=kLoop, calls=%fused_computation.20 | loop fusion | bytes 32 | tf_op jit(solution)/shard_map/slice | solution.py:325
  26.8 0.1 fusion.11
  26.9 0.1 copy.19
  27.0 0.1 copy.20
  27.1 1.4 %copy.41 = f32[32,8,8,128]{3,2,1,0:T(8,128)S(1)} copy(f32[32,8,8,128]{3,1,2,0:T(8,128)} %bitcast.48) | data formatting | bytes 2097152
  28.6 1.7 %convolution_bitcast_fusion.1 = f32[4,4,64,128]{3,0,2,1:T(4,128)S(1)} fusion(s32[4,8]{1,0:T(4,128)S(1)} %multiply_add_fusion, s32[4,4]{0,1:T(4,128)S(1)} %copy.20, pred[4,4]{0,1:T(4,128)(4,1)S(1)} %copy.19, f32[4,64,8,128]{3,2,1,0:T(8,128)S(1)} %bitcast.47), kind=kOutput, calls=%fused_computation.1 | convolution fusion | flops 50333184 | bytes 1573072 | tf_op jit(solution)/shard_map/xsyl,yrlb->xsrb/dot_general | solution.py:333
  30.3 1.3 %reshape.179 = f32[8,64,2,128]{3,2,1,0:T(2,128)S(1)} reshape(f32[8,64,256]{2,1,0:T(8,128)} %get-tuple-element.33) | data formatting | bytes 1048576 | tf_op jit(solution)/shard_map/reshape | solution.py:321
  31.6 1.3 %convolution_bitcast_fusion.2 = f32[4,64,128]{2,0,1:T(4,128)S(1)} fusion(f32[8,64,2,128]{3,2,1,0:T(2,128)S(1)} %reshape.179, s32[8,2]{0,1:T(2,128)S(1)} %multiply_add_fusion.1, s32[4]{0:T(128)} %bitcast.51), kind=kOutput, calls=%fused_computation.2 | convolution fusion | flops 6291520 | bytes 655440 | tf_op jit(solution)/shard_map/svt,vrta->sra/dot_general | solution.py:320
  33.0 0.1 copy_multiply_fusion.usel_ref
  33.0 0.7 fusion.9
  33.8 0.1 reshape.181.hot_ref
  33.9 0.8 copy.25
  34.7 0.7 copy-done
  35.4 28.1 %shard_map.87 = (f32[4,4,64,128]{3,2,1,0:T(8,128)S(1)}, f32[8,64,256]{2,1,0:T(8,128)S(1)}) custom-call(f32[64]{0:T(128)S(1)} %reshape.181.hot_ref, f32[4,32,128,128]{3,2,1,0:T(8,128)} %bitcast.46, f32[4,4,64,128]{3,2,1,0:T(8,128)S(1)} %copy.26.send_sel, f32[4,64,128]{2,1,0:T(8,128)S(1)} %copy_multiply_fusion.usel_ref, f32[32,64]{1,0:T(8,128)S(1)} %copy-done, ...), custom_call_target="tpu_custom_call" | custom-call | flops 536870912 | bytes 8388608 | tf_op jit(solution)/shard_map/pallas_call | solution.py:235
  63.5 1.4 %convolution_bitcast_fusion = f32[4,64,8,128]{3,2,0,1:T(8,128)S(1)} fusion(f32[4,4,64,128,1]{3,2,1,0,4:T(8,128)S(1)} %bitcast.44, s32[4,8]{1,0:T(4,128)S(1)} %multiply_add_fusion, s32[4,4]{0,1:T(4,128)S(1)} %copy.20, pred[4,4]{0,1:T(4,128)(4,1)S(1)} %copy.19), kind=kOutput, calls=%fused_computation | convolution fusion | flops 50333184 | bytes 1573072 | tf_op jit(solution)/shard_map/xsyl,xsrb->yrlb/dot_general | solution.py:339
  64.9 0.4 reshape.190
  65.3 1.6 %copy.40.refs_0_ = f32[4,64,1024]{2,1,0:T(8,128)} copy(f32[4,64,1024]{2,0,1:T(4,128)S(1)} %reshape.190) | data formatting | bytes 2097152 | tf_op jit(solution)/shard_map/reshape | solution.py:339
  66.9 17.5 %shard_map.88 = f32[4,64,1024]{2,1,0:T(8,128)} custom-call(f32[4,64,1024]{2,1,0:T(8,128)} %copy.40.refs_0_), custom_call_target="tpu_custom_call" | custom-call | tf_op jit(solution)/shard_map/pallas_call | solution.py:87
  84.4 2.0 %reduce_sum.19 = f32[64,1024]{1,0:T(8,128)} reduce(f32[4,64,1024]{2,1,0:T(8,128)} %shard_map.88, f32[]{:T(128)} %constant.92.clone.1), dimensions={0}, to_apply=%region_1.0 | reduce | flops 196608 | bytes 1310724 | tf_op jit(solution)/shard_map/reduce_sum | solution.py:342
  86.4 0.7 reduce_sum.18
  (8 shorter events, 0.1 us)
Async XLA Ops:
  2.0 0.6 copy-start.1
  34.7 0.7 copy-start

commit v5 on v4

--- a/solution.py
+++ b/solution.py
@@ -111,19 +111,26 @@
     iterm_ref[0] = jnp.dot(stacked, flat, precision=HIGHEST, preferred_element_type=jnp.float32)
 
 
-def _fused_kernel(hot_ref, tiles_hbm, send_sel, usel_ref, w_ref, wt_ref, terms_out, parts_out,
-                  xbuf, xsem, land_sel, iterm, land_terms, upart, land_up,
-                  sel_s, sel_r, trm_s, trm_r, up_s, up_r):
+def _fused_kernel(hot_ref, tiles_hbm, send_sel, usel_ref, w_ref, wt_ref, users_out, items_out,
+                  xbuf, xsem, land_sel, iterm, land_terms, upart, land_up, ipart, land_ip,
+                  sel_s, sel_r, trm_s, trm_r, up_s, up_r, ip_s, ip_r):
     slots, weeks, users, items = xbuf.shape
     n_x = send_sel.shape[0]
+    n_y = ipart.shape[0]
     n_z, n_c = lax.axis_size("iz"), lax.axis_size("ic")
     n_v = n_z * n_c
-    per_owner = parts_out.shape[2] // users
+    per_owner = upart.shape[2] // users
+    item_own = ipart.shape[2] // items
     me_x = lax.axis_index("ux")
+    me_y = lax.axis_index("uy")
     me_v = lax.axis_index("iz") * n_c + lax.axis_index("ic")
+    item_hot_at = slots * n_v * per_owner
 
     def xpeer(d):
         return {"ux": d}
+
+    def ypeer(d):
+        return {"uy": d}
 
     def vpeer(d):
         return {"iz": d // n_c, "ic": d % n_c}
@@ -131,9 +138,11 @@
     barrier = pltpu.get_barrier_semaphore()
     for k in range(1, n_x):
         pl.semaphore_signal(barrier, inc=1, device_id=xpeer(lax.rem(me_x + k, n_x)), device_id_type=MESH_IDS)
+    for k in range(1, n_y):
+        pl.semaphore_signal(barrier, inc=1, device_id=ypeer(lax.rem(me_y + k, n_y)), device_id_type=MESH_IDS)
     for k in range(1, n_v):
         pl.semaphore_signal(barrier, inc=1, device_id=vpeer(lax.rem(me_v + k, n_v)), device_id_type=MESH_IDS)
-    pl.semaphore_wait(barrier, n_x - 1 + n_v - 1)
+    pl.semaphore_wait(barrier, n_x - 1 + n_y - 1 + n_v - 1)
 
     loads = []
     for s in range(slots):
@@ -141,14 +150,26 @@
         cp.start()
         loads.append(cp)
 
-    sel_copies = []
-    for k in range(1, n_x):
-        d = lax.rem(me_x + k, n_x)
-        cp = pltpu.make_async_remote_copy(
-            src_ref=send_sel.at[d], dst_ref=land_sel.at[me_x], send_sem=sel_s.at[k], recv_sem=sel_r.at[k],
-            device_id=xpeer(d), device_id_type=MESH_IDS)
-        cp.start()
-        sel_copies.append((k, cp))
+    def send_rows(buf, land, ssem, rsem, n, me, peer, whole):
+        started = []
+        for k in range(1, n):
+            d = lax.rem(me + k, n)
+            cp = pltpu.make_async_remote_copy(
+                src_ref=buf if whole else buf.at[d], dst_ref=land.at[me], send_sem=ssem.at[k], recv_sem=rsem.at[k],
+                device_id=peer(d), device_id_type=MESH_IDS)
+            cp.start()
+            started.append((k, cp))
+        return started
+
+    def finish(started, land, ssem, rsem, n, me, peer):
+        for k, cp in started:
+            cp.wait_send()
+            src = lax.rem(me + n - k, n)
+            pltpu.make_async_remote_copy(
+                src_ref=land.at[src], dst_ref=land.at[src], send_sem=ssem.at[k], recv_sem=rsem.at[k],
+                device_id=peer(src), device_id_type=MESH_IDS).wait_recv()
+
+    sel_copies = send_rows(send_sel, land_sel, sel_s, sel_r, n_x, me_x, xpeer, False)
 
     wt = wt_ref[...]
     for s in range(slots):
@@ -157,22 +178,10 @@
         usel = usel_ref[s]
         stacked = jnp.concatenate([usel * wt[:, k:k + 1] for k in range(weeks)], axis=1)
         iterm[s] = jnp.dot(stacked, flat, precision=HIGHEST, preferred_element_type=jnp.float32)
-
-    trm_copies = []
-    for k in range(1, n_x):
-        d = lax.rem(me_x + k, n_x)
-        cp = pltpu.make_async_remote_copy(
-            src_ref=iterm, dst_ref=land_terms.at[me_x], send_sem=trm_s.at[k], recv_sem=trm_r.at[k],
-            device_id=xpeer(d), device_id_type=MESH_IDS)
-        cp.start()
-        trm_copies.append((k, cp))
-
-    for k, cp in sel_copies:
-        cp.wait_send()
-        src = lax.rem(me_x + n_x - k, n_x)
-        pltpu.make_async_remote_copy(
-            src_ref=land_sel.at[src], dst_ref=land_sel.at[src], send_sem=sel_s.at[k], recv_sem=sel_r.at[k],
-            device_id=xpeer(src), device_id_type=MESH_IDS).wait_recv()
+    land_terms[me_x] = iterm[...]
+
+    trm_copies = send_rows(iterm, land_terms, trm_s, trm_r, n_x, me_x, xpeer, True)
+    finish(sel_copies, land_sel, sel_s, sel_r, n_x, me_x, xpeer)
 
     w = w_ref[...]
     uterms = []
@@ -193,50 +202,47 @@
             for s in range(1, slots):
                 acc = acc + uterms[s] * hot_ref[s * n_v * per_owner + col]
             upart[v, :, t * users:(t + 1) * users] = acc
-
-    up_copies = []
+    up_copies = send_rows(upart, land_up, up_s, up_r, n_v, me_v, vpeer, False)
+
+    finish(trm_copies, land_terms, trm_s, trm_r, n_x, me_x, xpeer)
+    sources = []
+    for x in range(n_x):
+        for s in range(slots):
+            sources.append((x, s))
+    for y in range(n_y):
+        for l in range(item_own):
+            acc = None
+            for x, s in sources:
+                at = item_hot_at + ((x * slots + s) * n_y + y) * item_own + l
+                term = land_terms[x, s] * hot_ref[at]
+                acc = term if acc is None else acc + term
+            ipart[y, :, l * items:(l + 1) * items] = acc
+    ip_copies = send_rows(ipart, land_ip, ip_s, ip_r, n_y, me_y, ypeer, False)
+
+    finish(up_copies, land_up, up_s, up_r, n_v, me_v, vpeer)
+    total_u = upart[me_v]
     for k in range(1, n_v):
-        d = lax.rem(me_v + k, n_v)
-        cp = pltpu.make_async_remote_copy(
-            src_ref=upart.at[d], dst_ref=land_up.at[me_v], send_sem=up_s.at[k], recv_sem=up_r.at[k],
-            device_id=vpeer(d), device_id_type=MESH_IDS)
-        cp.start()
-        up_copies.append((k, cp))
-
-    for k, cp in trm_copies:
-        cp.wait_send()
-        src = lax.rem(me_x + n_x - k, n_x)
-        pltpu.make_async_remote_copy(
-            src_ref=land_terms.at[src], dst_ref=land_terms.at[src], send_sem=trm_s.at[k], recv_sem=trm_r.at[k],
-            device_id=xpeer(src), device_id_type=MESH_IDS).wait_recv()
-    for k, cp in up_copies:
-        cp.wait_send()
-        src = lax.rem(me_v + n_v - k, n_v)
-        pltpu.make_async_remote_copy(
-            src_ref=land_up.at[src], dst_ref=land_up.at[src], send_sem=up_s.at[k], recv_sem=up_r.at[k],
-            device_id=vpeer(src), device_id_type=MESH_IDS).wait_recv()
-
-    for k in range(1, n_x):
-        src = lax.rem(me_x + k, n_x)
-        terms_out[src] = land_terms[src]
-    terms_out[me_x] = iterm[...]
-    for k in range(1, n_v):
-        src = lax.rem(me_v + k, n_v)
-        parts_out[src] = land_up[src]
-    parts_out[me_v] = upart[me_v]
-
-
-def fused_middle(hot, data, send_sel, user_sel, week_factor, n_v, collective_id):
+        total_u = total_u + land_up[lax.rem(me_v + k, n_v)]
+    users_out[...] = total_u
+    finish(ip_copies, land_ip, ip_s, ip_r, n_y, me_y, ypeer)
+    total_i = ipart[me_y]
+    for k in range(1, n_y):
+        total_i = total_i + land_ip[lax.rem(me_y + k, n_y)]
+    items_out[...] = total_i
+
+
+def fused_middle(hot, data, send_sel, user_sel, week_factor, n_v, n_y, per_owner, item_own, collective_id):
     slots, weeks, users, items = data.shape
     n_x = send_sel.shape[0]
     rank = week_factor.shape[1]
-    per_owner = hot.shape[0] // (slots * n_v)
     vmem = pl.BlockSpec(memory_space=pltpu.VMEM)
+    up_shape = (n_v, rank, per_owner * users)
+    ip_shape = (n_y, rank, item_own * items)
     return pl.pallas_call(
         _fused_kernel,
         out_shape=(
-            jax.ShapeDtypeStruct((n_x, slots, rank, items), jnp.float32),
-            jax.ShapeDtypeStruct((n_v, rank, per_owner * users), jnp.float32),
+            jax.ShapeDtypeStruct(up_shape[1:], jnp.float32),
+            jax.ShapeDtypeStruct(ip_shape[1:], jnp.float32),
         ),
         in_specs=[pl.BlockSpec(memory_space=pltpu.SMEM), pl.BlockSpec(memory_space=pl.ANY), vmem, vmem, vmem, vmem],
         out_specs=(vmem, vmem),
@@ -246,14 +252,18 @@
             pltpu.VMEM((n_x, slots, rank, items), jnp.float32),
             pltpu.VMEM((slots, rank, items), jnp.float32),
             pltpu.VMEM((n_x, slots, rank, items), jnp.float32),
-            pltpu.VMEM((n_v, rank, per_owner * users), jnp.float32),
-            pltpu.VMEM((n_v, rank, per_owner * users), jnp.float32),
+            pltpu.VMEM(up_shape, jnp.float32),
+            pltpu.VMEM(up_shape, jnp.float32),
+            pltpu.VMEM(ip_shape, jnp.float32),
+            pltpu.VMEM(ip_shape, jnp.float32),
             pltpu.SemaphoreType.DMA((n_x,)),
             pltpu.SemaphoreType.DMA((n_x,)),
             pltpu.SemaphoreType.DMA((n_x,)),
             pltpu.SemaphoreType.DMA((n_x,)),
             pltpu.SemaphoreType.DMA((n_v,)),
             pltpu.SemaphoreType.DMA((n_v,)),
+            pltpu.SemaphoreType.DMA((n_y,)),
+            pltpu.SemaphoreType.DMA((n_y,)),
         ],
         compiler_params=pltpu.CompilerParams(
             collective_id=collective_id, has_side_effects=True, vmem_limit_bytes=48 * 1024 * 1024),
@@ -332,14 +342,9 @@
     ).reshape(x_size, slot_total, y_size, item_own)
     send = jnp.einsum(
         "xsyl,yrlb->xsrb", hot, group_rows.reshape(y_size, rank_size, item_own, item_width), precision=HIGHEST)
-    all_terms, user_parts = fused_middle(
-        user_hot.reshape(-1), tiles[0, 0], send, user_sel, week_factor, n_v, 1)
-    m_users = jnp.sum(user_parts, axis=0)
-
-    part_items = jnp.einsum("xsyl,xsrb->yrlb", hot, all_terms, precision=HIGHEST).reshape(
-        y_size, rank_size, item_own * item_width)
-    (item_parts,) = exchange([(("uy",), (y_size,), "a2a")], [part_items], 2)
-    m_items = jnp.sum(item_parts, axis=0)
+    hot_all = jnp.concatenate([user_hot.reshape(-1), hot.reshape(-1)])
+    m_users, m_items = fused_middle(
+        hot_all, tiles[0, 0], send, user_sel, week_factor, n_v, y_size, user_own, item_own, 1)
     return (m_users, m_items)
 
 

time: 87.6 us -> 70.3 us (0.80)
  Pallas kernels: 68.2 us -> 55 us
  other arithmetic: 3.58 us -> 1.06 us
  matrix products: 4.41 us -> 2.99 us
    pallas_call x2 -> x1, Pallas kernels: 40.1 us -> 22.7 us  [exchange(): pl.pallas_call(functools.partial(_exchange_kernel, plan), out_shape=tuple...]
    pallas_call x1, Pallas kernels: 28.1 us -> 32.3 us  [fused_middle(): pl.pallas_call(_fused_kernel, out_shape=(jax.ShapeDtypeStruct(up_shape[1:...]
    reduce_sum x2 -> x0, other arithmetic: 2.67 us -> none  [the longest x1 2.01 us: on_device(): m_items = jnp.sum(item_parts, axis=0)]
    reshape x2 -> x0, local copies, waits for them, and re-layouts: 1.96 us -> none  [on_device(): jnp.einsum('xsyl,xsrb->yrlb', hot, all_terms, precision=HIGHEST)]
    dot_general x1 -> x0, matrix products: 1.42 us -> none  [on_device(): jnp.einsum('xsyl,xsrb->yrlb', hot, all_terms, precision=HIGHEST)]
    unnamed x6 -> x8, local copies, waits for them, and re-layouts: 3.53 us -> 4.86 us
where the time goes in v5:
time: 70.3 us; the launch traced here: 69.1 us
  Pallas kernels  55 us (78%)
  local copies, waits for them, and re-layouts  8.68 us (12%)
  matrix products  2.99 us (4%)
  between operations  1.38 us (2%)
  other arithmetic  1.06 us (2%)
    pallas_call x1, Pallas kernels, fused_middle(): pl.pallas_call(_fused_kernel, out_shape=(jax.ShapeDtypeStruct(up_shape[1:...  32.3 us
    pallas_call x1, Pallas kernels, exchange(): pl.pallas_call(functools.partial(_exchange_kernel, plan), out_shape=tuple...  22.7 us
    unnamed x8, local copies, waits for them, and re-layouts  4.86 us
    dot_general x1, matrix products, on_device(): jnp.einsum('xsyl,yrlb->xsrb', hot, group_rows.reshape(y_size, rank_size,...  1.68 us

profile of v5, /device:TPU:1, one launch (start us, length us, event | category | flops | bytes accessed | tf_op | source)
XLA Modules:
  0.0 69.1 jit_solution(17442886770801201261)
XLA Ops:
  1.3 0.7 scatter.6
  2.0 0.0 copy-start.1
  2.0 0.6 copy-done.1
  2.6 22.7 %shard_map.86 = (f32[4,64,1024]{2,1,0:T(8,128)}, s32[4,8,128]{2,1,0:T(8,128)}, f32[8,64,256]{2,1,0:T(8,128)}) custom-call(f32[64,1024]{1,0:T(8,128)} %refs_0_.1, s32[8,128]{1,0:T(8,128)} %copy-done.1, f32[64,256]{1,0:T(8,128)} %refs_2_.1), custom_call_target="tpu_custom_call" | custom-call | tf_op jit(solution)/shard_map/pallas_call | solution.py:87
  25.2 0.7 %slice.41 = s32[4,1,4]{2,1,0:T(1,128)S(1)} slice(s32[4,8,128]{2,1,0:T(8,128)} %get-tuple-element.29), slice={[0:4], [0:1], [0:4]} | slice | bytes 128 | tf_op jit(solution)/shard_map/slice | solution.py:334
  26.0 0.9 %slice_reduce_fusion = s32[4]{0:T(128)S(1)} fusion(s32[4,8,128]{2,1,0:T(8,128)} %get-tuple-element.29), kind=kLoop, calls=%fused_computation.27 | loop fusion | bytes 32 | tf_op jit(solution)/shard_map/slice | solution.py:335
  26.8 0.1 fusion.17
  26.9 1.4 %copy.22 = f32[32,8,8,128]{3,2,1,0:T(8,128)S(1)} copy(f32[32,8,8,128]{3,1,2,0:T(8,128)} %bitcast.37) | data formatting | bytes 2097152
  28.4 1.7 %convolution_bitcast_fusion = f32[4,4,64,128]{3,1,2,0:T(4,128)S(1)} fusion(s32[4,8]{1,0:T(4,128)S(1)} %multiply_add_fusion, s32[4,4]{1,0:T(4,128)S(1)} %add_select_fusion, pred[4,4]{1,0:T(4,128)(4,1)S(1)} %fusion.17, f32[4,64,8,128]{3,2,1,0:T(8,128)S(1)} %bitcast.36), kind=kOutput, calls=%fused_computation | convolution fusion | flops 50333184 | bytes 1573072 | tf_op jit(solution)/shard_map/xsyl,yrlb->xsrb/dot_general | solution.py:343
  30.1 0.1 copy.18.send_sel
  30.1 0.1 convert_select_fusion
  30.2 0.1 select_n.34
  30.3 0.7 %fusion.15 = f32[4,16]{1,0:T(4,128)S(1)} fusion(s32[4]{0:T(128)} %bitcast.40), kind=kLoop, calls=%fused_computation.31 | loop fusion | flops 128 | bytes 272 | tf_op jit(solution)/shard_map/convert_element_type | solution.py:328
  31.0 0.1 reshape.184
  31.1 0.1 pad_maximum_fusion.hot_ref
  31.2 1.3 %reshape.183 = f32[8,64,2,128]{3,2,1,0:T(2,128)S(1)} reshape(f32[8,64,256]{2,1,0:T(8,128)} %get-tuple-element.31) | data formatting | bytes 1048576 | tf_op jit(solution)/shard_map/reshape | solution.py:331
  32.5 1.3 %convolution_bitcast_fusion.1 = f32[4,64,128]{2,0,1:T(4,128)S(1)} fusion(f32[8,64,2,128]{3,2,1,0:T(2,128)S(1)} %reshape.183, s32[8,2]{0,1:T(2,128)S(1)} %multiply_add_fusion.1, s32[4]{0:T(128)} %bitcast.41), kind=kOutput, calls=%fused_computation.1 | convolution fusion | flops 6291520 | bytes 655440 | tf_op jit(solution)/shard_map/svt,vrta->sra/dot_general | solution.py:330
  33.8 0.1 copy_multiply_fusion.usel_ref
  33.9 0.8 %copy.17 = f32[32,64]{0,1:T(8,128)S(1)} copy(f32[32,64]{1,0:T(8,128)} %w_ref.1) | data formatting | bytes 16384 | tf_op args[6]
  34.7 0.0 copy-start
  34.7 0.7 %copy-done = f32[32,64]{1,0:T(8,128)S(1)} copy-done((f32[32,64]{1,0:T(8,128)S(1)}, f32[32,64]{1,0:T(8,128)}, u32[]{:S(2)}) %copy-start) | copy-done | bytes 8216
  35.4 32.3 %shard_map.87 = (f32[64,256]{1,0:T(8,128)S(1)}, f32[64,1024]{1,0:T(8,128)S(1)}) custom-call(f32[576]{0:T(1024)S(1)} %pad_maximum_fusion.hot_ref, f32[4,32,128,128]{3,2,1,0:T(8,128)} %bitcast.35, f32[4,4,64,128]{3,2,1,0:T(8,128)S(1)} %copy.18.send_sel, f32[4,64,128]{2,1,0:T(8,128)S(1)} %copy_multiply_fusion.usel_ref, f32[32,64]{1,0:T(8,128)S(1)} %copy-done, ...), custom_call_target="tpu_custom_call" | custom-call | flops 536870912 | bytes 8388608 | tf_op jit(solution)/shard_map/pallas_call | solution.py:241
  67.7 0.6 copy.34
  68.4 0.7 %copy.35 = f32[64,1024]{1,0:T(8,128)} copy(f32[64,1024]{1,0:T(8,128)S(1)} %get-tuple-element.35) | data formatting | bytes 524288
  (5 shorter events, 0.1 us)
Async XLA Ops:
  2.0 0.6 copy-start.1
  34.7 0.7 %copy-start = (f32[32,64]{1,0:T(8,128)S(1)}, f32[32,64]{1,0:T(8,128)}, u32[]{:S(2)}) copy-start(f32[32,64]{1,0:T(8,128)} %w_ref.1) | copy-start | bytes 24580

commit v6 on v5

--- a/solution.py
+++ b/solution.py
@@ -111,8 +111,8 @@
     iterm_ref[0] = jnp.dot(stacked, flat, precision=HIGHEST, preferred_element_type=jnp.float32)
 
 
-def _fused_kernel(hot_ref, tiles_hbm, send_sel, usel_ref, w_ref, wt_ref, users_out, items_out,
-                  xbuf, xsem, land_sel, iterm, land_terms, upart, land_up, ipart, land_ip,
+def _fused_kernel(hot_ref, idx_ref, tiles_hbm, group_ref, urows_ref, w_ref, wt_ref, users_out, items_out,
+                  send_sel, usel_ref, xbuf, xsem, land_sel, iterm, land_terms, upart, land_up, ipart, land_ip,
                   sel_s, sel_r, trm_s, trm_r, up_s, up_r, ip_s, ip_r):
     slots, weeks, users, items = xbuf.shape
     n_x = send_sel.shape[0]
@@ -169,7 +169,15 @@
                 src_ref=land.at[src], dst_ref=land.at[src], send_sem=ssem.at[k], recv_sem=rsem.at[k],
                 device_id=peer(src), device_id_type=MESH_IDS).wait_recv()
 
+    n_sel = n_x * slots
+    mask_at = item_hot_at + n_sel * n_y * item_own
+    for x in range(n_x):
+        for s in range(slots):
+            q = x * slots + s
+            send_sel[x, s] = group_ref[idx_ref[q]] * hot_ref[mask_at + q]
     sel_copies = send_rows(send_sel, land_sel, sel_s, sel_r, n_x, me_x, xpeer, False)
+    for s in range(slots):
+        usel_ref[s] = urows_ref[idx_ref[n_sel + s]] * hot_ref[mask_at + n_sel + s]
 
     wt = wt_ref[...]
     for s in range(slots):
@@ -231,11 +239,12 @@
     items_out[...] = total_i
 
 
-def fused_middle(hot, data, send_sel, user_sel, week_factor, n_v, n_y, per_owner, item_own, collective_id):
+def fused_middle(hot, idx, data, group_rows, user_rows, week_factor, n_x, n_v, n_y, per_owner, item_own,
+                 collective_id):
     slots, weeks, users, items = data.shape
-    n_x = send_sel.shape[0]
     rank = week_factor.shape[1]
     vmem = pl.BlockSpec(memory_space=pltpu.VMEM)
+    smem = pl.BlockSpec(memory_space=pltpu.SMEM)
     up_shape = (n_v, rank, per_owner * users)
     ip_shape = (n_y, rank, item_own * items)
     return pl.pallas_call(
@@ -244,9 +253,11 @@
             jax.ShapeDtypeStruct(up_shape[1:], jnp.float32),
             jax.ShapeDtypeStruct(ip_shape[1:], jnp.float32),
         ),
-        in_specs=[pl.BlockSpec(memory_space=pltpu.SMEM), pl.BlockSpec(memory_space=pl.ANY), vmem, vmem, vmem, vmem],
+        in_specs=[smem, smem, pl.BlockSpec(memory_space=pl.ANY), vmem, vmem, vmem, vmem],
         out_specs=(vmem, vmem),
         scratch_shapes=[
+            pltpu.VMEM((n_x, slots, rank, items), jnp.float32),
+            pltpu.VMEM((slots, rank, users), jnp.float32),
             pltpu.VMEM((slots, weeks, users, items), jnp.float32),
             pltpu.SemaphoreType.DMA((slots,)),
             pltpu.VMEM((n_x, slots, rank, items), jnp.float32),
@@ -270,7 +281,7 @@
         cost_estimate=pl.CostEstimate(
             flops=4 * slots * weeks * users * items * rank, transcendentals=0,
             bytes_accessed=4 * slots * weeks * users * items),
-    )(hot, data, send_sel, user_sel, week_factor, week_factor.T)
+    )(hot, idx, data, group_rows, user_rows, week_factor, week_factor.T)
 
 
 def slot_terms(data, item_sel, user_sel, week_factor):
@@ -320,31 +331,32 @@
 
     group_rows, id_rows, user_rows = exchange(
         [(("uy",), (y_size,), "bcast"), (("ux",), (x_size,), "bcast"), (("iz", "ic"), (z_size, c_size), "bcast")],
-        [item_factor, id_piece, user_factor],
+        [item_factor.reshape(rank_size, item_own, item_width).transpose(1, 0, 2), id_piece,
+         user_factor.reshape(rank_size, user_own, user_width).transpose(1, 0, 2)],
         0,
     )
+    group_rows = group_rows.reshape(-1, rank_size, item_width)
+    user_rows = user_rows.reshape(-1, rank_size, user_width)
     n_v = z_size * c_size
     user_block_total = n_v * user_own
     user_hot = (user_ids[:, None] == jnp.arange(user_block_total, dtype=jnp.int32)[None, :]).astype(jnp.float32)
-    user_hot = user_hot.reshape(slot_total, n_v, user_own)
-    user_sel = jnp.einsum(
-        "svt,vrta->sra", user_hot, user_rows.reshape(n_v, rank_size, user_own, user_width),
-        precision=HIGHEST) * live[:, None, None]
+    user_hot = user_hot * live[:, None]
 
     wanted = id_rows[:, 0, :slot_total]
     wanted_live = slot_order[None, :] < id_rows[:, 1, 0:1]
     owner_group = wanted // group_blocks
     local_block = wanted % group_blocks
+    take = (owner_group == me_x) & wanted_live
     hot = jnp.where(
-        ((owner_group == me_x) & wanted_live)[:, :, None],
+        take[:, :, None],
         (local_block[:, :, None] == jnp.arange(group_blocks, dtype=jnp.int32)[None, None, :]).astype(jnp.float32),
         0.0,
-    ).reshape(x_size, slot_total, y_size, item_own)
-    send = jnp.einsum(
-        "xsyl,yrlb->xsrb", hot, group_rows.reshape(y_size, rank_size, item_own, item_width), precision=HIGHEST)
-    hot_all = jnp.concatenate([user_hot.reshape(-1), hot.reshape(-1)])
+    )
+    hot_all = jnp.concatenate([user_hot.reshape(-1), hot.reshape(-1), take.astype(jnp.float32).reshape(-1), live])
+    idx_all = jnp.concatenate([local_block.reshape(-1), user_ids]).astype(jnp.int32)
     m_users, m_items = fused_middle(
-        hot_all, tiles[0, 0], send, user_sel, week_factor, n_v, y_size, user_own, item_own, 1)
+        hot_all, idx_all, tiles[0, 0], group_rows, user_rows, week_factor, x_size, n_v, y_size, user_own,
+        item_own, 1)
     return (m_users, m_items)
 
 

time: 70.3 us -> 69.3 us (0.986)
  matrix products: 2.99 us -> 0 us
  local copies, waits for them, and re-layouts: 8.68 us -> 9.97 us
    dot_general x2 -> x0, matrix products: 2.99 us -> none  [the longest x1 1.68 us: on_device(): jnp.einsum('xsyl,yrlb->xsrb', hot, group_rows.reshape(y_size, rank_size,...]
    transpose x0 -> x2, local copies, waits for them, and re-layouts: none -> 2.19 us  [the longest x1 1.47 us: on_device(): user_factor.reshape(rank_size, user_own, user_width).transpose(1, 0, 2)]
    reshape x1 -> x0, local copies, waits for them, and re-layouts: 1.3 us -> none  [on_device(): user_rows.reshape(n_v, rank_size, user_own, user_width)]
    concatenate x1 -> x2, other arithmetic: 0.08 us -> 0.81 us  [the longest x1 0.73 us: on_device(): jnp.concatenate([local_block.reshape(-1), user_ids]).astype(jnp.int32)]
    convert_element_type x1, other arithmetic: 0.73 us -> 0.02 us  [on_device(): take.astype(jnp.float32).reshape(-1)]
    unnamed x8 -> x13, local copies, waits for them, and re-layouts: 4.86 us -> 5.13 us
where the time goes in v6:
time: 69.3 us; the launch traced here: 68.1 us
  Pallas kernels  55 us (79%)
  local copies, waits for them, and re-layouts  9.97 us (14%)
  other arithmetic  1.73 us (2%)
  between operations  1.4 us (2%)
    pallas_call x1, Pallas kernels, fused_middle(): pl.pallas_call(_fused_kernel, out_shape=(jax.ShapeDtypeStruct(up_shape[1:...  32.3 us
    pallas_call x1, Pallas kernels, exchange(): pl.pallas_call(functools.partial(_exchange_kernel, plan), out_shape=tuple...  22.7 us
    unnamed x13, local copies, waits for them, and re-layouts  5.13 us
    transpose x1, local copies, waits for them, and re-layouts, on_device(): user_factor.reshape(rank_size, user_own, user_width).transpose(1, 0, 2)  1.47 us

profile of v6, /device:TPU:1, one launch (start us, length us, event | category | flops | bytes accessed | tf_op | source)
XLA Modules:
  0.0 68.1 jit_solution(7341960444696595807)
XLA Ops:
  0.6 0.0 copy-start
  1.3 0.7 scatter.6
  2.0 0.0 copy-done
  2.1 0.7 %bitcast_bitcast_fusion.refs_0_ = f32[8,64,128]{2,1,0:T(8,128)} fusion(f32[64,1024]{1,0:T(8,128)S(1)} %copy-done), kind=kLoop, calls=%fused_computation | loop fusion | bytes 524288 | tf_op jit(solution)/shard_map/transpose | solution.py:334
  2.8 1.5 %bitcast_bitcast_fusion.1.refs_2_ = f32[2,64,128]{2,1,0:T(8,128)} fusion(f32[64,256]{1,0:T(8,128)} %param.15), kind=kLoop, calls=%fused_computation.1 | loop fusion | bytes 131072 | tf_op jit(solution)/shard_map/transpose | solution.py:335
  4.3 22.7 %shard_map.86 = (f32[4,8,64,128]{3,2,1,0:T(8,128)}, s32[4,8,128]{2,1,0:T(8,128)}, f32[8,2,64,128]{3,2,1,0:T(8,128)}) custom-call(f32[8,64,128]{2,1,0:T(8,128)} %bitcast_bitcast_fusion.refs_0_, s32[8,128]{1,0:T(8,128)} %copy-done.4, f32[2,64,128]{2,1,0:T(8,128)} %bitcast_bitcast_fusion.1.refs_2_), custom_call_target="tpu_custom_call" | custom-call | tf_op jit(solution)/shard_map/pallas_call | solution.py:87
  26.9 0.7 %fusion.4 = (s32[4,1,4]{2,1,0:T(1,128)S(1)}, s32[4,4]{1,0:T(4,128)S(1)}) fusion(s32[4,8,128]{2,1,0:T(8,128)} %get-tuple-element.29), kind=kLoop, calls=%fused_computation.28 | loop fusion | bytes 192 | tf_op jit(solution)/shard_map/slice | solution.py:345
  27.7 0.9 %slice_reduce_fusion = s32[4]{0:T(128)S(1)} fusion(s32[4,8,128]{2,1,0:T(8,128)} %get-tuple-element.29), kind=kLoop, calls=%fused_computation.11 | loop fusion | bytes 32 | tf_op jit(solution)/shard_map/slice | solution.py:346
  28.5 0.1 fusion.3
  28.6 0.1 lt.48
  28.7 0.1 squeeze.17
  28.8 0.1 convert_select_fusion
  28.9 0.1 select_n.37
  29.0 0.7 %fusion.1 = f32[4,16]{1,0:T(4,128)S(1)} fusion(f32[4]{0:T(128)S(1)} %compare_convert_fusion, s32[4]{0:T(128)} %bitcast.30), kind=kLoop, calls=%fused_computation.15 | loop fusion | flops 128 | bytes 288 | tf_op jit(solution)/shard_map/mul | solution.py:343
  29.7 0.1 mul.12
  29.8 0.1 pad_maximum_fusion.hot_ref
  29.9 0.7 %pad_add_fusion.idx_ref = s32[20]{0:T(128)S(1)} fusion(s32[4]{0:T(128)} %bitcast.31, s32[16]{0:T(128)S(1)} %and_select_fusion), kind=kLoop, calls=%fused_computation.26 | loop fusion | flops 20 | bytes 160 | tf_op jit(solution)/shard_map/concatenate | solution.py:356
  30.6 0.8 %copy.12 = f32[32,64]{0,1:T(8,128)S(1)} copy(f32[32,64]{1,0:T(8,128)} %w_ref.1) | data formatting | bytes 16384 | tf_op args[6]
  31.4 1.2 %copy-done.1 = f32[4,8,64,128]{3,2,1,0:T(8,128)S(1)} copy-done((f32[4,8,64,128]{3,2,1,0:T(8,128)S(1)}, f32[4,8,64,128]{3,2,1,0:T(8,128)}, u32[]{:S(2)}) %copy-start.1) | copy-done | bytes 1048600
  32.7 1.0 %copy-done.2 = f32[8,2,64,128]{3,2,1,0:T(8,128)S(1)} copy-done((f32[8,2,64,128]{3,2,1,0:T(8,128)S(1)}, f32[8,2,64,128]{3,2,1,0:T(8,128)}, u32[]{:S(2)}) %copy-start.2) | copy-done | bytes 524312
  33.7 0.7 %copy-done.3 = f32[32,64]{1,0:T(8,128)S(1)} copy-done((f32[32,64]{1,0:T(8,128)S(1)}, f32[32,64]{1,0:T(8,128)}, u32[]{:S(2)}) %copy-start.3) | copy-done | bytes 8216
  34.4 32.3 %shard_map.87 = (f32[64,256]{1,0:T(8,128)S(1)}, f32[64,1024]{1,0:T(8,128)S(1)}) custom-call(f32[596]{0:T(1024)S(1)} %pad_maximum_fusion.hot_ref, s32[20]{0:T(128)S(1)} %pad_add_fusion.idx_ref, f32[4,32,128,128]{3,2,1,0:T(8,128)} %bitcast.26, f32[32,64,128]{2,1,0:T(8,128)S(1)} %bitcast.23, f32[16,64,128]{2,1,0:T(8,128)S(1)} %bitcast.24, ...), custom_call_target="tpu_custom_call" | custom-call | flops 536870912 | bytes 8388608 | tf_op jit(solution)/shard_map/pallas_call | solution.py:250
  66.8 0.6 copy.21
  67.4 0.7 %copy.22 = f32[64,1024]{1,0:T(8,128)} copy(f32[64,1024]{1,0:T(8,128)S(1)} %get-tuple-element.39) | data formatting | bytes 524288
  (10 shorter events, 0.1 us)
Async XLA Ops:
  0.6 1.4 %copy-start = (f32[64,1024]{1,0:T(8,128)S(1)}, f32[64,1024]{1,0:T(8,128)}, u32[]{:S(2)}) copy-start(f32[64,1024]{1,0:T(8,128)} %param.16) | copy-start | bytes 786436
  2.0 2.2 %copy-start.4 = (s32[8,128]{1,0:T(8,128)}, s32[8,128]{1,0:T(8,128)S(1)}, u32[]{:S(2)}) copy-start(s32[8,128]{1,0:T(8,128)S(1)} %scatter.9.refs_1_) | copy-start | bytes 12292
  31.4 1.2 %copy-start.1 = (f32[4,8,64,128]{3,2,1,0:T(8,128)S(1)}, f32[4,8,64,128]{3,2,1,0:T(8,128)}, u32[]{:S(2)}) copy-start(f32[4,8,64,128]{3,2,1,0:T(8,128)} %get-tuple-element.30) | copy-start | bytes 3145732
  32.6 1.0 %copy-start.2 = (f32[8,2,64,128]{3,2,1,0:T(8,128)S(1)}, f32[8,2,64,128]{3,2,1,0:T(8,128)}, u32[]{:S(2)}) copy-start(f32[8,2,64,128]{3,2,1,0:T(8,128)} %get-tuple-element.31) | copy-start | bytes 1572868
  33.7 0.7 %copy-start.3 = (f32[32,64]{1,0:T(8,128)S(1)}, f32[32,64]{1,0:T(8,128)}, u32[]{:S(2)}) copy-start(f32[32,64]{1,0:T(8,128)} %w_ref.1) | copy-start | bytes 24580

commit v7 on v6

--- a/solution.py
+++ b/solution.py
@@ -96,6 +96,7 @@
 
 HIGHEST = lax.Precision.HIGHEST
 Y_SPLIT = 4
+TERMS = lax.Precision.HIGH
 
 
 def _terms_kernel(x_ref, isel_ref, usel_ref, w_ref, wt_ref, uterm_ref, iterm_ref):
@@ -185,7 +186,7 @@
         flat = xbuf[s].reshape(weeks * users, items)
         usel = usel_ref[s]
         stacked = jnp.concatenate([usel * wt[:, k:k + 1] for k in range(weeks)], axis=1)
-        iterm[s] = jnp.dot(stacked, flat, precision=HIGHEST, preferred_element_type=jnp.float32)
+        iterm[s] = jnp.dot(stacked, flat, precision=TERMS, preferred_element_type=jnp.float32)
     land_terms[me_x] = iterm[...]
 
     trm_copies = send_rows(iterm, land_terms, trm_s, trm_r, n_x, me_x, xpeer, True)
@@ -199,7 +200,7 @@
             isel = isel + land_sel[lax.rem(me_x + k, n_x), s]
         flat = xbuf[s].reshape(weeks * users, items)
         by_items = lax.dot_general(
-            flat, isel, (((1,), (1,)), ((), ())), precision=HIGHEST, preferred_element_type=jnp.float32)
+            flat, isel, (((1,), (1,)), ((), ())), precision=TERMS, preferred_element_type=jnp.float32)
         weighted = by_items.reshape(weeks, users, -1) * w[:, None, :]
         uterms.append(jnp.sum(weighted, axis=0).T)
 

time: 69.3 us -> 67.3 us (0.971)
  Pallas kernels: 55 us -> 53 us
    pallas_call x1, Pallas kernels: 32.3 us -> 30.3 us  [fused_middle(): pl.pallas_call(_fused_kernel, out_shape=(jax.ShapeDtypeStruct(up_shape[1:...]
where the time goes in v7:
time: 67.3 us; the launch traced here: 66.1 us
  Pallas kernels  53 us (79%)
  local copies, waits for them, and re-layouts  9.97 us (15%)
  other arithmetic  1.73 us (3%)
  between operations  1.4 us (2%)
    pallas_call x1, Pallas kernels, fused_middle(): pl.pallas_call(_fused_kernel, out_shape=(jax.ShapeDtypeStruct(up_shape[1:...  30.3 us
    pallas_call x1, Pallas kernels, exchange(): pl.pallas_call(functools.partial(_exchange_kernel, plan), out_shape=tuple...  22.7 us
    unnamed x13, local copies, waits for them, and re-layouts  5.13 us
    transpose x1, local copies, waits for them, and re-layouts, on_device(): user_factor.reshape(rank_size, user_own, user_width).transpose(1, 0, 2)  1.47 us

profile of v7, /device:TPU:1, one launch (start us, length us, event | category | flops | bytes accessed | tf_op | source)
XLA Modules:
  0.0 66.1 jit_solution(3307080459528101107)
XLA Ops:
  0.6 0.0 copy-start
  1.3 0.7 %scatter.6 = s32[8,128]{1,0:T(8,128)S(1)} pad(s32[1,4]{1,0:T(1,128)} %bitcast.29, s32[]{:T(128)} %constant.85.clone.1), padding=0_7x0_124 | pad | bytes 4116 | tf_op jit(solution)/shard_map/scatter | solution.py:331
  2.0 0.0 copy-done
  2.1 0.7 %bitcast_bitcast_fusion.refs_0_ = f32[8,64,128]{2,1,0:T(8,128)} fusion(f32[64,1024]{1,0:T(8,128)S(1)} %copy-done), kind=kLoop, calls=%fused_computation | loop fusion | bytes 524288 | tf_op jit(solution)/shard_map/transpose | solution.py:335
  2.8 1.5 %bitcast_bitcast_fusion.1.refs_2_ = f32[2,64,128]{2,1,0:T(8,128)} fusion(f32[64,256]{1,0:T(8,128)} %param.15), kind=kLoop, calls=%fused_computation.1 | loop fusion | bytes 131072 | tf_op jit(solution)/shard_map/transpose | solution.py:336
  4.3 22.7 %shard_map.86 = (f32[4,8,64,128]{3,2,1,0:T(8,128)}, s32[4,8,128]{2,1,0:T(8,128)}, f32[8,2,64,128]{3,2,1,0:T(8,128)}) custom-call(f32[8,64,128]{2,1,0:T(8,128)} %bitcast_bitcast_fusion.refs_0_, s32[8,128]{1,0:T(8,128)} %copy-done.4, f32[2,64,128]{2,1,0:T(8,128)} %bitcast_bitcast_fusion.1.refs_2_), custom_call_target="tpu_custom_call" | custom-call | tf_op jit(solution)/shard_map/pallas_call | solution.py:87
  26.9 0.7 %fusion.4 = (s32[4,1,4]{2,1,0:T(1,128)S(1)}, s32[4,4]{1,0:T(4,128)S(1)}) fusion(s32[4,8,128]{2,1,0:T(8,128)} %get-tuple-element.29), kind=kLoop, calls=%fused_computation.28 | loop fusion | bytes 192 | tf_op jit(solution)/shard_map/slice | solution.py:346
  27.7 0.9 %slice_reduce_fusion = s32[4]{0:T(128)S(1)} fusion(s32[4,8,128]{2,1,0:T(8,128)} %get-tuple-element.29), kind=kLoop, calls=%fused_computation.11 | loop fusion | bytes 32 | tf_op jit(solution)/shard_map/slice | solution.py:347
  28.5 0.1 fusion.3
  28.6 0.1 lt.48
  28.7 0.1 squeeze.17
  28.8 0.1 convert_select_fusion
  28.9 0.1 select_n.37
  29.0 0.7 %fusion.1 = f32[4,16]{1,0:T(4,128)S(1)} fusion(f32[4]{0:T(128)S(1)} %compare_convert_fusion, s32[4]{0:T(128)} %bitcast.30), kind=kLoop, calls=%fused_computation.15 | loop fusion | flops 128 | bytes 288 | tf_op jit(solution)/shard_map/mul | solution.py:344
  29.7 0.1 mul.12
  29.8 0.1 pad_maximum_fusion.hot_ref
  29.9 0.7 %pad_add_fusion.idx_ref = s32[20]{0:T(128)S(1)} fusion(s32[4]{0:T(128)} %bitcast.31, s32[16]{0:T(128)S(1)} %and_select_fusion), kind=kLoop, calls=%fused_computation.26 | loop fusion | flops 20 | bytes 160 | tf_op jit(solution)/shard_map/concatenate | solution.py:357
  30.6 0.8 %copy.12 = f32[32,64]{0,1:T(8,128)S(1)} copy(f32[32,64]{1,0:T(8,128)} %w_ref.1) | data formatting | bytes 16384 | tf_op args[6]
  31.4 1.2 %copy-done.1 = f32[4,8,64,128]{3,2,1,0:T(8,128)S(1)} copy-done((f32[4,8,64,128]{3,2,1,0:T(8,128)S(1)}, f32[4,8,64,128]{3,2,1,0:T(8,128)}, u32[]{:S(2)}) %copy-start.1) | copy-done | bytes 1048600
  32.7 1.0 %copy-done.2 = f32[8,2,64,128]{3,2,1,0:T(8,128)S(1)} copy-done((f32[8,2,64,128]{3,2,1,0:T(8,128)S(1)}, f32[8,2,64,128]{3,2,1,0:T(8,128)}, u32[]{:S(2)}) %copy-start.2) | copy-done | bytes 524312
  33.7 0.7 %copy-done.3 = f32[32,64]{1,0:T(8,128)S(1)} copy-done((f32[32,64]{1,0:T(8,128)S(1)}, f32[32,64]{1,0:T(8,128)}, u32[]{:S(2)}) %copy-start.3) | copy-done | bytes 8216
  34.4 30.3 %shard_map.87 = (f32[64,256]{1,0:T(8,128)S(1)}, f32[64,1024]{1,0:T(8,128)S(1)}) custom-call(f32[596]{0:T(1024)S(1)} %pad_maximum_fusion.hot_ref, s32[20]{0:T(128)S(1)} %pad_add_fusion.idx_ref, f32[4,32,128,128]{3,2,1,0:T(8,128)} %bitcast.26, f32[32,64,128]{2,1,0:T(8,128)S(1)} %bitcast.23, f32[16,64,128]{2,1,0:T(8,128)S(1)} %bitcast.24, ...), custom_call_target="tpu_custom_call" | custom-call | flops 536870912 | bytes 8388608 | tf_op jit(solution)/shard_map/pallas_call | solution.py:251
  64.7 0.6 copy.21
  65.4 0.7 %copy.22 = f32[64,1024]{1,0:T(8,128)} copy(f32[64,1024]{1,0:T(8,128)S(1)} %get-tuple-element.39) | data formatting | bytes 524288
  (10 shorter events, 0.1 us)
Async XLA Ops:
  0.6 1.4 %copy-start = (f32[64,1024]{1,0:T(8,128)S(1)}, f32[64,1024]{1,0:T(8,128)}, u32[]{:S(2)}) copy-start(f32[64,1024]{1,0:T(8,128)} %param.16) | copy-start | bytes 786436
  2.0 2.2 %copy-start.4 = (s32[8,128]{1,0:T(8,128)}, s32[8,128]{1,0:T(8,128)S(1)}, u32[]{:S(2)}) copy-start(s32[8,128]{1,0:T(8,128)S(1)} %scatter.9.refs_1_) | copy-start | bytes 12292
  31.4 1.2 %copy-start.1 = (f32[4,8,64,128]{3,2,1,0:T(8,128)S(1)}, f32[4,8,64,128]{3,2,1,0:T(8,128)}, u32[]{:S(2)}) copy-start(f32[4,8,64,128]{3,2,1,0:T(8,128)} %get-tuple-element.30) | copy-start | bytes 3145732
  32.6 1.0 %copy-start.2 = (f32[8,2,64,128]{3,2,1,0:T(8,128)S(1)}, f32[8,2,64,128]{3,2,1,0:T(8,128)}, u32[]{:S(2)}) copy-start(f32[8,2,64,128]{3,2,1,0:T(8,128)} %get-tuple-element.31) | copy-start | bytes 1572868
  33.7 0.7 %copy-start.3 = (f32[32,64]{1,0:T(8,128)S(1)}, f32[32,64]{1,0:T(8,128)}, u32[]{:S(2)}) copy-start(f32[32,64]{1,0:T(8,128)} %w_ref.1) | copy-start | bytes 24580

commit v8 on v7

--- a/solution.py
+++ b/solution.py
@@ -96,7 +96,7 @@
 
 HIGHEST = lax.Precision.HIGHEST
 Y_SPLIT = 4
-TERMS = lax.Precision.HIGH
+TERMS = lax.Precision.HIGHEST
 
 
 def _terms_kernel(x_ref, isel_ref, usel_ref, w_ref, wt_ref, uterm_ref, iterm_ref):
@@ -112,20 +112,23 @@
     iterm_ref[0] = jnp.dot(stacked, flat, precision=HIGHEST, preferred_element_type=jnp.float32)
 
 
-def _fused_kernel(hot_ref, idx_ref, tiles_hbm, group_ref, urows_ref, w_ref, wt_ref, users_out, items_out,
-                  send_sel, usel_ref, xbuf, xsem, land_sel, iterm, land_terms, upart, land_up, ipart, land_ip,
-                  sel_s, sel_r, trm_s, trm_r, up_s, up_r, ip_s, ip_r):
+def _fused_kernel(hot_ref, idx_ref, tiles_hbm, ga_ref, gb_ref, urows_ref, w_ref, wt_ref, users_out, items_out,
+                  sel_x, sel_y, usel_ref, xbuf, xsem, land_sx, land_sy, iterm, land_tx, land_ty,
+                  upart, land_up, part_a, land_a, part_b, land_b,
+                  sx_s, sx_r, sy_s, sy_r, tx_s, tx_r, ty_s, ty_r, up_s, up_r, pa_s, pa_r, pb_s, pb_r):
     slots, weeks, users, items = xbuf.shape
-    n_x = send_sel.shape[0]
-    n_y = ipart.shape[0]
+    n_x, n_y = sel_x.shape[0], sel_y.shape[0]
     n_z, n_c = lax.axis_size("iz"), lax.axis_size("ic")
     n_v = n_z * n_c
     per_owner = upart.shape[2] // users
-    item_own = ipart.shape[2] // items
+    half = part_a.shape[2] // items
     me_x = lax.axis_index("ux")
     me_y = lax.axis_index("uy")
     me_v = lax.axis_index("iz") * n_c + lax.axis_index("ic")
-    item_hot_at = slots * n_v * per_owner
+    n_q = n_x * slots
+    hot_a_at = slots * n_v * per_owner
+    hot_b_at = hot_a_at + n_q * n_y * half
+    mask_at = hot_b_at + n_q * n_x * half
 
     def xpeer(d):
         return {"ux": d}
@@ -170,15 +173,13 @@
                 src_ref=land.at[src], dst_ref=land.at[src], send_sem=ssem.at[k], recv_sem=rsem.at[k],
                 device_id=peer(src), device_id_type=MESH_IDS).wait_recv()
 
-    n_sel = n_x * slots
-    mask_at = item_hot_at + n_sel * n_y * item_own
-    for x in range(n_x):
-        for s in range(slots):
-            q = x * slots + s
-            send_sel[x, s] = group_ref[idx_ref[q]] * hot_ref[mask_at + q]
-    sel_copies = send_rows(send_sel, land_sel, sel_s, sel_r, n_x, me_x, xpeer, False)
+    for q in range(n_q):
+        sel_x[q // slots, q % slots] = ga_ref[idx_ref[q]] * hot_ref[mask_at + q]
+        sel_y[q // slots, q % slots] = gb_ref[idx_ref[n_q + q]] * hot_ref[mask_at + n_q + q]
+    sx_copies = send_rows(sel_x, land_sx, sx_s, sx_r, n_x, me_x, xpeer, False)
+    sy_copies = send_rows(sel_y, land_sy, sy_s, sy_r, n_y, me_y, ypeer, False)
     for s in range(slots):
-        usel_ref[s] = urows_ref[idx_ref[n_sel + s]] * hot_ref[mask_at + n_sel + s]
+        usel_ref[s] = urows_ref[idx_ref[2 * n_q + s]] * hot_ref[mask_at + 2 * n_q + s]
 
     wt = wt_ref[...]
     for s in range(slots):
@@ -187,17 +188,21 @@
         usel = usel_ref[s]
         stacked = jnp.concatenate([usel * wt[:, k:k + 1] for k in range(weeks)], axis=1)
         iterm[s] = jnp.dot(stacked, flat, precision=TERMS, preferred_element_type=jnp.float32)
-    land_terms[me_x] = iterm[...]
-
-    trm_copies = send_rows(iterm, land_terms, trm_s, trm_r, n_x, me_x, xpeer, True)
-    finish(sel_copies, land_sel, sel_s, sel_r, n_x, me_x, xpeer)
-
+    land_tx[me_x] = iterm[...]
+    land_ty[me_y] = iterm[...]
+    tx_copies = send_rows(iterm, land_tx, tx_s, tx_r, n_x, me_x, xpeer, True)
+    ty_copies = send_rows(iterm, land_ty, ty_s, ty_r, n_y, me_y, ypeer, True)
+
+    finish(sx_copies, land_sx, sx_s, sx_r, n_x, me_x, xpeer)
+    finish(sy_copies, land_sy, sy_s, sy_r, n_y, me_y, ypeer)
     w = w_ref[...]
     uterms = []
     for s in range(slots):
-        isel = send_sel[me_x, s]
+        isel = sel_x[me_x, s] + sel_y[me_y, s]
         for k in range(1, n_x):
-            isel = isel + land_sel[lax.rem(me_x + k, n_x), s]
+            isel = isel + land_sx[lax.rem(me_x + k, n_x), s]
+        for k in range(1, n_y):
+            isel = isel + land_sy[lax.rem(me_y + k, n_y), s]
         flat = xbuf[s].reshape(weeks * users, items)
         by_items = lax.dot_general(
             flat, isel, (((1,), (1,)), ((), ())), precision=TERMS, preferred_element_type=jnp.float32)
@@ -213,76 +218,82 @@
             upart[v, :, t * users:(t + 1) * users] = acc
     up_copies = send_rows(upart, land_up, up_s, up_r, n_v, me_v, vpeer, False)
 
-    finish(trm_copies, land_terms, trm_s, trm_r, n_x, me_x, xpeer)
-    sources = []
+    finish(tx_copies, land_tx, tx_s, tx_r, n_x, me_x, xpeer)
+    for y in range(n_y):
+        for l in range(half):
+            acc = None
+            for q in range(n_q):
+                term = land_tx[q // slots, q % slots] * hot_ref[hot_a_at + (q * n_y + y) * half + l]
+                acc = term if acc is None else acc + term
+            part_a[y, :, l * items:(l + 1) * items] = acc
+    pa_copies = send_rows(part_a, land_a, pa_s, pa_r, n_y, me_y, ypeer, False)
+    finish(ty_copies, land_ty, ty_s, ty_r, n_y, me_y, ypeer)
     for x in range(n_x):
-        for s in range(slots):
-            sources.append((x, s))
-    for y in range(n_y):
-        for l in range(item_own):
+        for l in range(half):
             acc = None
-            for x, s in sources:
-                at = item_hot_at + ((x * slots + s) * n_y + y) * item_own + l
-                term = land_terms[x, s] * hot_ref[at]
+            for q in range(n_q):
+                term = land_ty[q // slots, q % slots] * hot_ref[hot_b_at + (q * n_x + x) * half + l]
                 acc = term if acc is None else acc + term
-            ipart[y, :, l * items:(l + 1) * items] = acc
-    ip_copies = send_rows(ipart, land_ip, ip_s, ip_r, n_y, me_y, ypeer, False)
+            part_b[x, :, l * items:(l + 1) * items] = acc
+    pb_copies = send_rows(part_b, land_b, pb_s, pb_r, n_x, me_x, xpeer, False)
 
     finish(up_copies, land_up, up_s, up_r, n_v, me_v, vpeer)
     total_u = upart[me_v]
     for k in range(1, n_v):
         total_u = total_u + land_up[lax.rem(me_v + k, n_v)]
     users_out[...] = total_u
-    finish(ip_copies, land_ip, ip_s, ip_r, n_y, me_y, ypeer)
-    total_i = ipart[me_y]
+    finish(pa_copies, land_a, pa_s, pa_r, n_y, me_y, ypeer)
+    total_a = part_a[me_y]
     for k in range(1, n_y):
-        total_i = total_i + land_ip[lax.rem(me_y + k, n_y)]
-    items_out[...] = total_i
-
-
-def fused_middle(hot, idx, data, group_rows, user_rows, week_factor, n_x, n_v, n_y, per_owner, item_own,
-                 collective_id):
+        total_a = total_a + land_a[lax.rem(me_y + k, n_y)]
+    items_out[:, :half * items] = total_a
+    finish(pb_copies, land_b, pb_s, pb_r, n_x, me_x, xpeer)
+    total_b = part_b[me_x]
+    for k in range(1, n_x):
+        total_b = total_b + land_b[lax.rem(me_x + k, n_x)]
+    items_out[:, half * items:] = total_b
+
+
+def fused_middle(hot, idx, data, ga, gb, user_rows, week_factor, n_x, n_y, n_v, per_owner, half, collective_id):
     slots, weeks, users, items = data.shape
     rank = week_factor.shape[1]
     vmem = pl.BlockSpec(memory_space=pltpu.VMEM)
     smem = pl.BlockSpec(memory_space=pltpu.SMEM)
+    f32 = jnp.float32
     up_shape = (n_v, rank, per_owner * users)
-    ip_shape = (n_y, rank, item_own * items)
     return pl.pallas_call(
         _fused_kernel,
         out_shape=(
-            jax.ShapeDtypeStruct(up_shape[1:], jnp.float32),
-            jax.ShapeDtypeStruct(ip_shape[1:], jnp.float32),
+            jax.ShapeDtypeStruct(up_shape[1:], f32),
+            jax.ShapeDtypeStruct((rank, 2 * half * items), f32),
         ),
-        in_specs=[smem, smem, pl.BlockSpec(memory_space=pl.ANY), vmem, vmem, vmem, vmem],
+        in_specs=[smem, smem, pl.BlockSpec(memory_space=pl.ANY), vmem, vmem, vmem, vmem, vmem],
         out_specs=(vmem, vmem),
         scratch_shapes=[
-            pltpu.VMEM((n_x, slots, rank, items), jnp.float32),
-            pltpu.VMEM((slots, rank, users), jnp.float32),
-            pltpu.VMEM((slots, weeks, users, items), jnp.float32),
+            pltpu.VMEM((n_x, slots, rank, items), f32),
+            pltpu.VMEM((n_y, slots, rank, items), f32),
+            pltpu.VMEM((slots, rank, users), f32),
+            pltpu.VMEM((slots, weeks, users, items), f32),
             pltpu.SemaphoreType.DMA((slots,)),
-            pltpu.VMEM((n_x, slots, rank, items), jnp.float32),
-            pltpu.VMEM((slots, rank, items), jnp.float32),
-            pltpu.VMEM((n_x, slots, rank, items), jnp.float32),
-            pltpu.VMEM(up_shape, jnp.float32),
-            pltpu.VMEM(up_shape, jnp.float32),
-            pltpu.VMEM(ip_shape, jnp.float32),
-            pltpu.VMEM(ip_shape, jnp.float32),
-            pltpu.SemaphoreType.DMA((n_x,)),
-            pltpu.SemaphoreType.DMA((n_x,)),
-            pltpu.SemaphoreType.DMA((n_x,)),
-            pltpu.SemaphoreType.DMA((n_x,)),
-            pltpu.SemaphoreType.DMA((n_v,)),
-            pltpu.SemaphoreType.DMA((n_v,)),
-            pltpu.SemaphoreType.DMA((n_y,)),
-            pltpu.SemaphoreType.DMA((n_y,)),
-        ],
+            pltpu.VMEM((n_x, slots, rank, items), f32),
+            pltpu.VMEM((n_y, slots, rank, items), f32),
+            pltpu.VMEM((slots, rank, items), f32),
+            pltpu.VMEM((n_x, slots, rank, items), f32),
+            pltpu.VMEM((n_y, slots, rank, items), f32),
+            pltpu.VMEM(up_shape, f32),
+            pltpu.VMEM(up_shape, f32),
+            pltpu.VMEM((n_y, rank, half * items), f32),
+            pltpu.VMEM((n_y, rank, half * items), f32),
+            pltpu.VMEM((n_x, rank, half * items), f32),
+            pltpu.VMEM((n_x, rank, half * items), f32),
+        ] + [pltpu.SemaphoreType.DMA((n,)) for n in (n_x, n_x, n_y, n_y, n_x, n_x, n_y, n_y, n_v, n_v, n_y, n_y,
+                                                     n_x, n_x)],
         compiler_params=pltpu.CompilerParams(
             collective_id=collective_id, has_side_effects=True, vmem_limit_bytes=48 * 1024 * 1024),
         cost_estimate=pl.CostEstimate(
             flops=4 * slots * weeks * users * items * rank, transcendentals=0,
             bytes_accessed=4 * slots * weeks * users * items),
-    )(hot, idx, data, group_rows, user_rows, week_factor, week_factor.T)
+    )(hot, idx, data, ga, gb, user_rows, week_factor, week_factor.T)
 
 
 def slot_terms(data, item_sel, user_sel, week_factor):
@@ -330,34 +341,50 @@
     live = (slot_order < counts[0, 0]).astype(jnp.float32)
     id_piece = jnp.zeros((8, 128), jnp.int32).at[0, :slot_total].set(item_ids).at[1, 0].set(counts[0, 0])
 
-    group_rows, id_rows, user_rows = exchange(
-        [(("uy",), (y_size,), "bcast"), (("ux",), (x_size,), "bcast"), (("iz", "ic"), (z_size, c_size), "bcast")],
-        [item_factor.reshape(rank_size, item_own, item_width).transpose(1, 0, 2), id_piece,
+    half = item_own // 2
+    blocks = item_factor.reshape(rank_size, item_own, item_width).transpose(1, 0, 2)
+    ga, gb, ids_x, ids_y, user_rows = exchange(
+        [(("uy",), (y_size,), "bcast"), (("ux",), (x_size,), "bcast"), (("ux",), (x_size,), "bcast"),
+         (("uy",), (y_size,), "bcast"), (("iz", "ic"), (z_size, c_size), "bcast")],
+        [blocks[:half], blocks[half:], id_piece, id_piece,
          user_factor.reshape(rank_size, user_own, user_width).transpose(1, 0, 2)],
         0,
     )
-    group_rows = group_rows.reshape(-1, rank_size, item_width)
+    ga = ga.reshape(-1, rank_size, item_width)
+    gb = gb.reshape(-1, rank_size, item_width)
     user_rows = user_rows.reshape(-1, rank_size, user_width)
+    me_y = lax.axis_index("uy")
+
     n_v = z_size * c_size
     user_block_total = n_v * user_own
     user_hot = (user_ids[:, None] == jnp.arange(user_block_total, dtype=jnp.int32)[None, :]).astype(jnp.float32)
     user_hot = user_hot * live[:, None]
 
-    wanted = id_rows[:, 0, :slot_total]
-    wanted_live = slot_order[None, :] < id_rows[:, 1, 0:1]
-    owner_group = wanted // group_blocks
-    local_block = wanted % group_blocks
-    take = (owner_group == me_x) & wanted_live
-    hot = jnp.where(
-        take[:, :, None],
-        (local_block[:, :, None] == jnp.arange(group_blocks, dtype=jnp.int32)[None, None, :]).astype(jnp.float32),
-        0.0,
-    )
-    hot_all = jnp.concatenate([user_hot.reshape(-1), hot.reshape(-1), take.astype(jnp.float32).reshape(-1), live])
-    idx_all = jnp.concatenate([local_block.reshape(-1), user_ids]).astype(jnp.int32)
+    def requests(id_rows):
+        wanted = id_rows[:, 0, :slot_total]
+        wanted_live = slot_order[None, :] < id_rows[:, 1, 0:1]
+        owner_x = wanted // group_blocks
+        owner_y = (wanted // item_own) % y_size
+        within = wanted % item_own
+        return wanted_live, owner_x, owner_y, within
+
+    live_x, ox_x, oy_x, l_x = requests(ids_x)
+    take_a = (ox_x == me_x) & (l_x < half) & live_x
+    idx_a = oy_x * half + l_x
+    hot_a = take_a[:, :, None, None] & (oy_x[:, :, None, None] == jnp.arange(y_size)[None, None, :, None]) & (
+        l_x[:, :, None, None] == jnp.arange(half)[None, None, None, :])
+    live_y, ox_y, oy_y, l_y = requests(ids_y)
+    take_b = (oy_y == me_y) & (l_y >= half) & live_y
+    idx_b = ox_y * half + (l_y - half)
+    hot_b = take_b[:, :, None, None] & (ox_y[:, :, None, None] == jnp.arange(x_size)[None, None, :, None]) & (
+        (l_y - half)[:, :, None, None] == jnp.arange(half)[None, None, None, :])
+    hot_all = jnp.concatenate([
+        user_hot.reshape(-1), hot_a.astype(jnp.float32).reshape(-1), hot_b.astype(jnp.float32).reshape(-1),
+        take_a.astype(jnp.float32).reshape(-1), take_b.astype(jnp.float32).reshape(-1), live])
+    idx_all = jnp.concatenate([
+        jnp.where(take_a, idx_a, 0).reshape(-1), jnp.where(take_b, idx_b, 0).reshape(-1), user_ids]).astype(jnp.int32)
     m_users, m_items = fused_middle(
-        hot_all, idx_all, tiles[0, 0], group_rows, user_rows, week_factor, x_size, n_v, y_size, user_own,
-        item_own, 1)
+        hot_all, idx_all, tiles[0, 0], ga, gb, user_rows, week_factor, x_size, y_size, n_v, user_own, half, 1)
     return (m_users, m_items)
 
 

time: 67.3 us -> 62.9 us (0.935)
  Pallas kernels: 53 us -> 46.3 us
  local copies, waits for them, and re-layouts: 9.97 us -> 12.3 us
    pallas_call x1, Pallas kernels: 22.7 us -> 17.4 us  [exchange(): pl.pallas_call(functools.partial(_exchange_kernel, plan), out_shape=tuple...]
    unnamed x13 -> x15, local copies, waits for them, and re-layouts: 5.13 us -> 6.93 us
    pallas_call x1, Pallas kernels: 30.3 us -> 29 us  [fused_middle(): pl.pallas_call(_fused_kernel, out_shape=(jax.ShapeDtypeStruct(up_shape[1:...]
    slice x2 -> x3, local copies, waits for them, and re-layouts: 1.61 us -> 2.44 us  [the longest x1 0.97 us: requests(): wanted_live = slot_order[None, :] < id_rows[:, 1, 0:1]]
    transpose x1, local copies, waits for them, and re-layouts: 0.72 us -> 0.02 us  [on_device(): item_factor.reshape(rank_size, item_own, item_width).transpose(1, 0, 2)]
where the time goes in v8:
time: 62.9 us; the launch traced here: 62.2 us
  Pallas kernels  46.3 us (74%)
  local copies, waits for them, and re-layouts  12.3 us (20%)
  other arithmetic  2.17 us (3%)
  between operations  1.41 us (2%)
    pallas_call x1, Pallas kernels, fused_middle(): pl.pallas_call(_fused_kernel, out_shape=(jax.ShapeDtypeStruct(up_shape[1:...  29 us
    pallas_call x1, Pallas kernels, exchange(): pl.pallas_call(functools.partial(_exchange_kernel, plan), out_shape=tuple...  17.4 us
    unnamed x15, local copies, waits for them, and re-layouts  6.93 us
    transpose x1, local copies, waits for them, and re-layouts, on_device(): user_factor.reshape(rank_size, user_own, user_width).transpose(1, 0, 2)  1.48 us

profile of v8, /device:TPU:1, one launch (start us, length us, event | category | flops | bytes accessed | tf_op | source)
XLA Modules:
  0.0 62.2 jit_solution(4351522017494530460)
XLA Ops:
  0.6 0.9 %copy-done = f32[64,1024]{1,0:T(8,128)S(1)} copy-done((f32[64,1024]{1,0:T(8,128)S(1)}, f32[64,1024]{1,0:T(8,128)}, u32[]{:S(2)}) %copy-start) | copy-done | bytes 262168
  1.6 0.7 %fusion.16 = (f32[4,64,128]{2,1,0:T(8,128)}, f32[4,64,128]{2,1,0:T(8,128)}) fusion(f32[8,64,128]{2,1,0:T(8,128)S(1)} %bitcast_bitcast_fusion), kind=kLoop, calls=%fused_computation.87 | loop fusion | bytes 524288 | tf_op jit(solution)/shard_map/slice | solution.py:349
  3.0 0.7 %scatter.6 = s32[8,128]{1,0:T(8,128)S(1)} pad(s32[1,4]{1,0:T(1,128)} %bitcast.36, s32[]{:T(128)} %constant.138.clone.1), padding=0_7x0_124 | pad | bytes 4116 | tf_op jit(solution)/shard_map/scatter | solution.py:342
  3.7 1.5 %bitcast_bitcast_fusion.1.refs_4_ = f32[2,64,128]{2,1,0:T(8,128)} fusion(f32[64,256]{1,0:T(8,128)} %param.15), kind=kLoop, calls=%fused_computation.1 | loop fusion | bytes 131072 | tf_op jit(solution)/shard_map/transpose | solution.py:350
  5.2 17.4 %shard_map.86 = (f32[4,4,64,128]{3,2,1,0:T(8,128)}, f32[4,4,64,128]{3,2,1,0:T(8,128)}, s32[4,8,128]{2,1,0:T(8,128)}, s32[4,8,128]{2,1,0:T(8,128)}, f32[8,2,64,128]{3,2,1,0:T(8,128)}) custom-call(f32[4,64,128]{2,1,0:T(8,128)} %get-tuple-element.41.refs_0_, f32[4,64,128]{2,1,0:T(8,128)} %get-tuple-element.40.refs_1_, s32[8,128]{1,0:T(8,128)} %copy-done.5, ...), custom_call_target="tpu_custom_call" | custom-call | tf_op jit(solution)/shard_map/pallas_call | solution.py:87
  22.5 0.8 %slice_reduce_fusion.2 = (s32[4,4]{1,0:T(4,128)S(1)}, s32[4,1,4]{2,1,0:T(1,128)S(1)}, s32[4,1,4]{2,1,0:T(1,128)S(1)}, s32[4,4]{1,0:T(4,128)S(1)}) fusion(s32[4,8,128]{2,1,0:T(8,128)} %get-tuple-element.32, s32[4,8,128]{2,1,0:T(8,128)} %get-tuple-element.31), kind=kLoop, calls=%fused_computation.85 | loop fusion | bytes 384 | tf_op jit(solution)/shard_map/slice | solution.py:364
  23.3 1.0 %slice_reduce_fusion = (s32[4]{0:T(128)S(1)}, s32[4]{0:T(128)S(1)}) fusion(s32[4,8,128]{2,1,0:T(8,128)} %get-tuple-element.32, s32[4,8,128]{2,1,0:T(8,128)} %get-tuple-element.31), kind=kLoop, calls=%fused_computation.42 | loop fusion | bytes 64 | tf_op jit(solution)/shard_map/slice | solution.py:365
  24.4 0.1 lt.115
  24.6 0.1 lt.112
  24.8 0.7 %pad_add_fusion.idx_ref = s32[36]{0:T(128)S(1)} fusion(s32[4]{0:T(128)} %bitcast.34, s32[16]{0:T(128)S(1)} %get-tuple-element.38, s32[16]{0:T(128)S(1)} %get-tuple-element.36), kind=kLoop, calls=%fused_computation.81 | loop fusion | flops 72 | bytes 288 | tf_op jit(solution)/shard_map/concatenate | solution.py:384
  25.7 0.1 and_convert_fusion
  25.8 0.1 reshape.393
  26.1 0.1 and_convert_fusion.1
  26.2 0.1 reshape.392
  26.4 0.7 %fusion.8 = f32[4,16]{1,0:T(4,128)S(1)} fusion(f32[4]{0:T(128)S(1)} %compare_convert_fusion, s32[4]{0:T(128)} %bitcast.35), kind=kLoop, calls=%fused_computation.49 | loop fusion | flops 128 | bytes 288 | tf_op jit(solution)/shard_map/mul | solution.py:361
  27.1 0.1 mul.20
  27.2 0.8 %copy.12 = f32[32,64]{0,1:T(8,128)S(1)} copy(f32[32,64]{1,0:T(8,128)} %w_ref.1) | data formatting | bytes 16384 | tf_op args[6]
  28.1 1.0 %copy-done.1 = f32[4,4,64,128]{3,2,1,0:T(8,128)S(1)} copy-done((f32[4,4,64,128]{3,2,1,0:T(8,128)S(1)}, f32[4,4,64,128]{3,2,1,0:T(8,128)}, u32[]{:S(2)}) %copy-start.1) | copy-done | bytes 524312
  29.1 1.0 %copy-done.2 = f32[4,4,64,128]{3,2,1,0:T(8,128)S(1)} copy-done((f32[4,4,64,128]{3,2,1,0:T(8,128)S(1)}, f32[4,4,64,128]{3,2,1,0:T(8,128)}, u32[]{:S(2)}) %copy-start.2) | copy-done | bytes 524312
  30.1 1.0 %copy-done.3 = f32[8,2,64,128]{3,2,1,0:T(8,128)S(1)} copy-done((f32[8,2,64,128]{3,2,1,0:T(8,128)S(1)}, f32[8,2,64,128]{3,2,1,0:T(8,128)}, u32[]{:S(2)}) %copy-start.3) | copy-done | bytes 524312
  31.2 0.7 %copy-done.4 = f32[32,64]{1,0:T(8,128)S(1)} copy-done((f32[32,64]{1,0:T(8,128)S(1)}, f32[32,64]{1,0:T(8,128)}, u32[]{:S(2)}) %copy-start.4) | copy-done | bytes 8216
  31.9 29.0 %shard_map.87 = (f32[64,256]{1,0:T(8,128)S(1)}, f32[64,1024]{1,0:T(8,128)S(1)}) custom-call(f32[612]{0:T(1024)S(1)} %concatenate.10.hot_ref, s32[36]{0:T(128)S(1)} %pad_add_fusion.idx_ref, f32[4,32,128,128]{3,2,1,0:T(8,128)} %bitcast.29, f32[16,64,128]{2,1,0:T(8,128)S(1)} %bitcast.25, f32[16,64,128]{2,1,0:T(8,128)S(1)} %bitcast.26, ...), custom_call_target="tpu_custom_call" | custom-call | flops 536870912 | bytes 8388608 | tf_op jit(solution)/shard_map/pallas_call | solution.py:264
  60.9 0.6 %copy.21 = f32[64,256]{1,0:T(8,128)} copy(f32[64,256]{1,0:T(8,128)S(1)} %get-tuple-element.60) | data formatting | bytes 131072
  61.5 0.7 %copy.22 = f32[64,1024]{1,0:T(8,128)} copy(f32[64,1024]{1,0:T(8,128)S(1)} %get-tuple-element.61) | data formatting | bytes 524288
  (25 shorter events, 0.9 us)
Async XLA Ops:
  0.6 1.0 %copy-start = (f32[64,1024]{1,0:T(8,128)S(1)}, f32[64,1024]{1,0:T(8,128)}, u32[]{:S(2)}) copy-start(f32[64,1024]{1,0:T(8,128)} %param.16) | copy-start | bytes 786436
  3.7 1.5 %copy-start.5 = (s32[8,128]{1,0:T(8,128)}, s32[8,128]{1,0:T(8,128)S(1)}, u32[]{:S(2)}) copy-start(s32[8,128]{1,0:T(8,128)S(1)} %scatter.9.refs_2_.refs_3_) | copy-start | bytes 12292
  28.0 1.0 %copy-start.1 = (f32[4,4,64,128]{3,2,1,0:T(8,128)S(1)}, f32[4,4,64,128]{3,2,1,0:T(8,128)}, u32[]{:S(2)}) copy-start(f32[4,4,64,128]{3,2,1,0:T(8,128)} %get-tuple-element.33) | copy-start | bytes 1572868
  29.1 1.0 %copy-start.2 = (f32[4,4,64,128]{3,2,1,0:T(8,128)S(1)}, f32[4,4,64,128]{3,2,1,0:T(8,128)}, u32[]{:S(2)}) copy-start(f32[4,4,64,128]{3,2,1,0:T(8,128)} %get-tuple-element.34) | copy-start | bytes 1572868
  30.1 1.0 %copy-start.3 = (f32[8,2,64,128]{3,2,1,0:T(8,128)S(1)}, f32[8,2,64,128]{3,2,1,0:T(8,128)}, u32[]{:S(2)}) copy-start(f32[8,2,64,128]{3,2,1,0:T(8,128)} %get-tuple-element.35) | copy-start | bytes 1572868
  31.2 0.7 %copy-start.4 = (f32[32,64]{1,0:T(8,128)S(1)}, f32[32,64]{1,0:T(8,128)}, u32[]{:S(2)}) copy-start(f32[32,64]{1,0:T(8,128)} %w_ref.1) | copy-start | bytes 24580

commit v9 on v8

--- a/solution.py
+++ b/solution.py
@@ -112,8 +112,8 @@
     iterm_ref[0] = jnp.dot(stacked, flat, precision=HIGHEST, preferred_element_type=jnp.float32)
 
 
-def _fused_kernel(hot_ref, idx_ref, tiles_hbm, ga_ref, gb_ref, urows_ref, w_ref, wt_ref, users_out, items_out,
-                  sel_x, sel_y, usel_ref, xbuf, xsem, land_sx, land_sy, iterm, land_tx, land_ty,
+def _fused_kernel(hot_ref, idx_ref, tiles_hbm, ga_hbm, gb_hbm, urows_hbm, w_ref, wt_ref, users_out, items_out,
+                  ga_ref, gb_ref, urows_ref, gsem, sel_x, sel_y, usel_ref, xbuf, xsem, land_sx, land_sy, iterm, land_tx, land_ty,
                   upart, land_up, part_a, land_a, part_b, land_b,
                   sx_s, sx_r, sy_s, sy_r, tx_s, tx_r, ty_s, ty_r, up_s, up_r, pa_s, pa_r, pb_s, pb_r):
     slots, weeks, users, items = xbuf.shape
@@ -139,6 +139,12 @@
     def vpeer(d):
         return {"iz": d // n_c, "ic": d % n_c}
 
+    factor_loads = []
+    for i, (src, dst) in enumerate(((ga_hbm, ga_ref), (gb_hbm, gb_ref), (urows_hbm, urows_ref))):
+        cp = pltpu.make_async_copy(src, dst, gsem.at[i])
+        cp.start()
+        factor_loads.append(cp)
+
     barrier = pltpu.get_barrier_semaphore()
     for k in range(1, n_x):
         pl.semaphore_signal(barrier, inc=1, device_id=xpeer(lax.rem(me_x + k, n_x)), device_id_type=MESH_IDS)
@@ -173,6 +179,8 @@
                 src_ref=land.at[src], dst_ref=land.at[src], send_sem=ssem.at[k], recv_sem=rsem.at[k],
                 device_id=peer(src), device_id_type=MESH_IDS).wait_recv()
 
+    for cp in factor_loads:
+        cp.wait()
     for q in range(n_q):
         sel_x[q // slots, q % slots] = ga_ref[idx_ref[q]] * hot_ref[mask_at + q]
         sel_y[q // slots, q % slots] = gb_ref[idx_ref[n_q + q]] * hot_ref[mask_at + n_q + q]
@@ -267,9 +275,13 @@
             jax.ShapeDtypeStruct(up_shape[1:], f32),
             jax.ShapeDtypeStruct((rank, 2 * half * items), f32),
         ),
-        in_specs=[smem, smem, pl.BlockSpec(memory_space=pl.ANY), vmem, vmem, vmem, vmem, vmem],
+        in_specs=[smem, smem] + [pl.BlockSpec(memory_space=pl.ANY)] * 4 + [vmem, vmem],
         out_specs=(vmem, vmem),
         scratch_shapes=[
+            pltpu.VMEM(ga.shape, f32),
+            pltpu.VMEM(gb.shape, f32),
+            pltpu.VMEM(user_rows.shape, f32),
+            pltpu.SemaphoreType.DMA((3,)),
             pltpu.VMEM((n_x, slots, rank, items), f32),
             pltpu.VMEM((n_y, slots, rank, items), f32),
             pltpu.VMEM((slots, rank, users), f32),

time: 62.9 us -> 62.8 us (level)
  no operation moved by 1% of the time
where the time goes in v9:
time: 62.8 us; the launch traced here: 62.1 us
  Pallas kernels  46.3 us (74%)
  local copies, waits for them, and re-layouts  12.3 us (20%)
  other arithmetic  2.17 us (3%)
  between operations  1.41 us (2%)
    pallas_call x1, Pallas kernels, fused_middle(): pl.pallas_call(_fused_kernel, out_shape=(jax.ShapeDtypeStruct(up_shape[1:...  28.9 us
    pallas_call x1, Pallas kernels, exchange(): pl.pallas_call(functools.partial(_exchange_kernel, plan), out_shape=tuple...  17.4 us
    unnamed x15, local copies, waits for them, and re-layouts  6.93 us
    transpose x1, local copies, waits for them, and re-layouts, on_device(): user_factor.reshape(rank_size, user_own, user_width).transpose(1, 0, 2)  1.48 us

profile of v9, /device:TPU:1, one launch (start us, length us, event | category | flops | bytes accessed | tf_op | source)
XLA Modules:
  0.0 62.1 jit_solution(10540776529168052221)
XLA Ops:
  0.6 0.9 %copy-done = f32[64,1024]{1,0:T(8,128)S(1)} copy-done((f32[64,1024]{1,0:T(8,128)S(1)}, f32[64,1024]{1,0:T(8,128)}, u32[]{:S(2)}) %copy-start) | copy-done | bytes 262168
  1.6 0.7 %fusion.16 = (f32[4,64,128]{2,1,0:T(8,128)}, f32[4,64,128]{2,1,0:T(8,128)}) fusion(f32[8,64,128]{2,1,0:T(8,128)S(1)} %bitcast_bitcast_fusion), kind=kLoop, calls=%fused_computation.87 | loop fusion | bytes 524288 | tf_op jit(solution)/shard_map/slice | solution.py:361
  3.0 0.7 %scatter.6 = s32[8,128]{1,0:T(8,128)S(1)} pad(s32[1,4]{1,0:T(1,128)} %bitcast.36, s32[]{:T(128)} %constant.138.clone.1), padding=0_7x0_124 | pad | bytes 4116 | tf_op jit(solution)/shard_map/scatter | solution.py:354
  3.7 1.5 %bitcast_bitcast_fusion.1.refs_4_ = f32[2,64,128]{2,1,0:T(8,128)} fusion(f32[64,256]{1,0:T(8,128)} %param.15), kind=kLoop, calls=%fused_computation.1 | loop fusion | bytes 131072 | tf_op jit(solution)/shard_map/transpose | solution.py:362
  5.2 17.4 %shard_map.86 = (f32[4,4,64,128]{3,2,1,0:T(8,128)}, f32[4,4,64,128]{3,2,1,0:T(8,128)}, s32[4,8,128]{2,1,0:T(8,128)}, s32[4,8,128]{2,1,0:T(8,128)}, f32[8,2,64,128]{3,2,1,0:T(8,128)}) custom-call(f32[4,64,128]{2,1,0:T(8,128)} %get-tuple-element.41.refs_0_, f32[4,64,128]{2,1,0:T(8,128)} %get-tuple-element.40.refs_1_, s32[8,128]{1,0:T(8,128)} %copy-done.5, ...), custom_call_target="tpu_custom_call" | custom-call | tf_op jit(solution)/shard_map/pallas_call | solution.py:87
  22.5 0.8 %slice_reduce_fusion.2 = (s32[4,4]{1,0:T(4,128)S(1)}, s32[4,1,4]{2,1,0:T(1,128)S(1)}, s32[4,1,4]{2,1,0:T(1,128)S(1)}, s32[4,4]{1,0:T(4,128)S(1)}) fusion(s32[4,8,128]{2,1,0:T(8,128)} %get-tuple-element.32, s32[4,8,128]{2,1,0:T(8,128)} %get-tuple-element.31), kind=kLoop, calls=%fused_computation.85 | loop fusion | bytes 384 | tf_op jit(solution)/shard_map/slice | solution.py:376
  23.3 1.0 %slice_reduce_fusion = (s32[4]{0:T(128)S(1)}, s32[4]{0:T(128)S(1)}) fusion(s32[4,8,128]{2,1,0:T(8,128)} %get-tuple-element.32, s32[4,8,128]{2,1,0:T(8,128)} %get-tuple-element.31), kind=kLoop, calls=%fused_computation.42 | loop fusion | bytes 64 | tf_op jit(solution)/shard_map/slice | solution.py:377
  24.4 0.1 lt.115
  24.6 0.1 lt.112
  24.8 0.7 %pad_add_fusion.idx_ref = s32[36]{0:T(128)S(1)} fusion(s32[4]{0:T(128)} %bitcast.34, s32[16]{0:T(128)S(1)} %get-tuple-element.38, s32[16]{0:T(128)S(1)} %get-tuple-element.36), kind=kLoop, calls=%fused_computation.81 | loop fusion | flops 72 | bytes 288 | tf_op jit(solution)/shard_map/concatenate | solution.py:396
  25.7 0.1 and_convert_fusion
  25.8 0.1 reshape.393
  26.1 0.1 and_convert_fusion.1
  26.2 0.1 reshape.392
  26.4 0.7 %fusion.8 = f32[4,16]{1,0:T(4,128)S(1)} fusion(f32[4]{0:T(128)S(1)} %compare_convert_fusion, s32[4]{0:T(128)} %bitcast.35), kind=kLoop, calls=%fused_computation.49 | loop fusion | flops 128 | bytes 288 | tf_op jit(solution)/shard_map/mul | solution.py:373
  27.1 0.1 mul.20
  27.2 0.8 %copy.12 = f32[32,64]{0,1:T(8,128)S(1)} copy(f32[32,64]{1,0:T(8,128)} %w_ref.1) | data formatting | bytes 16384 | tf_op args[6]
  28.1 1.0 %copy-done.1 = f32[4,4,64,128]{3,2,1,0:T(8,128)S(1)} copy-done((f32[4,4,64,128]{3,2,1,0:T(8,128)S(1)}, f32[4,4,64,128]{3,2,1,0:T(8,128)}, u32[]{:S(2)}) %copy-start.1) | copy-done | bytes 524312
  29.1 1.0 %copy-done.2 = f32[4,4,64,128]{3,2,1,0:T(8,128)S(1)} copy-done((f32[4,4,64,128]{3,2,1,0:T(8,128)S(1)}, f32[4,4,64,128]{3,2,1,0:T(8,128)}, u32[]{:S(2)}) %copy-start.2) | copy-done | bytes 524312
  30.1 1.0 %copy-done.3 = f32[8,2,64,128]{3,2,1,0:T(8,128)S(1)} copy-done((f32[8,2,64,128]{3,2,1,0:T(8,128)S(1)}, f32[8,2,64,128]{3,2,1,0:T(8,128)}, u32[]{:S(2)}) %copy-start.3) | copy-done | bytes 524312
  31.2 0.7 %copy-done.4 = f32[32,64]{1,0:T(8,128)S(1)} copy-done((f32[32,64]{1,0:T(8,128)S(1)}, f32[32,64]{1,0:T(8,128)}, u32[]{:S(2)}) %copy-start.4) | copy-done | bytes 8216
  31.9 28.9 %shard_map.87 = (f32[64,256]{1,0:T(8,128)S(1)}, f32[64,1024]{1,0:T(8,128)S(1)}) custom-call(f32[612]{0:T(1024)S(1)} %concatenate.10.hot_ref, s32[36]{0:T(128)S(1)} %pad_add_fusion.idx_ref, f32[4,32,128,128]{3,2,1,0:T(8,128)} %bitcast.29, f32[16,64,128]{2,1,0:T(8,128)S(1)} %bitcast.25, f32[16,64,128]{2,1,0:T(8,128)S(1)} %bitcast.26, ...), custom_call_target="tpu_custom_call" | custom-call | flops 536870912 | bytes 8388608 | tf_op jit(solution)/shard_map/pallas_call | solution.py:272
  60.8 0.6 %copy.21 = f32[64,256]{1,0:T(8,128)} copy(f32[64,256]{1,0:T(8,128)S(1)} %get-tuple-element.60) | data formatting | bytes 131072
  61.4 0.7 %copy.22 = f32[64,1024]{1,0:T(8,128)} copy(f32[64,1024]{1,0:T(8,128)S(1)} %get-tuple-element.61) | data formatting | bytes 524288
  (25 shorter events, 0.9 us)
Async XLA Ops:
  0.6 1.0 %copy-start = (f32[64,1024]{1,0:T(8,128)S(1)}, f32[64,1024]{1,0:T(8,128)}, u32[]{:S(2)}) copy-start(f32[64,1024]{1,0:T(8,128)} %param.16) | copy-start | bytes 786436
  3.7 1.5 %copy-start.5 = (s32[8,128]{1,0:T(8,128)}, s32[8,128]{1,0:T(8,128)S(1)}, u32[]{:S(2)}) copy-start(s32[8,128]{1,0:T(8,128)S(1)} %scatter.9.refs_2_.refs_3_) | copy-start | bytes 12292
  28.0 1.0 %copy-start.1 = (f32[4,4,64,128]{3,2,1,0:T(8,128)S(1)}, f32[4,4,64,128]{3,2,1,0:T(8,128)}, u32[]{:S(2)}) copy-start(f32[4,4,64,128]{3,2,1,0:T(8,128)} %get-tuple-element.33) | copy-start | bytes 1572868
  29.1 1.0 %copy-start.2 = (f32[4,4,64,128]{3,2,1,0:T(8,128)S(1)}, f32[4,4,64,128]{3,2,1,0:T(8,128)}, u32[]{:S(2)}) copy-start(f32[4,4,64,128]{3,2,1,0:T(8,128)} %get-tuple-element.34) | copy-start | bytes 1572868
  30.1 1.0 %copy-start.3 = (f32[8,2,64,128]{3,2,1,0:T(8,128)S(1)}, f32[8,2,64,128]{3,2,1,0:T(8,128)}, u32[]{:S(2)}) copy-start(f32[8,2,64,128]{3,2,1,0:T(8,128)} %get-tuple-element.35) | copy-start | bytes 1572868
  31.2 0.7 %copy-start.4 = (f32[32,64]{1,0:T(8,128)S(1)}, f32[32,64]{1,0:T(8,128)}, u32[]{:S(2)}) copy-start(f32[32,64]{1,0:T(8,128)} %w_ref.1) | copy-start | bytes 24580

commit v10 on v9

--- a/solution.py
+++ b/solution.py
@@ -275,7 +275,7 @@
             jax.ShapeDtypeStruct(up_shape[1:], f32),
             jax.ShapeDtypeStruct((rank, 2 * half * items), f32),
         ),
-        in_specs=[smem, smem] + [pl.BlockSpec(memory_space=pl.ANY)] * 4 + [vmem, vmem],
+        in_specs=[smem, smem] + [pl.BlockSpec(memory_space=pltpu.HBM)] * 4 + [vmem, vmem],
         out_specs=(vmem, vmem),
         scratch_shapes=[
             pltpu.VMEM(ga.shape, f32),
@@ -301,7 +301,7 @@
         ] + [pltpu.SemaphoreType.DMA((n,)) for n in (n_x, n_x, n_y, n_y, n_x, n_x, n_y, n_y, n_v, n_v, n_y, n_y,
                                                      n_x, n_x)],
         compiler_params=pltpu.CompilerParams(
-            collective_id=collective_id, has_side_effects=True, vmem_limit_bytes=48 * 1024 * 1024),
+            collective_id=collective_id, has_side_effects=True),
         cost_estimate=pl.CostEstimate(
             flops=4 * slots * weeks * users * items * rank, transcendentals=0,
             bytes_accessed=4 * slots * weeks * users * items),

time: 62.8 us -> 63.4 us (level)
  Pallas kernels: 46.3 us -> 47.3 us
  local copies, waits for them, and re-layouts: 12.3 us -> 11.5 us
    unnamed x15 -> x7, local copies, waits for them, and re-layouts: 6.93 us -> 5.51 us
    pallas_call x1, Pallas kernels: 28.9 us -> 29.9 us  [fused_middle(): pl.pallas_call(_fused_kernel, out_shape=(jax.ShapeDtypeStruct(up_shape[1:...]
where the time goes in v10:
time: 63.4 us; the launch traced here: 62.8 us
  Pallas kernels  47.3 us (75%)
  local copies, waits for them, and re-layouts  11.5 us (18%)
  other arithmetic  2.69 us (4%)
  between operations  1.41 us (2%)
    pallas_call x1, Pallas kernels, fused_middle(): pl.pallas_call(_fused_kernel, out_shape=(jax.ShapeDtypeStruct(up_shape[1:...  29.9 us
    pallas_call x1, Pallas kernels, exchange(): pl.pallas_call(functools.partial(_exchange_kernel, plan), out_shape=tuple...  17.4 us
    unnamed x7, local copies, waits for them, and re-layouts  5.51 us
    transpose x1, local copies, waits for them, and re-layouts, on_device(): user_factor.reshape(rank_size, user_own, user_width).transpose(1, 0, 2)  1.48 us

profile of v10, /device:TPU:1, one launch (start us, length us, event | category | flops | bytes accessed | tf_op | source)
XLA Modules:
  0.0 62.8 jit_solution(2644401872005212572)
XLA Ops:
  0.6 0.9 %copy-done = f32[64,1024]{1,0:T(8,128)S(1)} copy-done((f32[64,1024]{1,0:T(8,128)S(1)}, f32[64,1024]{1,0:T(8,128)}, u32[]{:S(2)}) %copy-start) | copy-done | bytes 262168
  1.6 0.7 %fusion.16 = (f32[4,64,128]{2,1,0:T(8,128)}, f32[4,64,128]{2,1,0:T(8,128)}) fusion(f32[8,64,128]{2,1,0:T(8,128)S(1)} %bitcast_bitcast_fusion), kind=kLoop, calls=%fused_computation.87 | loop fusion | bytes 524288 | tf_op jit(solution)/shard_map/slice | solution.py:361
  3.0 0.7 %scatter.6 = s32[8,128]{1,0:T(8,128)S(1)} pad(s32[1,4]{1,0:T(1,128)} %bitcast.36, s32[]{:T(128)} %constant.138.clone.1), padding=0_7x0_124 | pad | bytes 4116 | tf_op jit(solution)/shard_map/scatter | solution.py:354
  3.7 1.5 %bitcast_bitcast_fusion.1.refs_4_ = f32[2,64,128]{2,1,0:T(8,128)} fusion(f32[64,256]{1,0:T(8,128)} %param.15), kind=kLoop, calls=%fused_computation.1 | loop fusion | bytes 131072 | tf_op jit(solution)/shard_map/transpose | solution.py:362
  5.2 17.4 %shard_map.86 = (f32[4,4,64,128]{3,2,1,0:T(8,128)}, f32[4,4,64,128]{3,2,1,0:T(8,128)}, s32[4,8,128]{2,1,0:T(8,128)}, s32[4,8,128]{2,1,0:T(8,128)}, f32[8,2,64,128]{3,2,1,0:T(8,128)}) custom-call(f32[4,64,128]{2,1,0:T(8,128)} %get-tuple-element.41.refs_0_, f32[4,64,128]{2,1,0:T(8,128)} %get-tuple-element.40.refs_1_, s32[8,128]{1,0:T(8,128)} %copy-done.1, ...), custom_call_target="tpu_custom_call" | custom-call | tf_op jit(solution)/shard_map/pallas_call | solution.py:87
  22.5 0.8 %slice_reduce_fusion.2 = (s32[4,4]{1,0:T(4,128)S(1)}, s32[4,1,4]{2,1,0:T(1,128)S(1)}, s32[4,1,4]{2,1,0:T(1,128)S(1)}, s32[4,4]{1,0:T(4,128)S(1)}) fusion(s32[4,8,128]{2,1,0:T(8,128)} %get-tuple-element.32, s32[4,8,128]{2,1,0:T(8,128)} %get-tuple-element.31), kind=kLoop, calls=%fused_computation.85 | loop fusion | bytes 384 | tf_op jit(solution)/shard_map/slice | solution.py:376
  23.3 1.0 %slice_reduce_fusion = (s32[4]{0:T(128)S(1)}, s32[4]{0:T(128)S(1)}) fusion(s32[4,8,128]{2,1,0:T(8,128)} %get-tuple-element.32, s32[4,8,128]{2,1,0:T(8,128)} %get-tuple-element.31), kind=kLoop, calls=%fused_computation.42 | loop fusion | bytes 64 | tf_op jit(solution)/shard_map/slice | solution.py:377
  24.3 0.1 lt.115
  24.4 0.1 squeeze.25
  24.6 0.1 lt.112
  24.7 0.1 squeeze.24
  24.8 1.2 %pad_add_fusion.idx_ref = s32[36]{0:T(128)} fusion(s32[4]{0:T(128)} %bitcast.34, s32[16]{0:T(128)S(1)} %get-tuple-element.38, s32[16]{0:T(128)S(1)} %get-tuple-element.36), kind=kLoop, calls=%fused_computation.81 | loop fusion | flops 72 | bytes 288 | tf_op jit(solution)/shard_map/concatenate | solution.py:396
  26.1 0.1 fusion.1
  26.2 0.1 and_convert_fusion
  26.3 0.1 reshape.393
  26.6 0.1 and_convert_fusion.1
  26.7 0.1 reshape.392
  26.9 0.7 %fusion.8 = f32[4,16]{1,0:T(4,128)S(1)} fusion(f32[4]{0:T(128)S(1)} %compare_convert_fusion, s32[4]{0:T(128)} %bitcast.35), kind=kLoop, calls=%fused_computation.49 | loop fusion | flops 128 | bytes 288 | tf_op jit(solution)/shard_map/mul | solution.py:373
  27.6 0.1 mul.20
  27.7 0.7 %concatenate.10.hot_ref = f32[612]{0:T(1024)} concatenate(f32[64]{0:T(128)S(1)} %mul.20, f32[256]{0:T(256)S(1)} %reshape.392, f32[256]{0:T(256)S(1)} %reshape.393, f32[16]{0:T(128)S(1)} %convert_element_type.35, f32[16]{0:T(128)S(1)} %convert_element_type.36, f32[4]{0:T(128)S(1)} %compare_convert_fusion), dimensions={0} | concatenate | bytes 4896 | tf_op jit(solution)/shard_map/concatenate | solution.py:393
  28.3 1.4 %copy.12 = f32[32,64]{0,1:T(8,128)} copy(f32[32,64]{1,0:T(8,128)} %w_ref.1) | data formatting | bytes 16384 | tf_op args[6]
  29.8 29.9 %shard_map.87 = (f32[64,256]{1,0:T(8,128)}, f32[64,1024]{1,0:T(8,128)}) custom-call(f32[612]{0:T(1024)} %concatenate.10.hot_ref, s32[36]{0:T(128)} %pad_add_fusion.idx_ref, f32[4,32,128,128]{3,2,1,0:T(8,128)} %bitcast.25, f32[16,64,128]{2,1,0:T(8,128)} %bitcast.26, f32[16,64,128]{2,1,0:T(8,128)} %bitcast.27, f32[16,64,128]{2,1,0:T(8,128)} %bitcast.28, ...), custom_call_target="tpu_custom_call" | custom-call | flops 536870912 | bytes 8388608 | tf_op jit(solution)/shard_map/pallas_call | solution.py:272
  59.7 1.5 %copy.21 = f32[64,256]{1,0:T(8,128)} copy(f32[64,256]{1,0:T(8,128)} %get-tuple-element.60) | data formatting | bytes 131072
  61.1 1.7 %copy.22 = f32[64,1024]{1,0:T(8,128)} copy(f32[64,1024]{1,0:T(8,128)} %get-tuple-element.61) | data formatting | bytes 524288
  (17 shorter events, 0.5 us)
Async XLA Ops:
  0.6 1.0 %copy-start = (f32[64,1024]{1,0:T(8,128)S(1)}, f32[64,1024]{1,0:T(8,128)}, u32[]{:S(2)}) copy-start(f32[64,1024]{1,0:T(8,128)} %param.16) | copy-start | bytes 786436
  3.7 1.5 %copy-start.1 = (s32[8,128]{1,0:T(8,128)}, s32[8,128]{1,0:T(8,128)S(1)}, u32[]{:S(2)}) copy-start(s32[8,128]{1,0:T(8,128)S(1)} %scatter.9.refs_2_.refs_3_) | copy-start | bytes 12292

commit v11 on v9

--- a/solution.py
+++ b/solution.py
@@ -112,7 +112,7 @@
     iterm_ref[0] = jnp.dot(stacked, flat, precision=HIGHEST, preferred_element_type=jnp.float32)
 
 
-def _fused_kernel(hot_ref, idx_ref, tiles_hbm, ga_hbm, gb_hbm, urows_hbm, w_ref, wt_ref, users_out, items_out,
+def _fused_kernel(req_ref, tiles_hbm, ga_hbm, gb_hbm, urows_hbm, w_ref, wt_ref, users_out, items_out,
                   ga_ref, gb_ref, urows_ref, gsem, sel_x, sel_y, usel_ref, xbuf, xsem, land_sx, land_sy, iterm, land_tx, land_ty,
                   upart, land_up, part_a, land_a, part_b, land_b,
                   sx_s, sx_r, sy_s, sy_r, tx_s, tx_r, ty_s, ty_r, up_s, up_r, pa_s, pa_r, pb_s, pb_r):
@@ -126,9 +126,25 @@
     me_y = lax.axis_index("uy")
     me_v = lax.axis_index("iz") * n_c + lax.axis_index("ic")
     n_q = n_x * slots
-    hot_a_at = slots * n_v * per_owner
-    hot_b_at = hot_a_at + n_q * n_y * half
-    mask_at = hot_b_at + n_q * n_x * half
+    group_blocks = n_y * 2 * half
+    one = jnp.float32(1.0)
+    zero = jnp.float32(0.0)
+
+    def request(q, base, cnt_base):
+        j = req_ref[base + q]
+        live = (q % slots) < req_ref[cnt_base + q // slots]
+        return j // group_blocks, (j // (2 * half)) % n_y, j % (2 * half), live
+
+    path_a, path_b = [], []
+    for q in range(n_q):
+        ox, oy, l, live = request(q, 0, n_q)
+        take = (ox == me_x) & (l < half) & live
+        path_a.append((take, oy, l, jnp.where(take, oy * half + l, 0)))
+        ox, oy, l, live = request(q, n_q + n_x, 2 * n_q + n_x)
+        take = (oy == me_y) & (l >= half) & live
+        path_b.append((take, ox, l - half, jnp.where(take, ox * half + l - half, 0)))
+    own_at = 2 * n_q + n_x + n_y
+    own_live = [s < req_ref[own_at + slots] for s in range(slots)]
 
     def xpeer(d):
         return {"ux": d}
@@ -182,12 +198,12 @@
     for cp in factor_loads:
         cp.wait()
     for q in range(n_q):
-        sel_x[q // slots, q % slots] = ga_ref[idx_ref[q]] * hot_ref[mask_at + q]
-        sel_y[q // slots, q % slots] = gb_ref[idx_ref[n_q + q]] * hot_ref[mask_at + n_q + q]
+        sel_x[q // slots, q % slots] = ga_ref[path_a[q][3]] * jnp.where(path_a[q][0], one, zero)
+        sel_y[q // slots, q % slots] = gb_ref[path_b[q][3]] * jnp.where(path_b[q][0], one, zero)
     sx_copies = send_rows(sel_x, land_sx, sx_s, sx_r, n_x, me_x, xpeer, False)
     sy_copies = send_rows(sel_y, land_sy, sy_s, sy_r, n_y, me_y, ypeer, False)
     for s in range(slots):
-        usel_ref[s] = urows_ref[idx_ref[2 * n_q + s]] * hot_ref[mask_at + 2 * n_q + s]
+        usel_ref[s] = urows_ref[req_ref[own_at + s]] * jnp.where(own_live[s], one, zero)
 
     wt = wt_ref[...]
     for s in range(slots):
@@ -220,9 +236,11 @@
     for v in range(n_v):
         for t in range(per_owner):
             col = v * per_owner + t
-            acc = uterms[0] * hot_ref[col]
-            for s in range(1, slots):
-                acc = acc + uterms[s] * hot_ref[s * n_v * per_owner + col]
+            acc = None
+            for s in range(slots):
+                hit = (req_ref[own_at + s] == col) & own_live[s]
+                term = uterms[s] * jnp.where(hit, one, zero)
+                acc = term if acc is None else acc + term
             upart[v, :, t * users:(t + 1) * users] = acc
     up_copies = send_rows(upart, land_up, up_s, up_r, n_v, me_v, vpeer, False)
 
@@ -231,7 +249,8 @@
         for l in range(half):
             acc = None
             for q in range(n_q):
-                term = land_tx[q // slots, q % slots] * hot_ref[hot_a_at + (q * n_y + y) * half + l]
+                take, oy, lq, _ = path_a[q]
+                term = land_tx[q // slots, q % slots] * jnp.where(take & (oy == y) & (lq == l), one, zero)
                 acc = term if acc is None else acc + term
             part_a[y, :, l * items:(l + 1) * items] = acc
     pa_copies = send_rows(part_a, land_a, pa_s, pa_r, n_y, me_y, ypeer, False)
@@ -240,7 +259,8 @@
         for l in range(half):
             acc = None
             for q in range(n_q):
-                term = land_ty[q // slots, q % slots] * hot_ref[hot_b_at + (q * n_x + x) * half + l]
+                take, ox, lq, _ = path_b[q]
+                term = land_ty[q // slots, q % slots] * jnp.where(take & (ox == x) & (lq == l), one, zero)
                 acc = term if acc is None else acc + term
             part_b[x, :, l * items:(l + 1) * items] = acc
     pb_copies = send_rows(part_b, land_b, pb_s, pb_r, n_x, me_x, xpeer, False)
@@ -262,7 +282,7 @@
     items_out[:, half * items:] = total_b
 
 
-def fused_middle(hot, idx, data, ga, gb, user_rows, week_factor, n_x, n_y, n_v, per_owner, half, collective_id):
+def fused_middle(req, data, ga, gb, user_rows, week_factor, n_x, n_y, n_v, per_owner, half, collective_id):
     slots, weeks, users, items = data.shape
     rank = week_factor.shape[1]
     vmem = pl.BlockSpec(memory_space=pltpu.VMEM)
@@ -275,7 +295,7 @@
             jax.ShapeDtypeStruct(up_shape[1:], f32),
             jax.ShapeDtypeStruct((rank, 2 * half * items), f32),
         ),
-        in_specs=[smem, smem] + [pl.BlockSpec(memory_space=pl.ANY)] * 4 + [vmem, vmem],
+        in_specs=[smem] + [pl.BlockSpec(memory_space=pl.ANY)] * 4 + [vmem, vmem],
         out_specs=(vmem, vmem),
         scratch_shapes=[
             pltpu.VMEM(ga.shape, f32),
@@ -305,7 +325,7 @@
         cost_estimate=pl.CostEstimate(
             flops=4 * slots * weeks * users * items * rank, transcendentals=0,
             bytes_accessed=4 * slots * weeks * users * items),
-    )(hot, idx, data, ga, gb, user_rows, week_factor, week_factor.T)
+    )(req, data, ga, gb, user_rows, week_factor, week_factor.T)
 
 
 def slot_terms(data, item_sel, user_sel, week_factor):
@@ -368,35 +388,11 @@
     me_y = lax.axis_index("uy")
 
     n_v = z_size * c_size
-    user_block_total = n_v * user_own
-    user_hot = (user_ids[:, None] == jnp.arange(user_block_total, dtype=jnp.int32)[None, :]).astype(jnp.float32)
-    user_hot = user_hot * live[:, None]
-
-    def requests(id_rows):
-        wanted = id_rows[:, 0, :slot_total]
-        wanted_live = slot_order[None, :] < id_rows[:, 1, 0:1]
-        owner_x = wanted // group_blocks
-        owner_y = (wanted // item_own) % y_size
-        within = wanted % item_own
-        return wanted_live, owner_x, owner_y, within
-
-    live_x, ox_x, oy_x, l_x = requests(ids_x)
-    take_a = (ox_x == me_x) & (l_x < half) & live_x
-    idx_a = oy_x * half + l_x
-    hot_a = take_a[:, :, None, None] & (oy_x[:, :, None, None] == jnp.arange(y_size)[None, None, :, None]) & (
-        l_x[:, :, None, None] == jnp.arange(half)[None, None, None, :])
-    live_y, ox_y, oy_y, l_y = requests(ids_y)
-    take_b = (oy_y == me_y) & (l_y >= half) & live_y
-    idx_b = ox_y * half + (l_y - half)
-    hot_b = take_b[:, :, None, None] & (ox_y[:, :, None, None] == jnp.arange(x_size)[None, None, :, None]) & (
-        (l_y - half)[:, :, None, None] == jnp.arange(half)[None, None, None, :])
-    hot_all = jnp.concatenate([
-        user_hot.reshape(-1), hot_a.astype(jnp.float32).reshape(-1), hot_b.astype(jnp.float32).reshape(-1),
-        take_a.astype(jnp.float32).reshape(-1), take_b.astype(jnp.float32).reshape(-1), live])
-    idx_all = jnp.concatenate([
-        jnp.where(take_a, idx_a, 0).reshape(-1), jnp.where(take_b, idx_b, 0).reshape(-1), user_ids]).astype(jnp.int32)
+    req = jnp.concatenate([
+        ids_x[:, 0, :slot_total].reshape(-1), ids_x[:, 1, 0], ids_y[:, 0, :slot_total].reshape(-1), ids_y[:, 1, 0],
+        user_ids, counts[0, 0].reshape(1)]).astype(jnp.int32)
     m_users, m_items = fused_middle(
-        hot_all, idx_all, tiles[0, 0], ga, gb, user_rows, week_factor, x_size, y_size, n_v, user_own, half, 1)
+        req, tiles[0, 0], ga, gb, user_rows, week_factor, x_size, y_size, n_v, user_own, half, 1)
     return (m_users, m_items)
 
 

time: 62.8 us -> 61.3 us (0.976)
  other arithmetic: 2.17 us -> 0 us
    concatenate x1 -> x0, other arithmetic: 0.73 us -> none  [on_device(): jnp.concatenate([jnp.where(take_a, idx_a, 0).reshape(-1), jnp.where(take_...]
    mul x1 -> x0, other arithmetic: 0.73 us -> none  [on_device(): user_hot = user_hot * live[:, None]]
    concatenate x1, local copies, waits for them, and re-layouts: 0.08 us -> 0.73 us  [on_device(): jnp.concatenate([ids_x[:, 0, :slot_total].reshape(-1), ids_x[:, 1, 0], id...]
    pallas_call x1, Pallas kernels: 28.9 us -> 29.5 us  [fused_middle(): pl.pallas_call(_fused_kernel, out_shape=(jax.ShapeDtypeStruct(up_shape[1:...]
where the time goes in v11:
time: 61.3 us; the launch traced here: 60.7 us
  Pallas kernels  46.9 us (77%)
  local copies, waits for them, and re-layouts  12.5 us (20%)
  between operations  1.34 us (2%)
    pallas_call x1, Pallas kernels, fused_middle(): pl.pallas_call(_fused_kernel, out_shape=(jax.ShapeDtypeStruct(up_shape[1:...  29.5 us
    pallas_call x1, Pallas kernels, exchange(): pl.pallas_call(functools.partial(_exchange_kernel, plan), out_shape=tuple...  17.3 us
    unnamed x15, local copies, waits for them, and re-layouts  6.93 us
    transpose x1, local copies, waits for them, and re-layouts, on_device(): user_factor.reshape(rank_size, user_own, user_width).transpose(1, 0, 2)  1.48 us

profile of v11, /device:TPU:1, one launch (start us, length us, event | category | flops | bytes accessed | tf_op | source)
XLA Modules:
  0.0 60.7 jit_solution(10570789603208683869)
XLA Ops:
  0.6 0.0 copy-start
  0.6 0.9 %copy-done = f32[64,1024]{1,0:T(8,128)S(1)} copy-done((f32[64,1024]{1,0:T(8,128)S(1)}, f32[64,1024]{1,0:T(8,128)}, u32[]{:S(2)}) %copy-start) | copy-done | bytes 262168
  1.6 0.7 %fusion = (f32[4,64,128]{2,1,0:T(8,128)}, f32[4,64,128]{2,1,0:T(8,128)}) fusion(f32[8,64,128]{2,1,0:T(8,128)S(1)} %bitcast_bitcast_fusion), kind=kLoop, calls=%fused_computation.6 | loop fusion | bytes 524288 | tf_op jit(solution)/shard_map/slice | solution.py:381
  3.0 0.7 %scatter.6 = s32[8,128]{1,0:T(8,128)S(1)} pad(s32[1,4]{1,0:T(1,128)} %bitcast.28, s32[]{:T(128)} %constant.54.clone.1), padding=0_7x0_124 | pad | bytes 4116 | tf_op jit(solution)/shard_map/scatter | solution.py:374
  3.7 0.0 copy-start.5
  3.7 1.5 %bitcast_bitcast_fusion.1.refs_4_ = f32[2,64,128]{2,1,0:T(8,128)} fusion(f32[64,256]{1,0:T(8,128)} %param.15), kind=kLoop, calls=%fused_computation.1 | loop fusion | bytes 131072 | tf_op jit(solution)/shard_map/transpose | solution.py:382
  5.2 0.0 copy-done.5
  5.2 17.3 %shard_map.86 = (f32[4,4,64,128]{3,2,1,0:T(8,128)}, f32[4,4,64,128]{3,2,1,0:T(8,128)}, s32[4,8,128]{2,1,0:T(8,128)}, s32[4,8,128]{2,1,0:T(8,128)}, f32[8,2,64,128]{3,2,1,0:T(8,128)}) custom-call(f32[4,64,128]{2,1,0:T(8,128)} %get-tuple-element.37.refs_0_, f32[4,64,128]{2,1,0:T(8,128)} %get-tuple-element.36.refs_1_, s32[8,128]{1,0:T(8,128)} %copy-done.5, ...), custom_call_target="tpu_custom_call" | custom-call | tf_op jit(solution)/shard_map/pallas_call | solution.py:87
  22.5 1.0 %slice_reduce_fusion = (s32[4]{0:T(128)S(1)}, s32[4]{0:T(128)S(1)}) fusion(s32[4,8,128]{2,1,0:T(8,128)} %get-tuple-element.32, s32[4,8,128]{2,1,0:T(8,128)} %get-tuple-element.31), kind=kLoop, calls=%fused_computation.2 | loop fusion | bytes 64 | tf_op jit(solution)/shard_map/slice | solution.py:392
  23.5 0.8 %slice_reduce_fusion.1 = (s32[4,4]{1,0:T(4,128)S(1)}, s32[4,4]{1,0:T(4,128)S(1)}) fusion(s32[4,8,128]{2,1,0:T(8,128)} %get-tuple-element.32, s32[4,8,128]{2,1,0:T(8,128)} %get-tuple-element.31), kind=kLoop, calls=%fused_computation.3 | loop fusion | bytes 256 | tf_op jit(solution)/shard_map/slice | solution.py:392
  24.2 0.1 reshape_squeeze.10
  24.3 0.1 reshape_squeeze.9
  24.4 0.7 %concatenate.7.req_ref = s32[45]{0:T(128)S(1)} concatenate(s32[16]{0:T(128)S(1)} %reshape_squeeze.9, s32[4]{0:T(128)S(1)} %get-tuple-element.41, s32[16]{0:T(128)S(1)} %reshape_squeeze.10, s32[4]{0:T(128)S(1)} %get-tuple-element.40, s32[4]{0:T(128)} %bitcast.29, s32[1]{0:T(128)} %bitcast.22), dimensions={0} | concatenate | bytes 360 | tf_op jit(solution)/shard_map/concatenate | solution.py:391
  25.1 0.8 %copy.12 = f32[32,64]{0,1:T(8,128)S(1)} copy(f32[32,64]{1,0:T(8,128)} %w_ref.1) | data formatting | bytes 16384 | tf_op args[6]
  25.9 0.0 copy-start.1
  25.9 1.0 %copy-done.1 = f32[4,4,64,128]{3,2,1,0:T(8,128)S(1)} copy-done((f32[4,4,64,128]{3,2,1,0:T(8,128)S(1)}, f32[4,4,64,128]{3,2,1,0:T(8,128)}, u32[]{:S(2)}) %copy-start.1) | copy-done | bytes 524312
  27.0 0.0 copy-start.2
  27.0 1.0 %copy-done.2 = f32[4,4,64,128]{3,2,1,0:T(8,128)S(1)} copy-done((f32[4,4,64,128]{3,2,1,0:T(8,128)S(1)}, f32[4,4,64,128]{3,2,1,0:T(8,128)}, u32[]{:S(2)}) %copy-start.2) | copy-done | bytes 524312
  28.0 0.0 copy-start.3
  28.0 1.0 %copy-done.3 = f32[8,2,64,128]{3,2,1,0:T(8,128)S(1)} copy-done((f32[8,2,64,128]{3,2,1,0:T(8,128)S(1)}, f32[8,2,64,128]{3,2,1,0:T(8,128)}, u32[]{:S(2)}) %copy-start.3) | copy-done | bytes 524312
  29.1 0.7 %copy-done.4 = f32[32,64]{1,0:T(8,128)S(1)} copy-done((f32[32,64]{1,0:T(8,128)S(1)}, f32[32,64]{1,0:T(8,128)}, u32[]{:S(2)}) %copy-start.4) | copy-done | bytes 8216
  29.8 29.5 %shard_map.87 = (f32[64,256]{1,0:T(8,128)S(1)}, f32[64,1024]{1,0:T(8,128)S(1)}) custom-call(s32[45]{0:T(128)S(1)} %concatenate.7.req_ref, f32[4,32,128,128]{3,2,1,0:T(8,128)} %bitcast.27, f32[16,64,128]{2,1,0:T(8,128)S(1)} %bitcast.23, f32[16,64,128]{2,1,0:T(8,128)S(1)} %bitcast.24, f32[16,64,128]{2,1,0:T(8,128)S(1)} %bitcast.25, f32[32,64]{1,0:T(8,128)S(1)} %copy-done.4, ...), custom_call_target="tpu_custom_call" | custom-call | flops 536870912 | bytes 8388608 | tf_op jit(solution)/shard_map/pallas_call | solution.py:292
  59.3 0.6 %copy.21 = f32[64,256]{1,0:T(8,128)} copy(f32[64,256]{1,0:T(8,128)S(1)} %get-tuple-element.44) | data formatting | bytes 131072
  60.0 0.7 %copy.22 = f32[64,1024]{1,0:T(8,128)} copy(f32[64,1024]{1,0:T(8,128)S(1)} %get-tuple-element.45) | data formatting | bytes 524288
  (3 shorter events, 0.1 us)
Async XLA Ops:
  0.6 1.0 %copy-start = (f32[64,1024]{1,0:T(8,128)S(1)}, f32[64,1024]{1,0:T(8,128)}, u32[]{:S(2)}) copy-start(f32[64,1024]{1,0:T(8,128)} %param.16) | copy-start | bytes 786436
  3.7 1.5 %copy-start.5 = (s32[8,128]{1,0:T(8,128)}, s32[8,128]{1,0:T(8,128)S(1)}, u32[]{:S(2)}) copy-start(s32[8,128]{1,0:T(8,128)S(1)} %scatter.9.refs_2_.refs_3_) | copy-start | bytes 12292
  25.9 1.0 %copy-start.1 = (f32[4,4,64,128]{3,2,1,0:T(8,128)S(1)}, f32[4,4,64,128]{3,2,1,0:T(8,128)}, u32[]{:S(2)}) copy-start(f32[4,4,64,128]{3,2,1,0:T(8,128)} %get-tuple-element.33) | copy-start | bytes 1572868
  27.0 1.0 %copy-start.2 = (f32[4,4,64,128]{3,2,1,0:T(8,128)S(1)}, f32[4,4,64,128]{3,2,1,0:T(8,128)}, u32[]{:S(2)}) copy-start(f32[4,4,64,128]{3,2,1,0:T(8,128)} %get-tuple-element.34) | copy-start | bytes 1572868
  28.0 1.0 %copy-start.3 = (f32[8,2,64,128]{3,2,1,0:T(8,128)S(1)}, f32[8,2,64,128]{3,2,1,0:T(8,128)}, u32[]{:S(2)}) copy-start(f32[8,2,64,128]{3,2,1,0:T(8,128)} %get-tuple-element.35) | copy-start | bytes 1572868
  29.1 0.7 %copy-start.4 = (f32[32,64]{1,0:T(8,128)S(1)}, f32[32,64]{1,0:T(8,128)}, u32[]{:S(2)}) copy-start(f32[32,64]{1,0:T(8,128)} %w_ref.1) | copy-start | bytes 24580

commit v12 on v11

--- a/solution.py
+++ b/solution.py
@@ -50,11 +50,23 @@
         me = _group_me(axes, sizes)
         for k in range(1, n):
             d = lax.rem(me + k, n)
-            src = ins[e].at[d] if mode == "a2a" else ins[e]
-            cp = pltpu.make_async_remote_copy(
-                src_ref=src, dst_ref=lands[e].at[me], send_sem=sends[e].at[k], recv_sem=recvs[e].at[k],
-                device_id=_peer(axes, sizes, d), device_id_type=MESH_IDS)
-            cp.start()
+            if isinstance(mode, tuple):
+                first, count = mode[1], mode[2]
+                width = lands[e].shape[-1]
+                for b in range(count):
+                    pltpu.make_async_remote_copy(
+                        src_ref=ins[e].at[:, (first + b) * width:(first + b + 1) * width],
+                        dst_ref=lands[e].at[me, b], send_sem=sends[e].at[k], recv_sem=recvs[e].at[k],
+                        device_id=_peer(axes, sizes, d), device_id_type=MESH_IDS).start()
+                cp = pltpu.make_async_remote_copy(
+                    src_ref=lands[e].at[me], dst_ref=lands[e].at[me], send_sem=sends[e].at[k],
+                    recv_sem=recvs[e].at[k], device_id=_peer(axes, sizes, d), device_id_type=MESH_IDS)
+            else:
+                src = ins[e].at[d] if mode == "a2a" else ins[e]
+                cp = pltpu.make_async_remote_copy(
+                    src_ref=src, dst_ref=lands[e].at[me], send_sem=sends[e].at[k], recv_sem=recvs[e].at[k],
+                    device_id=_peer(axes, sizes, d), device_id_type=MESH_IDS)
+                cp.start()
             copies.append((e, n, me, k, cp))
     for e, n, me, k, cp in copies:
         cp.wait_send()
@@ -70,7 +82,12 @@
         for k in range(1, n):
             src = lax.rem(me + k, n)
             outs[e][src] = lands[e][src]
-        outs[e][me] = ins[e][me] if mode == "a2a" else ins[e][...]
+        if isinstance(mode, tuple):
+            width = lands[e].shape[-1]
+            for b in range(mode[2]):
+                outs[e][me, b] = ins[e][:, (mode[1] + b) * width:(mode[1] + b + 1) * width]
+        else:
+            outs[e][me] = ins[e][me] if mode == "a2a" else ins[e][...]
 
 
 def exchange(plan, arrays, collective_id):
@@ -79,7 +96,10 @@
         n = 1
         for s in sizes:
             n *= s
-        piece = x.shape[1:] if mode == "a2a" else x.shape
+        if isinstance(mode, tuple):
+            piece = (mode[2], x.shape[0], mode[3])
+        else:
+            piece = x.shape[1:] if mode == "a2a" else x.shape
         out_shapes.append(jax.ShapeDtypeStruct((n,) + tuple(piece), x.dtype))
         scratch_lands.append(pltpu.VMEM((n,) + tuple(piece), x.dtype))
         sems_s.append(pltpu.SemaphoreType.DMA((n,)))
@@ -374,12 +394,12 @@
     id_piece = jnp.zeros((8, 128), jnp.int32).at[0, :slot_total].set(item_ids).at[1, 0].set(counts[0, 0])
 
     half = item_own // 2
-    blocks = item_factor.reshape(rank_size, item_own, item_width).transpose(1, 0, 2)
     ga, gb, ids_x, ids_y, user_rows = exchange(
-        [(("uy",), (y_size,), "bcast"), (("ux",), (x_size,), "bcast"), (("ux",), (x_size,), "bcast"),
-         (("uy",), (y_size,), "bcast"), (("iz", "ic"), (z_size, c_size), "bcast")],
-        [blocks[:half], blocks[half:], id_piece, id_piece,
-         user_factor.reshape(rank_size, user_own, user_width).transpose(1, 0, 2)],
+        [(("uy",), (y_size,), ("blocks", 0, half, item_width)),
+         (("ux",), (x_size,), ("blocks", half, half, item_width)),
+         (("ux",), (x_size,), "bcast"), (("uy",), (y_size,), "bcast"),
+         (("iz", "ic"), (z_size, c_size), ("blocks", 0, user_own, user_width))],
+        [item_factor, item_factor, id_piece, id_piece, user_factor],
         0,
     )
     ga = ga.reshape(-1, rank_size, item_width)

time: 61.3 us -> 58.4 us (0.953)
  local copies, waits for them, and re-layouts: 12.5 us -> 9.31 us
    transpose x2 -> x0, local copies, waits for them, and re-layouts: 1.49 us -> none  [the longest x1 1.48 us: on_device(): user_factor.reshape(rank_size, user_own, user_width).transpose(1, 0, 2)]
    unnamed x15 -> x13, local copies, waits for them, and re-layouts: 6.93 us -> 5.98 us
    slice x1 -> x0, local copies, waits for them, and re-layouts: 0.71 us -> none  [on_device(): blocks[half:]]
where the time goes in v12:
time: 58.4 us; the launch traced here: 57.8 us
  Pallas kernels  47.1 us (81%)
  local copies, waits for them, and re-layouts  9.31 us (16%)
  between operations  1.32 us (2%)
    pallas_call x1, Pallas kernels, fused_middle(): pl.pallas_call(_fused_kernel, out_shape=(jax.ShapeDtypeStruct(up_shape[1:...  29.6 us
    pallas_call x1, Pallas kernels, exchange(): pl.pallas_call(functools.partial(_exchange_kernel, plan), out_shape=tuple...  17.6 us
    unnamed x13, local copies, waits for them, and re-layouts  5.98 us

profile of v12, /device:TPU:1, one launch (start us, length us, event | category | flops | bytes accessed | tf_op | source)
XLA Modules:
  0.0 57.8 jit_solution(2641061425952452028)
XLA Ops:
  1.3 0.7 %scatter.6 = s32[8,128]{1,0:T(8,128)S(1)} pad(s32[1,4]{1,0:T(1,128)} %bitcast.14, s32[]{:T(128)} %constant.54.clone.1), padding=0_7x0_124 | pad | bytes 4116 | tf_op jit(solution)/shard_map/scatter | solution.py:394
  2.0 0.0 copy-start.4
  2.0 0.8 %copy.10 = f32[32,64]{0,1:T(8,128)S(1)} copy(f32[32,64]{1,0:T(8,128)} %w_ref.1) | data formatting | bytes 16384 | tf_op args[6]
  2.8 0.0 copy-done.4
  2.8 17.6 %shard_map.86 = (f32[4,4,64,128]{3,2,1,0:T(8,128)}, f32[4,4,64,128]{3,2,1,0:T(8,128)}, s32[4,8,128]{2,1,0:T(8,128)}, s32[4,8,128]{2,1,0:T(8,128)}, f32[8,2,64,128]{3,2,1,0:T(8,128)}) custom-call(f32[64,1024]{1,0:T(8,128)} %refs_1_.1, f32[64,1024]{1,0:T(8,128)} %refs_1_.1, s32[8,128]{1,0:T(8,128)} %copy-done.4, s32[8,128]{1,0:T(8,128)} %copy-done.4, ...), custom_call_target="tpu_custom_call" | custom-call | tf_op jit(solution)/shard_map/pallas_call | solution.py:107
  20.4 1.0 %slice_reduce_fusion = (s32[4]{0:T(128)S(1)}, s32[4]{0:T(128)S(1)}) fusion(s32[4,8,128]{2,1,0:T(8,128)} %get-tuple-element.32, s32[4,8,128]{2,1,0:T(8,128)} %get-tuple-element.31), kind=kLoop, calls=%fused_computation | loop fusion | bytes 64 | tf_op jit(solution)/shard_map/slice | solution.py:412
  21.3 0.8 %slice_reduce_fusion.1 = (s32[4,4]{1,0:T(4,128)S(1)}, s32[4,4]{1,0:T(4,128)S(1)}) fusion(s32[4,8,128]{2,1,0:T(8,128)} %get-tuple-element.32, s32[4,8,128]{2,1,0:T(8,128)} %get-tuple-element.31), kind=kLoop, calls=%fused_computation.1 | loop fusion | bytes 256 | tf_op jit(solution)/shard_map/slice | solution.py:412
  22.1 0.1 reshape_squeeze.10
  22.2 0.1 reshape_squeeze.9
  22.3 0.7 %concatenate.7.req_ref = s32[45]{0:T(128)S(1)} concatenate(s32[16]{0:T(128)S(1)} %reshape_squeeze.9, s32[4]{0:T(128)S(1)} %get-tuple-element.39, s32[16]{0:T(128)S(1)} %reshape_squeeze.10, s32[4]{0:T(128)S(1)} %get-tuple-element.38, s32[4]{0:T(128)} %bitcast.15, s32[1]{0:T(128)} %bitcast.8), dimensions={0} | concatenate | bytes 360 | tf_op jit(solution)/shard_map/concatenate | solution.py:411
  23.0 0.0 copy-start
  23.0 1.0 %copy-done = f32[4,4,64,128]{3,2,1,0:T(8,128)S(1)} copy-done((f32[4,4,64,128]{3,2,1,0:T(8,128)S(1)}, f32[4,4,64,128]{3,2,1,0:T(8,128)}, u32[]{:S(2)}) %copy-start) | copy-done | bytes 524312
  24.1 0.0 copy-start.1
  24.1 1.0 %copy-done.1 = f32[4,4,64,128]{3,2,1,0:T(8,128)S(1)} copy-done((f32[4,4,64,128]{3,2,1,0:T(8,128)S(1)}, f32[4,4,64,128]{3,2,1,0:T(8,128)}, u32[]{:S(2)}) %copy-start.1) | copy-done | bytes 524312
  25.1 0.0 copy-start.2
  25.1 1.0 %copy-done.2 = f32[8,2,64,128]{3,2,1,0:T(8,128)S(1)} copy-done((f32[8,2,64,128]{3,2,1,0:T(8,128)S(1)}, f32[8,2,64,128]{3,2,1,0:T(8,128)}, u32[]{:S(2)}) %copy-start.2) | copy-done | bytes 524312
  26.1 0.0 copy-start.3
  26.1 0.7 %copy-done.3 = f32[32,64]{1,0:T(8,128)S(1)} copy-done((f32[32,64]{1,0:T(8,128)S(1)}, f32[32,64]{1,0:T(8,128)}, u32[]{:S(2)}) %copy-start.3) | copy-done | bytes 8216
  26.9 29.6 %shard_map.87 = (f32[64,256]{1,0:T(8,128)S(1)}, f32[64,1024]{1,0:T(8,128)S(1)}) custom-call(s32[45]{0:T(128)S(1)} %concatenate.7.req_ref, f32[4,32,128,128]{3,2,1,0:T(8,128)} %bitcast.13, f32[16,64,128]{2,1,0:T(8,128)S(1)} %bitcast.9, f32[16,64,128]{2,1,0:T(8,128)S(1)} %bitcast.10, f32[16,64,128]{2,1,0:T(8,128)S(1)} %bitcast.11, f32[32,64]{1,0:T(8,128)S(1)} %copy-done.3, ...), custom_call_target="tpu_custom_call" | custom-call | flops 536870912 | bytes 8388608 | tf_op jit(solution)/shard_map/pallas_call | solution.py:312
  56.4 0.6 %copy.15 = f32[64,256]{1,0:T(8,128)} copy(f32[64,256]{1,0:T(8,128)S(1)} %get-tuple-element.42) | data formatting | bytes 131072
  57.0 0.7 %copy.16 = f32[64,1024]{1,0:T(8,128)} copy(f32[64,1024]{1,0:T(8,128)S(1)} %get-tuple-element.43) | data formatting | bytes 524288
  (1 shorter events, 0.0 us)
Async XLA Ops:
  2.0 0.8 %copy-start.4 = (s32[8,128]{1,0:T(8,128)}, s32[8,128]{1,0:T(8,128)S(1)}, u32[]{:S(2)}) copy-start(s32[8,128]{1,0:T(8,128)S(1)} %scatter.9.refs_2_.refs_3_) | copy-start | bytes 12292
  23.0 1.0 %copy-start = (f32[4,4,64,128]{3,2,1,0:T(8,128)S(1)}, f32[4,4,64,128]{3,2,1,0:T(8,128)}, u32[]{:S(2)}) copy-start(f32[4,4,64,128]{3,2,1,0:T(8,128)} %get-tuple-element.33) | copy-start | bytes 1572868
  24.1 1.0 %copy-start.1 = (f32[4,4,64,128]{3,2,1,0:T(8,128)S(1)}, f32[4,4,64,128]{3,2,1,0:T(8,128)}, u32[]{:S(2)}) copy-start(f32[4,4,64,128]{3,2,1,0:T(8,128)} %get-tuple-element.34) | copy-start | bytes 1572868
  25.1 1.0 %copy-start.2 = (f32[8,2,64,128]{3,2,1,0:T(8,128)S(1)}, f32[8,2,64,128]{3,2,1,0:T(8,128)}, u32[]{:S(2)}) copy-start(f32[8,2,64,128]{3,2,1,0:T(8,128)} %get-tuple-element.35) | copy-start | bytes 1572868
  26.1 0.7 %copy-start.3 = (f32[32,64]{1,0:T(8,128)S(1)}, f32[32,64]{1,0:T(8,128)}, u32[]{:S(2)}) copy-start(f32[32,64]{1,0:T(8,128)} %w_ref.1) | copy-start | bytes 24580

commit v13 on v12

--- a/solution.py
+++ b/solution.py
@@ -132,8 +132,8 @@
     iterm_ref[0] = jnp.dot(stacked, flat, precision=HIGHEST, preferred_element_type=jnp.float32)
 
 
-def _fused_kernel(req_ref, tiles_hbm, ga_hbm, gb_hbm, urows_hbm, w_ref, wt_ref, users_out, items_out,
-                  ga_ref, gb_ref, urows_ref, gsem, sel_x, sel_y, usel_ref, xbuf, xsem, land_sx, land_sy, iterm, land_tx, land_ty,
+def _fused_kernel(req_ref, tiles_hbm, ga_hbm, gb_hbm, urows_hbm, w_hbm, wt_hbm, users_hbm, items_hbm,
+                  ga_ref, gb_ref, urows_ref, w_ref, wt_ref, users_out, items_out, gsem, sel_x, sel_y, usel_ref, xbuf, xsem, land_sx, land_sy, iterm, land_tx, land_ty,
                   upart, land_up, part_a, land_a, part_b, land_b,
                   sx_s, sx_r, sy_s, sy_r, tx_s, tx_r, ty_s, ty_r, up_s, up_r, pa_s, pa_r, pb_s, pb_r):
     slots, weeks, users, items = xbuf.shape
@@ -176,7 +176,8 @@
         return {"iz": d // n_c, "ic": d % n_c}
 
     factor_loads = []
-    for i, (src, dst) in enumerate(((ga_hbm, ga_ref), (gb_hbm, gb_ref), (urows_hbm, urows_ref))):
+    for i, (src, dst) in enumerate(((ga_hbm, ga_ref), (gb_hbm, gb_ref), (urows_hbm, urows_ref), (w_hbm, w_ref),
+                                    (wt_hbm, wt_ref))):
         cp = pltpu.make_async_copy(src, dst, gsem.at[i])
         cp.start()
         factor_loads.append(cp)
@@ -300,6 +301,10 @@
     for k in range(1, n_x):
         total_b = total_b + land_b[lax.rem(me_x + k, n_x)]
     items_out[:, half * items:] = total_b
+    for i, (src, dst) in enumerate(((users_out, users_hbm), (items_out, items_hbm))):
+        cp = pltpu.make_async_copy(src, dst, gsem.at[5 + i])
+        cp.start()
+        cp.wait()
 
 
 def fused_middle(req, data, ga, gb, user_rows, week_factor, n_x, n_y, n_v, per_owner, half, collective_id):
@@ -315,13 +320,17 @@
             jax.ShapeDtypeStruct(up_shape[1:], f32),
             jax.ShapeDtypeStruct((rank, 2 * half * items), f32),
         ),
-        in_specs=[smem] + [pl.BlockSpec(memory_space=pl.ANY)] * 4 + [vmem, vmem],
-        out_specs=(vmem, vmem),
+        in_specs=[smem] + [pl.BlockSpec(memory_space=pl.ANY)] * 6,
+        out_specs=(pl.BlockSpec(memory_space=pl.ANY), pl.BlockSpec(memory_space=pl.ANY)),
         scratch_shapes=[
             pltpu.VMEM(ga.shape, f32),
             pltpu.VMEM(gb.shape, f32),
             pltpu.VMEM(user_rows.shape, f32),
-            pltpu.SemaphoreType.DMA((3,)),
+            pltpu.VMEM(week_factor.shape, f32),
+            pltpu.VMEM(week_factor.T.shape, f32),
+            pltpu.VMEM(up_shape[1:], f32),
+            pltpu.VMEM((rank, 2 * half * items), f32),
+            pltpu.SemaphoreType.DMA((7,)),
             pltpu.VMEM((n_x, slots, rank, items), f32),
             pltpu.VMEM((n_y, slots, rank, items), f32),
             pltpu.VMEM((slots, rank, users), f32),
@@ -341,7 +350,7 @@
         ] + [pltpu.SemaphoreType.DMA((n,)) for n in (n_x, n_x, n_y, n_y, n_x, n_x, n_y, n_y, n_v, n_v, n_y, n_y,
                                                      n_x, n_x)],
         compiler_params=pltpu.CompilerParams(
-            collective_id=collective_id, has_side_effects=True, vmem_limit_bytes=48 * 1024 * 1024),
+            collective_id=collective_id, has_side_effects=True),
         cost_estimate=pl.CostEstimate(
             flops=4 * slots * weeks * users * items * rank, transcendentals=0,
             bytes_accessed=4 * slots * weeks * users * items),

time: 58.4 us -> 58.7 us (level)
  Pallas kernels: 47.1 us -> 48.4 us
  local copies, waits for them, and re-layouts: 9.31 us -> 8.41 us
    unnamed x13 -> x5, local copies, waits for them, and re-layouts: 5.98 us -> 4.57 us
    pallas_call x1, Pallas kernels: 29.6 us -> 30.9 us  [fused_middle(): pl.pallas_call(_fused_kernel, out_shape=(jax.ShapeDtypeStruct(up_shape[1:...]
where the time goes in v13:
time: 58.7 us; the launch traced here: 58.1 us
  Pallas kernels  48.4 us (82%)
  local copies, waits for them, and re-layouts  8.41 us (14%)
  between operations  1.31 us (2%)
    pallas_call x1, Pallas kernels, fused_middle(): pl.pallas_call(_fused_kernel, out_shape=(jax.ShapeDtypeStruct(up_shape[1:...  30.9 us
    pallas_call x1, Pallas kernels, exchange(): pl.pallas_call(functools.partial(_exchange_kernel, plan), out_shape=tuple...  17.5 us
    unnamed x5, local copies, waits for them, and re-layouts  4.57 us
    concatenate x1, local copies, waits for them, and re-layouts, on_device(): jnp.concatenate([ids_x[:, 0, :slot_total].reshape(-1), ids_x[:, 1, 0], id...  1.25 us

profile of v13, /device:TPU:1, one launch (start us, length us, event | category | flops | bytes accessed | tf_op | source)
XLA Modules:
  0.0 58.1 jit_solution(15897738665394507087)
XLA Ops:
  1.3 0.7 %scatter.6 = s32[8,128]{1,0:T(8,128)S(1)} pad(s32[1,4]{1,0:T(1,128)} %bitcast.14, s32[]{:T(128)} %constant.54.clone.1), padding=0_7x0_124 | pad | bytes 4116 | tf_op jit(solution)/shard_map/scatter | solution.py:403
  2.0 0.0 copy-start
  2.0 1.4 %copy.10 = f32[32,64]{0,1:T(8,128)} copy(f32[32,64]{1,0:T(8,128)} %w_hbm.1) | data formatting | bytes 16384 | tf_op args[6]
  3.4 0.0 copy-done
  3.4 17.5 %shard_map.86 = (f32[4,4,64,128]{3,2,1,0:T(8,128)}, f32[4,4,64,128]{3,2,1,0:T(8,128)}, s32[4,8,128]{2,1,0:T(8,128)}, s32[4,8,128]{2,1,0:T(8,128)}, f32[8,2,64,128]{3,2,1,0:T(8,128)}) custom-call(f32[64,1024]{1,0:T(8,128)} %refs_1_.1, f32[64,1024]{1,0:T(8,128)} %refs_1_.1, s32[8,128]{1,0:T(8,128)} %copy-done, s32[8,128]{1,0:T(8,128)} %copy-done, ...), custom_call_target="tpu_custom_call" | custom-call | tf_op jit(solution)/shard_map/pallas_call | solution.py:107
  20.9 1.0 %slice_reduce_fusion = (s32[4]{0:T(128)S(1)}, s32[4]{0:T(128)S(1)}) fusion(s32[4,8,128]{2,1,0:T(8,128)} %get-tuple-element.32, s32[4,8,128]{2,1,0:T(8,128)} %get-tuple-element.31), kind=kLoop, calls=%fused_computation | loop fusion | bytes 64 | tf_op jit(solution)/shard_map/slice | solution.py:421
  21.9 0.8 %slice_reduce_fusion.1 = (s32[4,4]{1,0:T(4,128)S(1)}, s32[4,4]{1,0:T(4,128)S(1)}) fusion(s32[4,8,128]{2,1,0:T(8,128)} %get-tuple-element.32, s32[4,8,128]{2,1,0:T(8,128)} %get-tuple-element.31), kind=kLoop, calls=%fused_computation.1 | loop fusion | bytes 256 | tf_op jit(solution)/shard_map/slice | solution.py:421
  22.6 0.1 reshape_squeeze.10
  22.7 0.1 reshape_squeeze.9
  22.8 1.3 %concatenate.7.req_ref = s32[45]{0:T(128)} concatenate(s32[16]{0:T(128)S(1)} %reshape_squeeze.9, s32[4]{0:T(128)S(1)} %get-tuple-element.39, s32[16]{0:T(128)S(1)} %reshape_squeeze.10, s32[4]{0:T(128)S(1)} %get-tuple-element.38, s32[4]{0:T(128)} %bitcast.15, s32[1]{0:T(128)} %bitcast.8), dimensions={0} | concatenate | bytes 360 | tf_op jit(solution)/shard_map/concatenate | solution.py:420
  24.1 30.9 %shard_map.87 = (f32[64,256]{1,0:T(8,128)}, f32[64,1024]{1,0:T(8,128)}) custom-call(s32[45]{0:T(128)} %concatenate.7.req_ref, f32[4,32,128,128]{3,2,1,0:T(8,128)} %bitcast.9, f32[16,64,128]{2,1,0:T(8,128)} %bitcast.10, f32[16,64,128]{2,1,0:T(8,128)} %bitcast.11, f32[16,64,128]{2,1,0:T(8,128)} %bitcast.12, f32[32,64]{1,0:T(8,128)} %w_hbm.1, f32[64,32]{1,0:T(8,128)} %bitcast.13), custom_call_target="tpu_custom_call" | custom-call | flops 536870912 | bytes 8388608 | tf_op jit(solution)/shard_map/pallas_call | solution.py:317
  55.0 1.5 %copy.15 = f32[64,256]{1,0:T(8,128)} copy(f32[64,256]{1,0:T(8,128)} %get-tuple-element.42) | data formatting | bytes 131072
  56.5 1.7 %copy.16 = f32[64,1024]{1,0:T(8,128)} copy(f32[64,1024]{1,0:T(8,128)} %get-tuple-element.43) | data formatting | bytes 524288
  (1 shorter events, 0.0 us)
Async XLA Ops:
  2.0 1.4 %copy-start = (s32[8,128]{1,0:T(8,128)}, s32[8,128]{1,0:T(8,128)S(1)}, u32[]{:S(2)}) copy-start(s32[8,128]{1,0:T(8,128)S(1)} %scatter.9.refs_2_.refs_3_) | copy-start | bytes 12292

commit v14 on v12

--- a/solution.py
+++ b/solution.py
@@ -132,7 +132,7 @@
     iterm_ref[0] = jnp.dot(stacked, flat, precision=HIGHEST, preferred_element_type=jnp.float32)
 
 
-def _fused_kernel(req_ref, tiles_hbm, ga_hbm, gb_hbm, urows_hbm, w_ref, wt_ref, users_out, items_out,
+def _fused_kernel(idsx_ref, idsy_ref, req_ref, tiles_hbm, ga_hbm, gb_hbm, urows_hbm, w_ref, wt_ref, users_out, items_out,
                   ga_ref, gb_ref, urows_ref, gsem, sel_x, sel_y, usel_ref, xbuf, xsem, land_sx, land_sy, iterm, land_tx, land_ty,
                   upart, land_up, part_a, land_a, part_b, land_b,
                   sx_s, sx_r, sy_s, sy_r, tx_s, tx_r, ty_s, ty_r, up_s, up_r, pa_s, pa_r, pb_s, pb_r):
@@ -150,20 +150,20 @@
     one = jnp.float32(1.0)
     zero = jnp.float32(0.0)
 
-    def request(q, base, cnt_base):
-        j = req_ref[base + q]
-        live = (q % slots) < req_ref[cnt_base + q // slots]
+    def request(ids_ref, q):
+        j = ids_ref[q // slots, 0, q % slots]
+        live = (q % slots) < ids_ref[q // slots, 1, 0]
         return j // group_blocks, (j // (2 * half)) % n_y, j % (2 * half), live
 
     path_a, path_b = [], []
     for q in range(n_q):
-        ox, oy, l, live = request(q, 0, n_q)
+        ox, oy, l, live = request(idsx_ref, q)
         take = (ox == me_x) & (l < half) & live
         path_a.append((take, oy, l, jnp.where(take, oy * half + l, 0)))
-        ox, oy, l, live = request(q, n_q + n_x, 2 * n_q + n_x)
+        ox, oy, l, live = request(idsy_ref, q)
         take = (oy == me_y) & (l >= half) & live
         path_b.append((take, ox, l - half, jnp.where(take, ox * half + l - half, 0)))
-    own_at = 2 * n_q + n_x + n_y
+    own_at = 0
     own_live = [s < req_ref[own_at + slots] for s in range(slots)]
 
     def xpeer(d):
@@ -302,7 +302,7 @@
     items_out[:, half * items:] = total_b
 
 
-def fused_middle(req, data, ga, gb, user_rows, week_factor, n_x, n_y, n_v, per_owner, half, collective_id):
+def fused_middle(ids_x, ids_y, req, data, ga, gb, user_rows, week_factor, n_x, n_y, n_v, per_owner, half, collective_id):
     slots, weeks, users, items = data.shape
     rank = week_factor.shape[1]
     vmem = pl.BlockSpec(memory_space=pltpu.VMEM)
@@ -315,7 +315,7 @@
             jax.ShapeDtypeStruct(up_shape[1:], f32),
             jax.ShapeDtypeStruct((rank, 2 * half * items), f32),
         ),
-        in_specs=[smem] + [pl.BlockSpec(memory_space=pl.ANY)] * 4 + [vmem, vmem],
+        in_specs=[smem, smem, smem] + [pl.BlockSpec(memory_space=pl.ANY)] * 4 + [vmem, vmem],
         out_specs=(vmem, vmem),
         scratch_shapes=[
             pltpu.VMEM(ga.shape, f32),
@@ -345,7 +345,7 @@
         cost_estimate=pl.CostEstimate(
             flops=4 * slots * weeks * users * items * rank, transcendentals=0,
             bytes_accessed=4 * slots * weeks * users * items),
-    )(req, data, ga, gb, user_rows, week_factor, week_factor.T)
+    )(ids_x, ids_y, req, data, ga, gb, user_rows, week_factor, week_factor.T)
 
 
 def slot_terms(data, item_sel, user_sel, week_factor):
@@ -408,11 +408,9 @@
     me_y = lax.axis_index("uy")
 
     n_v = z_size * c_size
-    req = jnp.concatenate([
-        ids_x[:, 0, :slot_total].reshape(-1), ids_x[:, 1, 0], ids_y[:, 0, :slot_total].reshape(-1), ids_y[:, 1, 0],
-        user_ids, counts[0, 0].reshape(1)]).astype(jnp.int32)
+    req = jnp.concatenate([user_ids, counts[0, 0].reshape(1)]).astype(jnp.int32)
     m_users, m_items = fused_middle(
-        req, tiles[0, 0], ga, gb, user_rows, week_factor, x_size, y_size, n_v, user_own, half, 1)
+        ids_x, ids_y, req, tiles[0, 0], ga, gb, user_rows, week_factor, x_size, y_size, n_v, user_own, half, 1)
     return (m_users, m_items)
 
 

time: 58.4 us -> 58.3 us (level)
  local copies, waits for them, and re-layouts: 9.31 us -> 8.1 us
  other arithmetic: 0 us -> 0.73 us
    slice x2 -> x0, local copies, waits for them, and re-layouts: 1.73 us -> none  [the longest x1 0.97 us: on_device(): ids_y[:, 1, 0]]
    unnamed x13 -> x17, local copies, waits for them, and re-layouts: 5.98 us -> 7.41 us
    concatenate x1 -> x0, local copies, waits for them, and re-layouts: 0.73 us -> none  [on_device(): jnp.concatenate([ids_x[:, 0, :slot_total].reshape(-1), ids_x[:, 1, 0], id...]
    concatenate x0 -> x1, other arithmetic: none -> 0.73 us  [on_device(): req = jnp.concatenate([user_ids, counts[0, 0].reshape(1)]).astype(jnp.int32)]
where the time goes in v14:
time: 58.3 us; the launch traced here: 57.8 us
  Pallas kernels  47.6 us (82%)
  local copies, waits for them, and re-layouts  8.1 us (14%)
  between operations  1.33 us (2%)
  other arithmetic  0.73 us (1%)
    pallas_call x1, Pallas kernels, fused_middle(): pl.pallas_call(_fused_kernel, out_shape=(jax.ShapeDtypeStruct(up_shape[1:...  30.1 us
    pallas_call x1, Pallas kernels, exchange(): pl.pallas_call(functools.partial(_exchange_kernel, plan), out_shape=tuple...  17.6 us
    unnamed x17, local copies, waits for them, and re-layouts  7.41 us

profile of v14, /device:TPU:1, one launch (start us, length us, event | category | flops | bytes accessed | tf_op | source)
XLA Modules:
  0.0 57.8 jit_solution(17782685249688067028)
XLA Ops:
  1.3 0.7 %pad_add_fusion.req_ref = s32[5]{0:T(128)S(1)} fusion(s32[1]{0:T(128)} %bitcast.8, s32[4]{0:T(128)} %bitcast.15), kind=kLoop, calls=%fused_computation | loop fusion | flops 5 | bytes 40 | tf_op jit(solution)/shard_map/concatenate | solution.py:411
  2.0 0.7 %scatter.6 = s32[8,128]{1,0:T(8,128)S(1)} pad(s32[1,4]{1,0:T(1,128)} %bitcast.14, s32[]{:T(128)} %constant.54.clone.1), padding=0_7x0_124 | pad | bytes 4116 | tf_op jit(solution)/shard_map/scatter | solution.py:394
  2.7 0.0 copy-start.6
  2.7 0.8 %copy.9 = f32[32,64]{0,1:T(8,128)S(1)} copy(f32[32,64]{1,0:T(8,128)} %w_ref.1) | data formatting | bytes 16384 | tf_op args[6]
  3.5 0.0 copy-done.6
  3.5 17.6 %shard_map.86 = (f32[4,4,64,128]{3,2,1,0:T(8,128)}, f32[4,4,64,128]{3,2,1,0:T(8,128)}, s32[4,8,128]{2,1,0:T(8,128)}, s32[4,8,128]{2,1,0:T(8,128)}, f32[8,2,64,128]{3,2,1,0:T(8,128)}) custom-call(f32[64,1024]{1,0:T(8,128)} %refs_1_.1, f32[64,1024]{1,0:T(8,128)} %refs_1_.1, s32[8,128]{1,0:T(8,128)} %copy-done.6, s32[8,128]{1,0:T(8,128)} %copy-done.6, ...), custom_call_target="tpu_custom_call" | custom-call | tf_op jit(solution)/shard_map/pallas_call | solution.py:107
  21.1 0.0 copy-start
  21.1 1.0 %copy-done = f32[4,4,64,128]{3,2,1,0:T(8,128)S(1)} copy-done((f32[4,4,64,128]{3,2,1,0:T(8,128)S(1)}, f32[4,4,64,128]{3,2,1,0:T(8,128)}, u32[]{:S(2)}) %copy-start) | copy-done | bytes 524312
  22.1 0.0 copy-start.1
  22.1 1.0 %copy-done.1 = f32[4,4,64,128]{3,2,1,0:T(8,128)S(1)} copy-done((f32[4,4,64,128]{3,2,1,0:T(8,128)S(1)}, f32[4,4,64,128]{3,2,1,0:T(8,128)}, u32[]{:S(2)}) %copy-start.1) | copy-done | bytes 524312
  23.2 0.0 copy-start.2
  23.2 1.0 %copy-done.2 = f32[8,2,64,128]{3,2,1,0:T(8,128)S(1)} copy-done((f32[8,2,64,128]{3,2,1,0:T(8,128)S(1)}, f32[8,2,64,128]{3,2,1,0:T(8,128)}, u32[]{:S(2)}) %copy-start.2) | copy-done | bytes 524312
  24.2 0.0 copy-start.3
  24.2 0.7 %copy-done.3 = f32[32,64]{1,0:T(8,128)S(1)} copy-done((f32[32,64]{1,0:T(8,128)S(1)}, f32[32,64]{1,0:T(8,128)}, u32[]{:S(2)}) %copy-start.3) | copy-done | bytes 8216
  24.9 0.0 copy-start.4
  24.9 0.7 %copy-done.4 = s32[4,8,128]{2,1,0:T(8,128)S(1)} copy-done((s32[4,8,128]{2,1,0:T(8,128)S(1)}, s32[4,8,128]{2,1,0:T(8,128)}, u32[]{:S(2)}) %copy-start.4) | copy-done | bytes 16408
  25.6 0.0 copy-start.5
  25.6 0.7 %copy-done.5 = s32[4,8,128]{2,1,0:T(8,128)S(1)} copy-done((s32[4,8,128]{2,1,0:T(8,128)S(1)}, s32[4,8,128]{2,1,0:T(8,128)}, u32[]{:S(2)}) %copy-start.5) | copy-done | bytes 16408
  26.4 30.1 %shard_map.87 = (f32[64,256]{1,0:T(8,128)S(1)}, f32[64,1024]{1,0:T(8,128)S(1)}) custom-call(s32[4,8,128]{2,1,0:T(8,128)S(1)} %copy-done.4, s32[4,8,128]{2,1,0:T(8,128)S(1)} %copy-done.5, s32[5]{0:T(128)S(1)} %pad_add_fusion.req_ref, f32[4,32,128,128]{3,2,1,0:T(8,128)} %bitcast.13, f32[16,64,128]{2,1,0:T(8,128)S(1)} %bitcast.9, f32[16,64,128]{2,1,0:T(8,128)S(1)} %bitcast.10, ...), custom_call_target="tpu_custom_call" | custom-call | flops 536870912 | bytes 8388608 | tf_op jit(solution)/shard_map/pallas_call | solution.py:312
  56.5 0.6 %copy.14 = f32[64,256]{1,0:T(8,128)} copy(f32[64,256]{1,0:T(8,128)S(1)} %get-tuple-element.38) | data formatting | bytes 131072
  57.1 0.7 %copy.15 = f32[64,1024]{1,0:T(8,128)} copy(f32[64,1024]{1,0:T(8,128)S(1)} %get-tuple-element.39) | data formatting | bytes 524288
  (1 shorter events, 0.0 us)
Async XLA Ops:
  2.7 0.8 %copy-start.6 = (s32[8,128]{1,0:T(8,128)}, s32[8,128]{1,0:T(8,128)S(1)}, u32[]{:S(2)}) copy-start(s32[8,128]{1,0:T(8,128)S(1)} %scatter.9.refs_2_.refs_3_) | copy-start | bytes 12292
  21.1 1.0 %copy-start = (f32[4,4,64,128]{3,2,1,0:T(8,128)S(1)}, f32[4,4,64,128]{3,2,1,0:T(8,128)}, u32[]{:S(2)}) copy-start(f32[4,4,64,128]{3,2,1,0:T(8,128)} %get-tuple-element.33) | copy-start | bytes 1572868
  22.1 1.0 %copy-start.1 = (f32[4,4,64,128]{3,2,1,0:T(8,128)S(1)}, f32[4,4,64,128]{3,2,1,0:T(8,128)}, u32[]{:S(2)}) copy-start(f32[4,4,64,128]{3,2,1,0:T(8,128)} %get-tuple-element.34) | copy-start | bytes 1572868
  23.2 1.0 %copy-start.2 = (f32[8,2,64,128]{3,2,1,0:T(8,128)S(1)}, f32[8,2,64,128]{3,2,1,0:T(8,128)}, u32[]{:S(2)}) copy-start(f32[8,2,64,128]{3,2,1,0:T(8,128)} %get-tuple-element.35) | copy-start | bytes 1572868
  24.2 0.7 %copy-start.3 = (f32[32,64]{1,0:T(8,128)S(1)}, f32[32,64]{1,0:T(8,128)}, u32[]{:S(2)}) copy-start(f32[32,64]{1,0:T(8,128)} %w_ref.1) | copy-start | bytes 24580
  24.9 0.7 %copy-start.4 = (s32[4,8,128]{2,1,0:T(8,128)S(1)}, s32[4,8,128]{2,1,0:T(8,128)}, u32[]{:S(2)}) copy-start(s32[4,8,128]{2,1,0:T(8,128)} %get-tuple-element.31.idsx_ref) | copy-start | bytes 49156
  25.6 0.7 %copy-start.5 = (s32[4,8,128]{2,1,0:T(8,128)S(1)}, s32[4,8,128]{2,1,0:T(8,128)}, u32[]{:S(2)}) copy-start(s32[4,8,128]{2,1,0:T(8,128)} %get-tuple-element.32.idsy_ref) | copy-start | bytes 49156

commit v15 on v12

--- a/solution.py
+++ b/solution.py
@@ -265,7 +265,9 @@
     up_copies = send_rows(upart, land_up, up_s, up_r, n_v, me_v, vpeer, False)
 
     finish(tx_copies, land_tx, tx_s, tx_r, n_x, me_x, xpeer)
-    for y in range(n_y):
+    finish(ty_copies, land_ty, ty_s, ty_r, n_y, me_y, ypeer)
+
+    def build_a(y):
         for l in range(half):
             acc = None
             for q in range(n_q):
@@ -273,9 +275,8 @@
                 term = land_tx[q // slots, q % slots] * jnp.where(take & (oy == y) & (lq == l), one, zero)
                 acc = term if acc is None else acc + term
             part_a[y, :, l * items:(l + 1) * items] = acc
-    pa_copies = send_rows(part_a, land_a, pa_s, pa_r, n_y, me_y, ypeer, False)
-    finish(ty_copies, land_ty, ty_s, ty_r, n_y, me_y, ypeer)
-    for x in range(n_x):
+
+    def build_b(x):
         for l in range(half):
             acc = None
             for q in range(n_q):
@@ -283,7 +284,25 @@
                 term = land_ty[q // slots, q % slots] * jnp.where(take & (ox == x) & (lq == l), one, zero)
                 acc = term if acc is None else acc + term
             part_b[x, :, l * items:(l + 1) * items] = acc
-    pb_copies = send_rows(part_b, land_b, pb_s, pb_r, n_x, me_x, xpeer, False)
+
+    def send_one(buf, land, ssem, rsem, n, me, peer, k):
+        d = lax.rem(me + k, n)
+        cp = pltpu.make_async_remote_copy(
+            src_ref=buf.at[d], dst_ref=land.at[me], send_sem=ssem.at[k], recv_sem=rsem.at[k],
+            device_id=peer(d), device_id_type=MESH_IDS)
+        cp.start()
+        return (k, cp)
+
+    pa_copies, pb_copies = [], []
+    for k in range(1, max(n_x, n_y)):
+        if k < n_y:
+            build_a(lax.rem(me_y + k, n_y))
+            pa_copies.append(send_one(part_a, land_a, pa_s, pa_r, n_y, me_y, ypeer, k))
+        if k < n_x:
+            build_b(lax.rem(me_x + k, n_x))
+            pb_copies.append(send_one(part_b, land_b, pb_s, pb_r, n_x, me_x, xpeer, k))
+    build_a(me_y)
+    build_b(me_x)
 
     finish(up_copies, land_up, up_s, up_r, n_v, me_v, vpeer)
     total_u = upart[me_v]

time: 58.4 us -> 58.3 us (level)
  no operation moved by 1% of the time
where the time goes in v15:
time: 58.3 us; the launch traced here: 57.6 us
  Pallas kernels  47 us (81%)
  local copies, waits for them, and re-layouts  9.31 us (16%)
  between operations  1.32 us (2%)
    pallas_call x1, Pallas kernels, fused_middle(): pl.pallas_call(_fused_kernel, out_shape=(jax.ShapeDtypeStruct(up_shape[1:...  29.4 us
    pallas_call x1, Pallas kernels, exchange(): pl.pallas_call(functools.partial(_exchange_kernel, plan), out_shape=tuple...  17.6 us
    unnamed x13, local copies, waits for them, and re-layouts  5.98 us

profile of v15, /device:TPU:1, one launch (start us, length us, event | category | flops | bytes accessed | tf_op | source)
XLA Modules:
  0.0 57.6 jit_solution(4703019620880964498)
XLA Ops:
  1.3 0.7 %scatter.6 = s32[8,128]{1,0:T(8,128)S(1)} pad(s32[1,4]{1,0:T(1,128)} %bitcast.14, s32[]{:T(128)} %constant.54.clone.1), padding=0_7x0_124 | pad | bytes 4116 | tf_op jit(solution)/shard_map/scatter | solution.py:413
  2.0 0.0 copy-start.4
  2.0 0.8 %copy.10 = f32[32,64]{0,1:T(8,128)S(1)} copy(f32[32,64]{1,0:T(8,128)} %w_ref.1) | data formatting | bytes 16384 | tf_op args[6]
  2.8 0.0 copy-done.4
  2.8 17.6 %shard_map.86 = (f32[4,4,64,128]{3,2,1,0:T(8,128)}, f32[4,4,64,128]{3,2,1,0:T(8,128)}, s32[4,8,128]{2,1,0:T(8,128)}, s32[4,8,128]{2,1,0:T(8,128)}, f32[8,2,64,128]{3,2,1,0:T(8,128)}) custom-call(f32[64,1024]{1,0:T(8,128)} %refs_1_.1, f32[64,1024]{1,0:T(8,128)} %refs_1_.1, s32[8,128]{1,0:T(8,128)} %copy-done.4, s32[8,128]{1,0:T(8,128)} %copy-done.4, ...), custom_call_target="tpu_custom_call" | custom-call | tf_op jit(solution)/shard_map/pallas_call | solution.py:107
  20.4 1.0 %slice_reduce_fusion = (s32[4]{0:T(128)S(1)}, s32[4]{0:T(128)S(1)}) fusion(s32[4,8,128]{2,1,0:T(8,128)} %get-tuple-element.32, s32[4,8,128]{2,1,0:T(8,128)} %get-tuple-element.31), kind=kLoop, calls=%fused_computation | loop fusion | bytes 64 | tf_op jit(solution)/shard_map/slice | solution.py:431
  21.3 0.8 %slice_reduce_fusion.1 = (s32[4,4]{1,0:T(4,128)S(1)}, s32[4,4]{1,0:T(4,128)S(1)}) fusion(s32[4,8,128]{2,1,0:T(8,128)} %get-tuple-element.32, s32[4,8,128]{2,1,0:T(8,128)} %get-tuple-element.31), kind=kLoop, calls=%fused_computation.1 | loop fusion | bytes 256 | tf_op jit(solution)/shard_map/slice | solution.py:431
  22.1 0.1 reshape_squeeze.10
  22.2 0.1 reshape_squeeze.9
  22.3 0.7 %concatenate.7.req_ref = s32[45]{0:T(128)S(1)} concatenate(s32[16]{0:T(128)S(1)} %reshape_squeeze.9, s32[4]{0:T(128)S(1)} %get-tuple-element.39, s32[16]{0:T(128)S(1)} %reshape_squeeze.10, s32[4]{0:T(128)S(1)} %get-tuple-element.38, s32[4]{0:T(128)} %bitcast.15, s32[1]{0:T(128)} %bitcast.8), dimensions={0} | concatenate | bytes 360 | tf_op jit(solution)/shard_map/concatenate | solution.py:430
  23.0 0.0 copy-start
  23.0 1.0 %copy-done = f32[4,4,64,128]{3,2,1,0:T(8,128)S(1)} copy-done((f32[4,4,64,128]{3,2,1,0:T(8,128)S(1)}, f32[4,4,64,128]{3,2,1,0:T(8,128)}, u32[]{:S(2)}) %copy-start) | copy-done | bytes 524312
  24.1 0.0 copy-start.1
  24.1 1.0 %copy-done.1 = f32[4,4,64,128]{3,2,1,0:T(8,128)S(1)} copy-done((f32[4,4,64,128]{3,2,1,0:T(8,128)S(1)}, f32[4,4,64,128]{3,2,1,0:T(8,128)}, u32[]{:S(2)}) %copy-start.1) | copy-done | bytes 524312
  25.1 0.0 copy-start.2
  25.1 1.0 %copy-done.2 = f32[8,2,64,128]{3,2,1,0:T(8,128)S(1)} copy-done((f32[8,2,64,128]{3,2,1,0:T(8,128)S(1)}, f32[8,2,64,128]{3,2,1,0:T(8,128)}, u32[]{:S(2)}) %copy-start.2) | copy-done | bytes 524312
  26.1 0.0 copy-start.3
  26.1 0.7 %copy-done.3 = f32[32,64]{1,0:T(8,128)S(1)} copy-done((f32[32,64]{1,0:T(8,128)S(1)}, f32[32,64]{1,0:T(8,128)}, u32[]{:S(2)}) %copy-start.3) | copy-done | bytes 8216
  26.9 29.4 %shard_map.87 = (f32[64,256]{1,0:T(8,128)S(1)}, f32[64,1024]{1,0:T(8,128)S(1)}) custom-call(s32[45]{0:T(128)S(1)} %concatenate.7.req_ref, f32[4,32,128,128]{3,2,1,0:T(8,128)} %bitcast.13, f32[16,64,128]{2,1,0:T(8,128)S(1)} %bitcast.9, f32[16,64,128]{2,1,0:T(8,128)S(1)} %bitcast.10, f32[16,64,128]{2,1,0:T(8,128)S(1)} %bitcast.11, f32[32,64]{1,0:T(8,128)S(1)} %copy-done.3, ...), custom_call_target="tpu_custom_call" | custom-call | flops 536870912 | bytes 8388608 | tf_op jit(solution)/shard_map/pallas_call | solution.py:331
  56.3 0.6 %copy.15 = f32[64,256]{1,0:T(8,128)} copy(f32[64,256]{1,0:T(8,128)S(1)} %get-tuple-element.42) | data formatting | bytes 131072
  56.9 0.7 %copy.16 = f32[64,1024]{1,0:T(8,128)} copy(f32[64,1024]{1,0:T(8,128)S(1)} %get-tuple-element.43) | data formatting | bytes 524288
  (1 shorter events, 0.0 us)
Async XLA Ops:
  2.0 0.8 %copy-start.4 = (s32[8,128]{1,0:T(8,128)}, s32[8,128]{1,0:T(8,128)S(1)}, u32[]{:S(2)}) copy-start(s32[8,128]{1,0:T(8,128)S(1)} %scatter.9.refs_2_.refs_3_) | copy-start | bytes 12292
  23.0 1.0 %copy-start = (f32[4,4,64,128]{3,2,1,0:T(8,128)S(1)}, f32[4,4,64,128]{3,2,1,0:T(8,128)}, u32[]{:S(2)}) copy-start(f32[4,4,64,128]{3,2,1,0:T(8,128)} %get-tuple-element.33) | copy-start | bytes 1572868
  24.1 1.0 %copy-start.1 = (f32[4,4,64,128]{3,2,1,0:T(8,128)S(1)}, f32[4,4,64,128]{3,2,1,0:T(8,128)}, u32[]{:S(2)}) copy-start(f32[4,4,64,128]{3,2,1,0:T(8,128)} %get-tuple-element.34) | copy-start | bytes 1572868
  25.1 1.0 %copy-start.2 = (f32[8,2,64,128]{3,2,1,0:T(8,128)S(1)}, f32[8,2,64,128]{3,2,1,0:T(8,128)}, u32[]{:S(2)}) copy-start(f32[8,2,64,128]{3,2,1,0:T(8,128)} %get-tuple-element.35) | copy-start | bytes 1572868
  26.1 0.7 %copy-start.3 = (f32[32,64]{1,0:T(8,128)S(1)}, f32[32,64]{1,0:T(8,128)}, u32[]{:S(2)}) copy-start(f32[32,64]{1,0:T(8,128)} %w_ref.1) | copy-start | bytes 24580

commit v16 on v12

--- a/solution.py
+++ b/solution.py
@@ -30,6 +30,7 @@
     ne = len(plan)
     ins, outs = refs[:ne], refs[ne:2 * ne]
     lands, sends, recvs = refs[2 * ne:3 * ne], refs[3 * ne:4 * ne], refs[4 * ne:5 * ne]
+    fwd = refs[5 * ne:6 * ne]
     barrier = pltpu.get_barrier_semaphore()
     total = 0
     for axes, sizes, mode in plan:
@@ -43,12 +44,16 @@
         total += n - 1
     pl.semaphore_wait(barrier, total)
     copies = []
+    relays = []
     for e, (axes, sizes, mode) in enumerate(plan):
         n = 1
         for s in sizes:
             n *= s
         me = _group_me(axes, sizes)
+        relay = n == 4
         for k in range(1, n):
+            if relay and k == 2:
+                continue
             d = lax.rem(me + k, n)
             if isinstance(mode, tuple):
                 first, count = mode[1], mode[2]
@@ -68,12 +73,38 @@
                     device_id=_peer(axes, sizes, d), device_id_type=MESH_IDS)
                 cp.start()
             copies.append((e, n, me, k, cp))
+        if relay:
+            relays.append(e)
     for e, n, me, k, cp in copies:
         cp.wait_send()
         src = lax.rem(me + n - k, n)
         pltpu.make_async_remote_copy(
             src_ref=lands[e].at[src], dst_ref=lands[e].at[src], send_sem=sends[e].at[k], recv_sem=recvs[e].at[k],
             device_id=_peer(plan[e][0], plan[e][1], src), device_id_type=MESH_IDS).wait_recv()
+    forwards = []
+    for e in relays:
+        axes, sizes, mode = plan[e]
+        me = _group_me(axes, sizes)
+        rows = lands[e].shape[1]
+        cut = rows // 2
+        for k, part in ((1, (0, cut)), (3, (cut, rows))):
+            origin = lax.rem(me + 4 - k, 4)
+            d = lax.rem(me + k, 4)
+            cp = pltpu.make_async_remote_copy(
+                src_ref=lands[e].at[origin, part[0]:part[1]], dst_ref=lands[e].at[origin, part[0]:part[1]],
+                send_sem=fwd[e].at[k], recv_sem=recvs[e].at[2],
+                device_id=_peer(axes, sizes, d), device_id_type=MESH_IDS)
+            cp.start()
+            forwards.append(cp)
+    for cp in forwards:
+        cp.wait_send()
+    for e in relays:
+        axes, sizes, mode = plan[e]
+        me = _group_me(axes, sizes)
+        src = lax.rem(me + 2, 4)
+        pltpu.make_async_remote_copy(
+            src_ref=lands[e].at[src], dst_ref=lands[e].at[src], send_sem=fwd[e].at[0], recv_sem=recvs[e].at[2],
+            device_id=_peer(axes, sizes, src), device_id_type=MESH_IDS).wait_recv()
     for e, (axes, sizes, mode) in enumerate(plan):
         n = 1
         for s in sizes:
@@ -109,7 +140,7 @@
         out_shape=tuple(out_shapes),
         in_specs=[pl.BlockSpec(memory_space=pltpu.VMEM)] * len(plan),
         out_specs=tuple(pl.BlockSpec(memory_space=pltpu.VMEM) for _ in plan),
-        scratch_shapes=scratch_lands + sems_s + sems_r,
+        scratch_shapes=scratch_lands + sems_s + sems_r + [pltpu.SemaphoreType.DMA((4,)) for _ in plan],
         compiler_params=pltpu.CompilerParams(collective_id=collective_id, has_side_effects=True),
     )(*arrays)
 

time: 58.4 us -> 62 us (1.062)
  Pallas kernels: 47.1 us -> 50.7 us
    pallas_call x1, Pallas kernels: 17.6 us -> 22.3 us  [exchange(): pl.pallas_call(functools.partial(_exchange_kernel, plan), out_shape=tuple...]
    pallas_call x1, Pallas kernels: 29.6 us -> 28.4 us  [fused_middle(): pl.pallas_call(_fused_kernel, out_shape=(jax.ShapeDtypeStruct(up_shape[1:...]
where the time goes in v16:
time: 62 us; the launch traced here: 61.3 us
  Pallas kernels  50.7 us (82%)
  local copies, waits for them, and re-layouts  9.31 us (15%)
  between operations  1.32 us (2%)
    pallas_call x1, Pallas kernels, fused_middle(): pl.pallas_call(_fused_kernel, out_shape=(jax.ShapeDtypeStruct(up_shape[1:...  28.4 us
    pallas_call x1, Pallas kernels, exchange(): pl.pallas_call(functools.partial(_exchange_kernel, plan), out_shape=tuple...  22.3 us
    unnamed x13, local copies, waits for them, and re-layouts  5.98 us

profile of v16, /device:TPU:1, one launch (start us, length us, event | category | flops | bytes accessed | tf_op | source)
XLA Modules:
  0.0 61.3 jit_solution(8812239092330031710)
XLA Ops:
  1.3 0.7 %scatter.6 = s32[8,128]{1,0:T(8,128)S(1)} pad(s32[1,4]{1,0:T(1,128)} %bitcast.14, s32[]{:T(128)} %constant.54.clone.1), padding=0_7x0_124 | pad | bytes 4116 | tf_op jit(solution)/shard_map/scatter | solution.py:425
  2.0 0.0 copy-start.4
  2.0 0.8 %copy.10 = f32[32,64]{0,1:T(8,128)S(1)} copy(f32[32,64]{1,0:T(8,128)} %w_ref.1) | data formatting | bytes 16384 | tf_op args[6]
  2.8 0.0 copy-done.4
  2.8 22.3 %shard_map.86 = (f32[4,4,64,128]{3,2,1,0:T(8,128)}, f32[4,4,64,128]{3,2,1,0:T(8,128)}, s32[4,8,128]{2,1,0:T(8,128)}, s32[4,8,128]{2,1,0:T(8,128)}, f32[8,2,64,128]{3,2,1,0:T(8,128)}) custom-call(f32[64,1024]{1,0:T(8,128)} %refs_1_.1, f32[64,1024]{1,0:T(8,128)} %refs_1_.1, s32[8,128]{1,0:T(8,128)} %copy-done.4, s32[8,128]{1,0:T(8,128)} %copy-done.4, ...), custom_call_target="tpu_custom_call" | custom-call | tf_op jit(solution)/shard_map/pallas_call | solution.py:138
  25.2 1.0 %slice_reduce_fusion = (s32[4]{0:T(128)S(1)}, s32[4]{0:T(128)S(1)}) fusion(s32[4,8,128]{2,1,0:T(8,128)} %get-tuple-element.32, s32[4,8,128]{2,1,0:T(8,128)} %get-tuple-element.31), kind=kLoop, calls=%fused_computation | loop fusion | bytes 64 | tf_op jit(solution)/shard_map/slice | solution.py:443
  26.1 0.8 %slice_reduce_fusion.1 = (s32[4,4]{1,0:T(4,128)S(1)}, s32[4,4]{1,0:T(4,128)S(1)}) fusion(s32[4,8,128]{2,1,0:T(8,128)} %get-tuple-element.32, s32[4,8,128]{2,1,0:T(8,128)} %get-tuple-element.31), kind=kLoop, calls=%fused_computation.1 | loop fusion | bytes 256 | tf_op jit(solution)/shard_map/slice | solution.py:443
  26.9 0.1 reshape_squeeze.10
  27.0 0.1 reshape_squeeze.9
  27.1 0.7 %concatenate.7.req_ref = s32[45]{0:T(128)S(1)} concatenate(s32[16]{0:T(128)S(1)} %reshape_squeeze.9, s32[4]{0:T(128)S(1)} %get-tuple-element.39, s32[16]{0:T(128)S(1)} %reshape_squeeze.10, s32[4]{0:T(128)S(1)} %get-tuple-element.38, s32[4]{0:T(128)} %bitcast.15, s32[1]{0:T(128)} %bitcast.8), dimensions={0} | concatenate | bytes 360 | tf_op jit(solution)/shard_map/concatenate | solution.py:442
  27.8 0.0 copy-start
  27.8 1.0 %copy-done = f32[4,4,64,128]{3,2,1,0:T(8,128)S(1)} copy-done((f32[4,4,64,128]{3,2,1,0:T(8,128)S(1)}, f32[4,4,64,128]{3,2,1,0:T(8,128)}, u32[]{:S(2)}) %copy-start) | copy-done | bytes 524312
  28.8 0.0 copy-start.1
  28.8 1.0 %copy-done.1 = f32[4,4,64,128]{3,2,1,0:T(8,128)S(1)} copy-done((f32[4,4,64,128]{3,2,1,0:T(8,128)S(1)}, f32[4,4,64,128]{3,2,1,0:T(8,128)}, u32[]{:S(2)}) %copy-start.1) | copy-done | bytes 524312
  29.9 0.0 copy-start.2
  29.9 1.0 %copy-done.2 = f32[8,2,64,128]{3,2,1,0:T(8,128)S(1)} copy-done((f32[8,2,64,128]{3,2,1,0:T(8,128)S(1)}, f32[8,2,64,128]{3,2,1,0:T(8,128)}, u32[]{:S(2)}) %copy-start.2) | copy-done | bytes 524312
  30.9 0.0 copy-start.3
  30.9 0.7 %copy-done.3 = f32[32,64]{1,0:T(8,128)S(1)} copy-done((f32[32,64]{1,0:T(8,128)S(1)}, f32[32,64]{1,0:T(8,128)}, u32[]{:S(2)}) %copy-start.3) | copy-done | bytes 8216
  31.6 28.4 %shard_map.87 = (f32[64,256]{1,0:T(8,128)S(1)}, f32[64,1024]{1,0:T(8,128)S(1)}) custom-call(s32[45]{0:T(128)S(1)} %concatenate.7.req_ref, f32[4,32,128,128]{3,2,1,0:T(8,128)} %bitcast.13, f32[16,64,128]{2,1,0:T(8,128)S(1)} %bitcast.9, f32[16,64,128]{2,1,0:T(8,128)S(1)} %bitcast.10, f32[16,64,128]{2,1,0:T(8,128)S(1)} %bitcast.11, f32[32,64]{1,0:T(8,128)S(1)} %copy-done.3, ...), custom_call_target="tpu_custom_call" | custom-call | flops 536870912 | bytes 8388608 | tf_op jit(solution)/shard_map/pallas_call | solution.py:343
  60.0 0.6 %copy.15 = f32[64,256]{1,0:T(8,128)} copy(f32[64,256]{1,0:T(8,128)S(1)} %get-tuple-element.42) | data formatting | bytes 131072
  60.6 0.7 %copy.16 = f32[64,1024]{1,0:T(8,128)} copy(f32[64,1024]{1,0:T(8,128)S(1)} %get-tuple-element.43) | data formatting | bytes 524288
  (1 shorter events, 0.0 us)
Async XLA Ops:
  2.0 0.8 %copy-start.4 = (s32[8,128]{1,0:T(8,128)}, s32[8,128]{1,0:T(8,128)S(1)}, u32[]{:S(2)}) copy-start(s32[8,128]{1,0:T(8,128)S(1)} %scatter.9.refs_2_.refs_3_) | copy-start | bytes 12292
  27.8 1.0 %copy-start = (f32[4,4,64,128]{3,2,1,0:T(8,128)S(1)}, f32[4,4,64,128]{3,2,1,0:T(8,128)}, u32[]{:S(2)}) copy-start(f32[4,4,64,128]{3,2,1,0:T(8,128)} %get-tuple-element.33) | copy-start | bytes 1572868
  28.8 1.0 %copy-start.1 = (f32[4,4,64,128]{3,2,1,0:T(8,128)S(1)}, f32[4,4,64,128]{3,2,1,0:T(8,128)}, u32[]{:S(2)}) copy-start(f32[4,4,64,128]{3,2,1,0:T(8,128)} %get-tuple-element.34) | copy-start | bytes 1572868
  29.9 1.0 %copy-start.2 = (f32[8,2,64,128]{3,2,1,0:T(8,128)S(1)}, f32[8,2,64,128]{3,2,1,0:T(8,128)}, u32[]{:S(2)}) copy-start(f32[8,2,64,128]{3,2,1,0:T(8,128)} %get-tuple-element.35) | copy-start | bytes 1572868
  30.9 0.7 %copy-start.3 = (f32[32,64]{1,0:T(8,128)S(1)}, f32[32,64]{1,0:T(8,128)}, u32[]{:S(2)}) copy-start(f32[32,64]{1,0:T(8,128)} %w_ref.1) | copy-start | bytes 24580

commit v17 on v12

--- a/solution.py
+++ b/solution.py
@@ -190,11 +190,8 @@
         pl.semaphore_signal(barrier, inc=1, device_id=vpeer(lax.rem(me_v + k, n_v)), device_id_type=MESH_IDS)
     pl.semaphore_wait(barrier, n_x - 1 + n_y - 1 + n_v - 1)
 
-    loads = []
-    for s in range(slots):
-        cp = pltpu.make_async_copy(tiles_hbm.at[s], xbuf.at[s], xsem.at[s])
-        cp.start()
-        loads.append(cp)
+    loads = [pltpu.make_async_copy(tiles_hbm.at[s], xbuf.at[s], xsem.at[s]) for s in range(slots)]
+    loads[0].start()
 
     def send_rows(buf, land, ssem, rsem, n, me, peer, whole):
         started = []
@@ -228,6 +225,8 @@
     wt = wt_ref[...]
     for s in range(slots):
         loads[s].wait()
+        if s + 1 < slots:
+            loads[s + 1].start()
         flat = xbuf[s].reshape(weeks * users, items)
         usel = usel_ref[s]
         stacked = jnp.concatenate([usel * wt[:, k:k + 1] for k in range(weeks)], axis=1)

time: 58.4 us -> 58.4 us (level)
  no operation moved by 1% of the time
where the time goes in v17:
time: 58.4 us; the launch traced here: 57.8 us
  Pallas kernels  47.1 us (81%)
  local copies, waits for them, and re-layouts  9.31 us (16%)
  between operations  1.32 us (2%)
    pallas_call x1, Pallas kernels, fused_middle(): pl.pallas_call(_fused_kernel, out_shape=(jax.ShapeDtypeStruct(up_shape[1:...  29.6 us
    pallas_call x1, Pallas kernels, exchange(): pl.pallas_call(functools.partial(_exchange_kernel, plan), out_shape=tuple...  17.6 us
    unnamed x13, local copies, waits for them, and re-layouts  5.98 us

profile of v17, /device:TPU:1, one launch (start us, length us, event | category | flops | bytes accessed | tf_op | source)
XLA Modules:
  0.0 57.8 jit_solution(16270935190348572699)
XLA Ops:
  1.3 0.7 %scatter.6 = s32[8,128]{1,0:T(8,128)S(1)} pad(s32[1,4]{1,0:T(1,128)} %bitcast.14, s32[]{:T(128)} %constant.54.clone.1), padding=0_7x0_124 | pad | bytes 4116 | tf_op jit(solution)/shard_map/scatter | solution.py:393
  2.0 0.0 copy-start.4
  2.0 0.8 %copy.10 = f32[32,64]{0,1:T(8,128)S(1)} copy(f32[32,64]{1,0:T(8,128)} %w_ref.1) | data formatting | bytes 16384 | tf_op args[6]
  2.8 0.0 copy-done.4
  2.8 17.6 %shard_map.86 = (f32[4,4,64,128]{3,2,1,0:T(8,128)}, f32[4,4,64,128]{3,2,1,0:T(8,128)}, s32[4,8,128]{2,1,0:T(8,128)}, s32[4,8,128]{2,1,0:T(8,128)}, f32[8,2,64,128]{3,2,1,0:T(8,128)}) custom-call(f32[64,1024]{1,0:T(8,128)} %refs_1_.1, f32[64,1024]{1,0:T(8,128)} %refs_1_.1, s32[8,128]{1,0:T(8,128)} %copy-done.4, s32[8,128]{1,0:T(8,128)} %copy-done.4, ...), custom_call_target="tpu_custom_call" | custom-call | tf_op jit(solution)/shard_map/pallas_call | solution.py:107
  20.4 1.0 %slice_reduce_fusion = (s32[4]{0:T(128)S(1)}, s32[4]{0:T(128)S(1)}) fusion(s32[4,8,128]{2,1,0:T(8,128)} %get-tuple-element.32, s32[4,8,128]{2,1,0:T(8,128)} %get-tuple-element.31), kind=kLoop, calls=%fused_computation | loop fusion | bytes 64 | tf_op jit(solution)/shard_map/slice | solution.py:411
  21.3 0.8 %slice_reduce_fusion.1 = (s32[4,4]{1,0:T(4,128)S(1)}, s32[4,4]{1,0:T(4,128)S(1)}) fusion(s32[4,8,128]{2,1,0:T(8,128)} %get-tuple-element.32, s32[4,8,128]{2,1,0:T(8,128)} %get-tuple-element.31), kind=kLoop, calls=%fused_computation.1 | loop fusion | bytes 256 | tf_op jit(solution)/shard_map/slice | solution.py:411
  22.1 0.1 reshape_squeeze.10
  22.2 0.1 reshape_squeeze.9
  22.3 0.7 %concatenate.7.req_ref = s32[45]{0:T(128)S(1)} concatenate(s32[16]{0:T(128)S(1)} %reshape_squeeze.9, s32[4]{0:T(128)S(1)} %get-tuple-element.39, s32[16]{0:T(128)S(1)} %reshape_squeeze.10, s32[4]{0:T(128)S(1)} %get-tuple-element.38, s32[4]{0:T(128)} %bitcast.15, s32[1]{0:T(128)} %bitcast.8), dimensions={0} | concatenate | bytes 360 | tf_op jit(solution)/shard_map/concatenate | solution.py:410
  23.0 0.0 copy-start
  23.0 1.0 %copy-done = f32[4,4,64,128]{3,2,1,0:T(8,128)S(1)} copy-done((f32[4,4,64,128]{3,2,1,0:T(8,128)S(1)}, f32[4,4,64,128]{3,2,1,0:T(8,128)}, u32[]{:S(2)}) %copy-start) | copy-done | bytes 524312
  24.1 0.0 copy-start.1
  24.1 1.0 %copy-done.1 = f32[4,4,64,128]{3,2,1,0:T(8,128)S(1)} copy-done((f32[4,4,64,128]{3,2,1,0:T(8,128)S(1)}, f32[4,4,64,128]{3,2,1,0:T(8,128)}, u32[]{:S(2)}) %copy-start.1) | copy-done | bytes 524312
  25.1 0.0 copy-start.2
  25.1 1.0 %copy-done.2 = f32[8,2,64,128]{3,2,1,0:T(8,128)S(1)} copy-done((f32[8,2,64,128]{3,2,1,0:T(8,128)S(1)}, f32[8,2,64,128]{3,2,1,0:T(8,128)}, u32[]{:S(2)}) %copy-start.2) | copy-done | bytes 524312
  26.1 0.0 copy-start.3
  26.1 0.7 %copy-done.3 = f32[32,64]{1,0:T(8,128)S(1)} copy-done((f32[32,64]{1,0:T(8,128)S(1)}, f32[32,64]{1,0:T(8,128)}, u32[]{:S(2)}) %copy-start.3) | copy-done | bytes 8216
  26.9 29.6 %shard_map.87 = (f32[64,256]{1,0:T(8,128)S(1)}, f32[64,1024]{1,0:T(8,128)S(1)}) custom-call(s32[45]{0:T(128)S(1)} %concatenate.7.req_ref, f32[4,32,128,128]{3,2,1,0:T(8,128)} %bitcast.13, f32[16,64,128]{2,1,0:T(8,128)S(1)} %bitcast.9, f32[16,64,128]{2,1,0:T(8,128)S(1)} %bitcast.10, f32[16,64,128]{2,1,0:T(8,128)S(1)} %bitcast.11, f32[32,64]{1,0:T(8,128)S(1)} %copy-done.3, ...), custom_call_target="tpu_custom_call" | custom-call | flops 536870912 | bytes 8388608 | tf_op jit(solution)/shard_map/pallas_call | solution.py:311
  56.4 0.6 %copy.15 = f32[64,256]{1,0:T(8,128)} copy(f32[64,256]{1,0:T(8,128)S(1)} %get-tuple-element.42) | data formatting | bytes 131072
  57.0 0.7 %copy.16 = f32[64,1024]{1,0:T(8,128)} copy(f32[64,1024]{1,0:T(8,128)S(1)} %get-tuple-element.43) | data formatting | bytes 524288
  (1 shorter events, 0.0 us)
Async XLA Ops:
  2.0 0.8 %copy-start.4 = (s32[8,128]{1,0:T(8,128)}, s32[8,128]{1,0:T(8,128)S(1)}, u32[]{:S(2)}) copy-start(s32[8,128]{1,0:T(8,128)S(1)} %scatter.9.refs_2_.refs_3_) | copy-start | bytes 12292
  23.0 1.0 %copy-start = (f32[4,4,64,128]{3,2,1,0:T(8,128)S(1)}, f32[4,4,64,128]{3,2,1,0:T(8,128)}, u32[]{:S(2)}) copy-start(f32[4,4,64,128]{3,2,1,0:T(8,128)} %get-tuple-element.33) | copy-start | bytes 1572868
  24.1 1.0 %copy-start.1 = (f32[4,4,64,128]{3,2,1,0:T(8,128)S(1)}, f32[4,4,64,128]{3,2,1,0:T(8,128)}, u32[]{:S(2)}) copy-start(f32[4,4,64,128]{3,2,1,0:T(8,128)} %get-tuple-element.34) | copy-start | bytes 1572868
  25.1 1.0 %copy-start.2 = (f32[8,2,64,128]{3,2,1,0:T(8,128)S(1)}, f32[8,2,64,128]{3,2,1,0:T(8,128)}, u32[]{:S(2)}) copy-start(f32[8,2,64,128]{3,2,1,0:T(8,128)} %get-tuple-element.35) | copy-start | bytes 1572868
  26.1 0.7 %copy-start.3 = (f32[32,64]{1,0:T(8,128)S(1)}, f32[32,64]{1,0:T(8,128)}, u32[]{:S(2)}) copy-start(f32[32,64]{1,0:T(8,128)} %w_ref.1) | copy-start | bytes 24580

commit v18 on v12

--- a/solution.py
+++ b/solution.py
@@ -249,9 +249,11 @@
             isel = isel + land_sy[lax.rem(me_y + k, n_y), s]
         flat = xbuf[s].reshape(weeks * users, items)
         by_items = lax.dot_general(
-            flat, isel, (((1,), (1,)), ((), ())), precision=TERMS, preferred_element_type=jnp.float32)
-        weighted = by_items.reshape(weeks, users, -1) * w[:, None, :]
-        uterms.append(jnp.sum(weighted, axis=0).T)
+            isel, flat, (((1,), (1,)), ((), ())), precision=TERMS, preferred_element_type=jnp.float32)
+        acc = by_items[:, 0:users] * wt[:, 0:1]
+        for k in range(1, weeks):
+            acc = acc + by_items[:, k * users:(k + 1) * users] * wt[:, k:k + 1]
+        uterms.append(acc)
 
     for v in range(n_v):
         for t in range(per_owner):

time: 58.4 us -> 59.5 us (1.019)
  Pallas kernels: 47.1 us -> 48.2 us
    pallas_call x1, Pallas kernels: 29.6 us -> 30.7 us  [fused_middle(): pl.pallas_call(_fused_kernel, out_shape=(jax.ShapeDtypeStruct(up_shape[1:...]
where the time goes in v18:
time: 59.5 us; the launch traced here: 58.9 us
  Pallas kernels  48.2 us (81%)
  local copies, waits for them, and re-layouts  9.31 us (16%)
  between operations  1.32 us (2%)
    pallas_call x1, Pallas kernels, fused_middle(): pl.pallas_call(_fused_kernel, out_shape=(jax.ShapeDtypeStruct(up_shape[1:...  30.7 us
    pallas_call x1, Pallas kernels, exchange(): pl.pallas_call(functools.partial(_exchange_kernel, plan), out_shape=tuple...  17.6 us
    unnamed x13, local copies, waits for them, and re-layouts  5.98 us

profile of v18, /device:TPU:1, one launch (start us, length us, event | category | flops | bytes accessed | tf_op | source)
XLA Modules:
  0.0 58.9 jit_solution(5711294220960927353)
XLA Ops:
  1.3 0.7 %scatter.6 = s32[8,128]{1,0:T(8,128)S(1)} pad(s32[1,4]{1,0:T(1,128)} %bitcast.14, s32[]{:T(128)} %constant.54.clone.1), padding=0_7x0_124 | pad | bytes 4116 | tf_op jit(solution)/shard_map/scatter | solution.py:396
  2.0 0.0 copy-start.4
  2.0 0.8 %copy.10 = f32[32,64]{0,1:T(8,128)S(1)} copy(f32[32,64]{1,0:T(8,128)} %w_ref.1) | data formatting | bytes 16384 | tf_op args[6]
  2.8 0.0 copy-done.4
  2.8 17.6 %shard_map.86 = (f32[4,4,64,128]{3,2,1,0:T(8,128)}, f32[4,4,64,128]{3,2,1,0:T(8,128)}, s32[4,8,128]{2,1,0:T(8,128)}, s32[4,8,128]{2,1,0:T(8,128)}, f32[8,2,64,128]{3,2,1,0:T(8,128)}) custom-call(f32[64,1024]{1,0:T(8,128)} %refs_1_.1, f32[64,1024]{1,0:T(8,128)} %refs_1_.1, s32[8,128]{1,0:T(8,128)} %copy-done.4, s32[8,128]{1,0:T(8,128)} %copy-done.4, ...), custom_call_target="tpu_custom_call" | custom-call | tf_op jit(solution)/shard_map/pallas_call | solution.py:107
  20.4 1.0 %slice_reduce_fusion = (s32[4]{0:T(128)S(1)}, s32[4]{0:T(128)S(1)}) fusion(s32[4,8,128]{2,1,0:T(8,128)} %get-tuple-element.32, s32[4,8,128]{2,1,0:T(8,128)} %get-tuple-element.31), kind=kLoop, calls=%fused_computation | loop fusion | bytes 64 | tf_op jit(solution)/shard_map/slice | solution.py:414
  21.3 0.8 %slice_reduce_fusion.1 = (s32[4,4]{1,0:T(4,128)S(1)}, s32[4,4]{1,0:T(4,128)S(1)}) fusion(s32[4,8,128]{2,1,0:T(8,128)} %get-tuple-element.32, s32[4,8,128]{2,1,0:T(8,128)} %get-tuple-element.31), kind=kLoop, calls=%fused_computation.1 | loop fusion | bytes 256 | tf_op jit(solution)/shard_map/slice | solution.py:414
  22.1 0.1 reshape_squeeze.10
  22.2 0.1 reshape_squeeze.9
  22.3 0.7 %concatenate.7.req_ref = s32[45]{0:T(128)S(1)} concatenate(s32[16]{0:T(128)S(1)} %reshape_squeeze.9, s32[4]{0:T(128)S(1)} %get-tuple-element.39, s32[16]{0:T(128)S(1)} %reshape_squeeze.10, s32[4]{0:T(128)S(1)} %get-tuple-element.38, s32[4]{0:T(128)} %bitcast.15, s32[1]{0:T(128)} %bitcast.8), dimensions={0} | concatenate | bytes 360 | tf_op jit(solution)/shard_map/concatenate | solution.py:413
  23.0 0.0 copy-start
  23.0 1.0 %copy-done = f32[4,4,64,128]{3,2,1,0:T(8,128)S(1)} copy-done((f32[4,4,64,128]{3,2,1,0:T(8,128)S(1)}, f32[4,4,64,128]{3,2,1,0:T(8,128)}, u32[]{:S(2)}) %copy-start) | copy-done | bytes 524312
  24.1 0.0 copy-start.1
  24.1 1.0 %copy-done.1 = f32[4,4,64,128]{3,2,1,0:T(8,128)S(1)} copy-done((f32[4,4,64,128]{3,2,1,0:T(8,128)S(1)}, f32[4,4,64,128]{3,2,1,0:T(8,128)}, u32[]{:S(2)}) %copy-start.1) | copy-done | bytes 524312
  25.1 0.0 copy-start.2
  25.1 1.0 %copy-done.2 = f32[8,2,64,128]{3,2,1,0:T(8,128)S(1)} copy-done((f32[8,2,64,128]{3,2,1,0:T(8,128)S(1)}, f32[8,2,64,128]{3,2,1,0:T(8,128)}, u32[]{:S(2)}) %copy-start.2) | copy-done | bytes 524312
  26.1 0.0 copy-start.3
  26.1 0.7 %copy-done.3 = f32[32,64]{1,0:T(8,128)S(1)} copy-done((f32[32,64]{1,0:T(8,128)S(1)}, f32[32,64]{1,0:T(8,128)}, u32[]{:S(2)}) %copy-start.3) | copy-done | bytes 8216
  26.9 30.7 %shard_map.87 = (f32[64,256]{1,0:T(8,128)S(1)}, f32[64,1024]{1,0:T(8,128)S(1)}) custom-call(s32[45]{0:T(128)S(1)} %concatenate.7.req_ref, f32[4,32,128,128]{3,2,1,0:T(8,128)} %bitcast.13, f32[16,64,128]{2,1,0:T(8,128)S(1)} %bitcast.9, f32[16,64,128]{2,1,0:T(8,128)S(1)} %bitcast.10, f32[16,64,128]{2,1,0:T(8,128)S(1)} %bitcast.11, f32[32,64]{1,0:T(8,128)S(1)} %copy-done.3, ...), custom_call_target="tpu_custom_call" | custom-call | flops 536870912 | bytes 8388608 | tf_op jit(solution)/shard_map/pallas_call | solution.py:314
  57.5 0.6 %copy.15 = f32[64,256]{1,0:T(8,128)} copy(f32[64,256]{1,0:T(8,128)S(1)} %get-tuple-element.42) | data formatting | bytes 131072
  58.1 0.7 %copy.16 = f32[64,1024]{1,0:T(8,128)} copy(f32[64,1024]{1,0:T(8,128)S(1)} %get-tuple-element.43) | data formatting | bytes 524288
  (1 shorter events, 0.0 us)
Async XLA Ops:
  2.0 0.8 %copy-start.4 = (s32[8,128]{1,0:T(8,128)}, s32[8,128]{1,0:T(8,128)S(1)}, u32[]{:S(2)}) copy-start(s32[8,128]{1,0:T(8,128)S(1)} %scatter.9.refs_2_.refs_3_) | copy-start | bytes 12292
  23.0 1.0 %copy-start = (f32[4,4,64,128]{3,2,1,0:T(8,128)S(1)}, f32[4,4,64,128]{3,2,1,0:T(8,128)}, u32[]{:S(2)}) copy-start(f32[4,4,64,128]{3,2,1,0:T(8,128)} %get-tuple-element.33) | copy-start | bytes 1572868
  24.1 1.0 %copy-start.1 = (f32[4,4,64,128]{3,2,1,0:T(8,128)S(1)}, f32[4,4,64,128]{3,2,1,0:T(8,128)}, u32[]{:S(2)}) copy-start(f32[4,4,64,128]{3,2,1,0:T(8,128)} %get-tuple-element.34) | copy-start | bytes 1572868
  25.1 1.0 %copy-start.2 = (f32[8,2,64,128]{3,2,1,0:T(8,128)S(1)}, f32[8,2,64,128]{3,2,1,0:T(8,128)}, u32[]{:S(2)}) copy-start(f32[8,2,64,128]{3,2,1,0:T(8,128)} %get-tuple-element.35) | copy-start | bytes 1572868
  26.1 0.7 %copy-start.3 = (f32[32,64]{1,0:T(8,128)S(1)}, f32[32,64]{1,0:T(8,128)}, u32[]{:S(2)}) copy-start(f32[32,64]{1,0:T(8,128)} %w_ref.1) | copy-start | bytes 24580

commit v19 on v12

--- a/solution.py
+++ b/solution.py
@@ -188,7 +188,6 @@
         pl.semaphore_signal(barrier, inc=1, device_id=ypeer(lax.rem(me_y + k, n_y)), device_id_type=MESH_IDS)
     for k in range(1, n_v):
         pl.semaphore_signal(barrier, inc=1, device_id=vpeer(lax.rem(me_v + k, n_v)), device_id_type=MESH_IDS)
-    pl.semaphore_wait(barrier, n_x - 1 + n_y - 1 + n_v - 1)
 
     loads = []
     for s in range(slots):
@@ -217,16 +216,19 @@
 
     for cp in factor_loads:
         cp.wait()
-    for q in range(n_q):
-        sel_x[q // slots, q % slots] = ga_ref[path_a[q][3]] * jnp.where(path_a[q][0], one, zero)
-        sel_y[q // slots, q % slots] = gb_ref[path_b[q][3]] * jnp.where(path_b[q][0], one, zero)
-    sx_copies = send_rows(sel_x, land_sx, sx_s, sx_r, n_x, me_x, xpeer, False)
-    sy_copies = send_rows(sel_y, land_sy, sy_s, sy_r, n_y, me_y, ypeer, False)
+
     for s in range(slots):
         usel_ref[s] = urows_ref[req_ref[own_at + s]] * jnp.where(own_live[s], one, zero)
-
     wt = wt_ref[...]
+    early = slots // 2
     for s in range(slots):
+        if s == early:
+            pl.semaphore_wait(barrier, n_x - 1 + n_y - 1 + n_v - 1)
+            for q in range(n_q):
+                sel_x[q // slots, q % slots] = ga_ref[path_a[q][3]] * jnp.where(path_a[q][0], one, zero)
+                sel_y[q // slots, q % slots] = gb_ref[path_b[q][3]] * jnp.where(path_b[q][0], one, zero)
+            sx_copies = send_rows(sel_x, land_sx, sx_s, sx_r, n_x, me_x, xpeer, False)
+            sy_copies = send_rows(sel_y, land_sy, sy_s, sy_r, n_y, me_y, ypeer, False)
         loads[s].wait()
         flat = xbuf[s].reshape(weeks * users, items)
         usel = usel_ref[s]

time: 58.4 us -> 60.5 us (1.036)
  the two profiles are of different devices: /device:TPU:1 before, /device:TPU:0 now
where the time goes in v19:
time: 60.5 us; the launch traced here: 59.8 us
  Pallas kernels  49.2 us (81%)
  local copies, waits for them, and re-layouts  9.31 us (15%)
  between operations  1.32 us (2%)
    pallas_call x1, Pallas kernels, fused_middle(): pl.pallas_call(_fused_kernel, out_shape=(jax.ShapeDtypeStruct(up_shape[1:...  32.2 us
    pallas_call x1, Pallas kernels, exchange(): pl.pallas_call(functools.partial(_exchange_kernel, plan), out_shape=tuple...  17 us
    unnamed x13, local copies, waits for them, and re-layouts  5.98 us

profile of v19, /device:TPU:0, one launch (start us, length us, event | category | flops | bytes accessed | tf_op | source)
XLA Modules:
  0.0 59.8 jit_solution(13156961025798929383)
XLA Ops:
  1.3 0.7 %scatter.6 = s32[8,128]{1,0:T(8,128)S(1)} pad(s32[1,4]{1,0:T(1,128)} %bitcast.14, s32[]{:T(128)} %constant.54.clone.1), padding=0_7x0_124 | pad | bytes 4116 | tf_op jit(solution)/shard_map/scatter | solution.py:396
  2.0 0.0 copy-start.4
  2.0 0.8 %copy.10 = f32[32,64]{0,1:T(8,128)S(1)} copy(f32[32,64]{1,0:T(8,128)} %w_ref.1) | data formatting | bytes 16384 | tf_op args[6]
  2.8 0.0 copy-done.4
  2.8 17.0 %shard_map.86 = (f32[4,4,64,128]{3,2,1,0:T(8,128)}, f32[4,4,64,128]{3,2,1,0:T(8,128)}, s32[4,8,128]{2,1,0:T(8,128)}, s32[4,8,128]{2,1,0:T(8,128)}, f32[8,2,64,128]{3,2,1,0:T(8,128)}) custom-call(f32[64,1024]{1,0:T(8,128)} %refs_1_.1, f32[64,1024]{1,0:T(8,128)} %refs_1_.1, s32[8,128]{1,0:T(8,128)} %copy-done.4, s32[8,128]{1,0:T(8,128)} %copy-done.4, ...), custom_call_target="tpu_custom_call" | custom-call | tf_op jit(solution)/shard_map/pallas_call | solution.py:107
  19.8 1.0 %slice_reduce_fusion = (s32[4]{0:T(128)S(1)}, s32[4]{0:T(128)S(1)}) fusion(s32[4,8,128]{2,1,0:T(8,128)} %get-tuple-element.32, s32[4,8,128]{2,1,0:T(8,128)} %get-tuple-element.31), kind=kLoop, calls=%fused_computation | loop fusion | bytes 64 | tf_op jit(solution)/shard_map/slice | solution.py:414
  20.8 0.8 %slice_reduce_fusion.1 = (s32[4,4]{1,0:T(4,128)S(1)}, s32[4,4]{1,0:T(4,128)S(1)}) fusion(s32[4,8,128]{2,1,0:T(8,128)} %get-tuple-element.32, s32[4,8,128]{2,1,0:T(8,128)} %get-tuple-element.31), kind=kLoop, calls=%fused_computation.1 | loop fusion | bytes 256 | tf_op jit(solution)/shard_map/slice | solution.py:414
  21.6 0.1 reshape_squeeze.10
  21.6 0.1 reshape_squeeze.9
  21.7 0.7 %concatenate.7.req_ref = s32[45]{0:T(128)S(1)} concatenate(s32[16]{0:T(128)S(1)} %reshape_squeeze.9, s32[4]{0:T(128)S(1)} %get-tuple-element.39, s32[16]{0:T(128)S(1)} %reshape_squeeze.10, s32[4]{0:T(128)S(1)} %get-tuple-element.38, s32[4]{0:T(128)} %bitcast.15, s32[1]{0:T(128)} %bitcast.8), dimensions={0} | concatenate | bytes 360 | tf_op jit(solution)/shard_map/concatenate | solution.py:413
  22.5 0.0 copy-start
  22.5 1.0 %copy-done = f32[4,4,64,128]{3,2,1,0:T(8,128)S(1)} copy-done((f32[4,4,64,128]{3,2,1,0:T(8,128)S(1)}, f32[4,4,64,128]{3,2,1,0:T(8,128)}, u32[]{:S(2)}) %copy-start) | copy-done | bytes 524312
  23.5 0.0 copy-start.1
  23.5 1.0 %copy-done.1 = f32[4,4,64,128]{3,2,1,0:T(8,128)S(1)} copy-done((f32[4,4,64,128]{3,2,1,0:T(8,128)S(1)}, f32[4,4,64,128]{3,2,1,0:T(8,128)}, u32[]{:S(2)}) %copy-start.1) | copy-done | bytes 524312
  24.5 0.0 copy-start.2
  24.5 1.0 %copy-done.2 = f32[8,2,64,128]{3,2,1,0:T(8,128)S(1)} copy-done((f32[8,2,64,128]{3,2,1,0:T(8,128)S(1)}, f32[8,2,64,128]{3,2,1,0:T(8,128)}, u32[]{:S(2)}) %copy-start.2) | copy-done | bytes 524312
  25.6 0.0 copy-start.3
  25.6 0.7 %copy-done.3 = f32[32,64]{1,0:T(8,128)S(1)} copy-done((f32[32,64]{1,0:T(8,128)S(1)}, f32[32,64]{1,0:T(8,128)}, u32[]{:S(2)}) %copy-start.3) | copy-done | bytes 8216
  26.3 32.2 %shard_map.87 = (f32[64,256]{1,0:T(8,128)S(1)}, f32[64,1024]{1,0:T(8,128)S(1)}) custom-call(s32[45]{0:T(128)S(1)} %concatenate.7.req_ref, f32[4,32,128,128]{3,2,1,0:T(8,128)} %bitcast.13, f32[16,64,128]{2,1,0:T(8,128)S(1)} %bitcast.9, f32[16,64,128]{2,1,0:T(8,128)S(1)} %bitcast.10, f32[16,64,128]{2,1,0:T(8,128)S(1)} %bitcast.11, f32[32,64]{1,0:T(8,128)S(1)} %copy-done.3, ...), custom_call_target="tpu_custom_call" | custom-call | flops 536870912 | bytes 8388608 | tf_op jit(solution)/shard_map/pallas_call | solution.py:314
  58.5 0.6 %copy.15 = f32[64,256]{1,0:T(8,128)} copy(f32[64,256]{1,0:T(8,128)S(1)} %get-tuple-element.42) | data formatting | bytes 131072
  59.1 0.7 %copy.16 = f32[64,1024]{1,0:T(8,128)} copy(f32[64,1024]{1,0:T(8,128)S(1)} %get-tuple-element.43) | data formatting | bytes 524288
  (1 shorter events, 0.0 us)
Async XLA Ops:
  2.0 0.8 %copy-start.4 = (s32[8,128]{1,0:T(8,128)}, s32[8,128]{1,0:T(8,128)S(1)}, u32[]{:S(2)}) copy-start(s32[8,128]{1,0:T(8,128)S(1)} %scatter.9.refs_2_.refs_3_) | copy-start | bytes 12292
  22.5 1.0 %copy-start = (f32[4,4,64,128]{3,2,1,0:T(8,128)S(1)}, f32[4,4,64,128]{3,2,1,0:T(8,128)}, u32[]{:S(2)}) copy-start(f32[4,4,64,128]{3,2,1,0:T(8,128)} %get-tuple-element.33) | copy-start | bytes 1572868
  23.5 1.0 %copy-start.1 = (f32[4,4,64,128]{3,2,1,0:T(8,128)S(1)}, f32[4,4,64,128]{3,2,1,0:T(8,128)}, u32[]{:S(2)}) copy-start(f32[4,4,64,128]{3,2,1,0:T(8,128)} %get-tuple-element.34) | copy-start | bytes 1572868
  24.5 1.0 %copy-start.2 = (f32[8,2,64,128]{3,2,1,0:T(8,128)S(1)}, f32[8,2,64,128]{3,2,1,0:T(8,128)}, u32[]{:S(2)}) copy-start(f32[8,2,64,128]{3,2,1,0:T(8,128)} %get-tuple-element.35) | copy-start | bytes 1572868
  25.6 0.7 %copy-start.3 = (f32[32,64]{1,0:T(8,128)S(1)}, f32[32,64]{1,0:T(8,128)}, u32[]{:S(2)}) copy-start(f32[32,64]{1,0:T(8,128)} %w_ref.1) | copy-start | bytes 24580
